TPU v7x, 32 devices: a whole 2x2x4 slice. The times are simulated.
32 devices in a mesh: seq: 4 (over z), row: 2 (over x), col: 4 (over y, core).
Axes of the slice: x: 2, y: 2, z: 4, core: 2. Of those that a mesh axis runs over, the one named last changes fastest.
Arguments:
- grads: bfloat16 [1024, 28672], P('row', ('seq', 'col')), may hold values from -6 to 6
- acts: bfloat16 [1024, 8192], P(('seq', 'col'), 'row'), may hold values from -6 to 6
- out_basis: bfloat16 [28672, 28672], P(('seq', 'col'), 'row'), may hold values from -0.03125 to 0.03125
- in_basis: bfloat16 [8192, 8192], P('row', ('seq', 'col')), may hold values from -0.0625 to 0.0625
- lengths: int32 [4], replicated, may hold values from 1 to 256, 768 in all
Outputs:
- eigenvalues: float32 [28672, 8192], P('row', ('seq', 'col'))
Inputs may be any that keep to these rules, and one draw needn't show every extreme that they name: lengths sum to 768; some sequence is full.
All inputs are finite; a program needn't handle non-finite values.
Results may differ from a plain program's by a relative error of at most 0.0036.
Values may be sent and summed in bfloat16 or wider, within the bound.
No kernel may reach another device: no remote copies, remote signals or barrier semaphores. Data moves between devices by JAX's collectives and lax.ppermute only.
A program may use at most 192 MiB of HBM per device.

v0:
```python
import jax
import jax.numpy as jnp
from jax import lax
from jax.sharding import PartitionSpec as P

SEQ_LEN = 256


def body(grads, acts, out_basis, in_basis, lengths):
    seq_count = lax.axis_size("seq")
    partial_value = jnp.dot(
        lax.all_gather(grads, "row", axis=0, tiled=True),
        out_basis,
        preferred_element_type=jnp.float32,
    )
    shared = lax.psum_scatter(
        partial_value, ("seq", "col"), scatter_dimension=0, tiled=True
    ).astype(jnp.bfloat16)
    grad_proj = lax.all_gather(shared, ("seq", "col"), axis=0, tiled=True)
    act_full = lax.all_gather(acts, ("seq", "col"), axis=0, tiled=True)
    row_count = act_full.shape[0] // lax.axis_size("row")
    act_share = lax.psum_scatter(
        jnp.dot(act_full, in_basis, preferred_element_type=jnp.float32),
        "row",
        scatter_dimension=0,
        tiled=True,
    )
    token_index = lax.axis_index("row") * row_count + jnp.arange(row_count, dtype=jnp.int32)
    seq_owner = token_index // SEQ_LEN
    position = token_index % SEQ_LEN
    seq_ids = jnp.arange(lengths.shape[0], dtype=jnp.int32)
    seq_length = jnp.sum(
        jnp.where(seq_owner[:, None] == seq_ids[None, :], lengths[None, :], 0), axis=1
    )
    is_live = (position < seq_length).astype(jnp.float32)
    act_rows = (act_share * is_live[:, None]).astype(jnp.bfloat16)
    act_proj = lax.all_gather(act_rows, "row", axis=0, tiled=True)
    grad_three = grad_proj.reshape(seq_count, SEQ_LEN, grad_proj.shape[1])
    act_three = act_proj.reshape(seq_count, SEQ_LEN, act_proj.shape[1])

    def accumulate(total, pair):
        grad_seq = lax.dot_general(
            pair[0], pair[1], (((0,), (0,)), ((), ())), preferred_element_type=jnp.float32
        )
        return (total + grad_seq * grad_seq, None)

    start_total = jnp.zeros((grad_proj.shape[1], act_proj.shape[1]), jnp.float32)
    total, unused = lax.scan(accumulate, start_total, (grad_three, act_three))
    return total / (seq_count * SEQ_LEN)


def solution(mesh):
    in_specs = (
        P("row", ("seq", "col")),
        P(("seq", "col"), "row"),
        P(("seq", "col"), "row"),
        P("row", ("seq", "col")),
        P(),
    )
    out_specs = P("row", ("seq", "col"))
    return jax.shard_map(body, mesh=mesh, in_specs=in_specs, out_specs=out_specs, check_vma=False)
```

profile of v0, /device:TPU:0, one launch (start us, length us, event | category | flops | bytes accessed | tf_op | source)
XLA Modules:
  0.0 1026.4 jit_solution(2737312579928235506)
XLA Ops:
  6.5 0.0 all-gather.9.cloned.1.call-start
  6.5 0.7 all-gather.9.cloned.1.call-update
  7.3 0.0 all-gather.5.cloned.1.call-start
  7.3 0.7 all-gather.5.cloned.1.call-update
  8.0 0.0 reduce-scatter.5.cloned.1.call-start
  8.1 78.5 %all-gather.9.cloned.1.call-done = bf16[1024,4096]{1,0:T(8,128)(2,1)} async-done(((bf16[64,4096]{1,0:T(8,128)(2,1)}), bf16[1024,4096]{1,0:T(8,128)(2,1)}) %all-gather.9.cloned.1.call-update) | async-done | bytes 8388624 | tf_op jit(solution)/shard_map/all_gather | solution.py:20
  86.5 10.4 %fusion.11 = f32[1024,512]{1,0:T(8,128)} fusion(bf16[1024,4096]{1,0:T(8,128)(2,1)} %all-gather.9.cloned.1.call-done, bf16[4096,512]{1,0:T(8,128)(2,1)} %param.10), kind=kOutput, calls=%fused_computation.23 | convolution fusion | flops 4294967296 | bytes 14680064 | tf_op jit(solution)/shard_map/dot_general | solution.py:23
  96.9 0.0 reduce-scatter.5.cloned.1.call-update
  97.0 0.0 reduce-scatter.3.cloned.1.call-start
  97.0 40.5 %all-gather.5.cloned.1.call-done = bf16[1024,1792]{1,0:T(8,128)(2,1)} async-done(((bf16[512,1792]{1,0:T(8,128)(2,1)}), bf16[1024,1792]{1,0:T(8,128)(2,1)}) %all-gather.5.cloned.1.call-update) | async-done | bytes 3670032 | tf_op jit(solution)/shard_map/all_gather | solution.py:12
  137.5 61.7 %fusion.10 = f32[1024,14336]{1,0:T(8,128)} fusion(bf16[1024,1792]{1,0:T(8,128)(2,1)} %all-gather.5.cloned.1.call-done, bf16[1792,14336]{1,0:T(8,128)(2,1)} %param.9), kind=kOutput, calls=%fused_computation.22 | convolution fusion | flops 52613349376 | bytes 113770496 | tf_op jit(solution)/shard_map/dot_general | solution.py:11
  199.2 0.0 copy-start
  199.2 0.0 reduce-scatter.3.cloned.1.call-update
  199.3 0.0 all-gather.11.cloned.1.call-start
  199.3 0.6 copy-done
  199.9 0.1 select_reduce_fusion
  200.0 0.0 reduce-scatter.5.cloned.1.call-done
  200.0 2.2 multiply_convert_fusion
  202.2 0.0 all-gather.11.cloned.1.call-update
  202.2 0.0 all-gather.7.cloned.1.call-start
  202.2 538.7 %reduce-scatter.3.cloned.1.call-done = f32[64,14336]{1,0:T(8,128)} async-done(((f32[1024,14336]{1,0:T(8,128)}), f32[64,14336]{1,0:T(8,128)}) %reduce-scatter.3.cloned.1.call-update) | async-done | bytes 3670032 | tf_op jit(solution)/shard_map/reduce_scatter | solution.py:16
  740.9 3.5 convert_element_type.13
  744.4 0.0 all-gather.7.cloned.1.call-update
  744.5 18.3 %all-gather.11.cloned.1.call-done = bf16[1024,512]{1,0:T(8,128)(2,1)} async-done(((bf16[512,512]{1,0:T(8,128)(2,1)}), bf16[1024,512]{1,0:T(8,128)(2,1)}) %all-gather.11.cloned.1.call-update) | async-done | bytes 1048592 | tf_op jit(solution)/shard_map/all_gather | solution.py:37
  762.7 149.8 %all-gather.7.cloned.1.call-done = bf16[1024,14336]{1,0:T(8,128)(2,1)} async-done(((bf16[64,14336]{1,0:T(8,128)(2,1)}), bf16[1024,14336]{1,0:T(8,128)(2,1)}) %all-gather.7.cloned.1.call-update) | async-done | bytes 29360144 | tf_op jit(solution)/shard_map/all_gather | solution.py:19
  912.5 85.2 %while.11 = (s32[]{:T(128)}, f32[14336,512]{1,0:T(8,128)}, bf16[4,256,14336]{2,1,0:T(8,128)(2,1)}, bf16[4,256,512]{2,1,0:T(8,128)(2,1)}, s32[]{:T(128)}, /*index=5*/s32[]{:T(128)}) while((s32[]{:T(128)}, f32[14336,512]{1,0:T(8,128)}, bf16[4,256,14336]{2,1,0:T(8,128)(2,1)}, bf16[4,256,512]{2,1,0:T(8,128)(2,1)}, s32[]{:T(128)}, ...), condition=%wide.region_4.5_spmd.clone, body=%wide.region_3.4_spmd.clone.sunk | while | flops 3780116480 | bytes 66323532 | solution.py:48
  912.5 13.2 %select_add_fusion.2 = f32[14336,512]{1,0:T(8,128)} fusion(f32[14336,512]{1,0:T(8,128)} %get-tuple-element.83, pred[]{:T(512)S(6)} %compare.14, bf16[4,256,14336]{2,1,0:T(8,128)(2,1)} %get-tuple-element.90, s32[]{:T(128)} %get-tuple-element.82, bf16[4,256,512]{2,1,0:T(8,128)(2,1)} %get-tuple-element.91), kind=kOutput, calls=%fused_computation.clone.1 | convolution fusion | flops 3780116480 | bytes 66323456 | tf_op jit(solution)/shard_map/while/body/eval_jaxpr/dot_general | solution.py:42
  925.7 24.0 %select_add_fusion.2 = f32[14336,512]{1,0:T(8,128)} fusion(f32[14336,512]{1,0:T(8,128)} %get-tuple-element.83, pred[]{:T(512)S(6)} %compare.14, bf16[4,256,14336]{2,1,0:T(8,128)(2,1)} %get-tuple-element.90, s32[]{:T(128)} %get-tuple-element.82, bf16[4,256,512]{2,1,0:T(8,128)(2,1)} %get-tuple-element.91), kind=kOutput, calls=%fused_computation.clone.1 | convolution fusion | flops 3780116480 | bytes 66323456 | tf_op jit(solution)/shard_map/while/body/eval_jaxpr/dot_general | solution.py:42
  949.7 24.0 %select_add_fusion.2 = f32[14336,512]{1,0:T(8,128)} fusion(f32[14336,512]{1,0:T(8,128)} %get-tuple-element.83, pred[]{:T(512)S(6)} %compare.14, bf16[4,256,14336]{2,1,0:T(8,128)(2,1)} %get-tuple-element.90, s32[]{:T(128)} %get-tuple-element.82, bf16[4,256,512]{2,1,0:T(8,128)(2,1)} %get-tuple-element.91), kind=kOutput, calls=%fused_computation.clone.1 | convolution fusion | flops 3780116480 | bytes 66323456 | tf_op jit(solution)/shard_map/while/body/eval_jaxpr/dot_general | solution.py:42
  973.7 24.0 %select_add_fusion.2 = f32[14336,512]{1,0:T(8,128)} fusion(f32[14336,512]{1,0:T(8,128)} %get-tuple-element.83, pred[]{:T(512)S(6)} %compare.14, bf16[4,256,14336]{2,1,0:T(8,128)(2,1)} %get-tuple-element.90, s32[]{:T(128)} %get-tuple-element.82, bf16[4,256,512]{2,1,0:T(8,128)(2,1)} %get-tuple-element.91), kind=kOutput, calls=%fused_computation.clone.1 | convolution fusion | flops 3780116480 | bytes 66323456 | tf_op jit(solution)/shard_map/while/body/eval_jaxpr/dot_general | solution.py:42
  997.7 21.9 %broadcast_multiply_fusion = f32[14336,512]{1,0:T(8,128)} fusion(f32[14336,512]{1,0:T(8,128)} %get-tuple-element.27), kind=kLoop, calls=%fused_computation.6 | loop fusion | flops 7340032 | bytes 58720256 | tf_op jit(solution)/shard_map/div | solution.py:49
  (3 shorter events, 0.0 us)
Async XLA Ops:
  6.5 80.0 %all-gather.9.cloned.1.call-start = ((), (), s32[]{:S(2)}) async-start(), calls=%async_computation.5 | async-start | bytes 8912896 | tf_op jit(solution)/shard_map/all_gather | solution.py:20
  7.3 130.3 %all-gather.5.cloned.1.call-start = ((), (), s32[]{:S(2)}) async-start(), calls=%async_computation.2 | async-start | bytes 5505024 | tf_op jit(solution)/shard_map/all_gather | solution.py:12
  8.0 192.0 %reduce-scatter.5.cloned.1.call-start = ((), (), s32[]{:S(2)}) async-start(), calls=%async_computation.6 | async-start | bytes 3145728 | tf_op jit(solution)/shard_map/reduce_scatter | solution.py:22
  97.0 644.0 %reduce-scatter.3.cloned.1.call-start = ((), (), s32[]{:S(2)}) async-start(), calls=%async_computation.3 | async-start | bytes 62390272 | tf_op jit(solution)/shard_map/reduce_scatter | solution.py:16
  199.2 0.7 copy-start
  199.3 563.5 %all-gather.11.cloned.1.call-start = ((), (), s32[]{:S(2)}) async-start(), calls=%async_computation.7 | async-start | bytes 1572864 | tf_op jit(solution)/shard_map/all_gather | solution.py:37
  202.2 710.3 %all-gather.7.cloned.1.call-start = ((), (), s32[]{:S(2)}) async-start(), calls=%async_computation.4 | async-start | bytes 31195136 | tf_op jit(solution)/shard_map/all_gather | solution.py:19
Sparse Core Ops, SparseCore 0:
  9.5 77.0 all-gather.8
  88.1 49.3 all-gather.4
  139.8 31.8 reduce-scatter.4
  199.4 541.5 reduce-scatter.2
  742.3 20.3 all-gather.10
  764.2 148.2 all-gather.6
where the time goes:
time: 1030 us
  waiting for transfers between devices  827 us (80%)
  matrix products  157 us (15%)
  other arithmetic  27.6 us (3%)
  between operations  13.5 us (1%)
    reduce_scatter x1, waiting for transfers between devices, body(): lax.psum_scatter(partial_value, ('seq', 'col'), scatter_dimension=0, tile...  539 us
    all_gather x1, waiting for transfers between devices, body(): grad_proj = lax.all_gather(shared, ('seq', 'col'), axis=0, tiled=True)  150 us
    dot_general x4, matrix products, accumulate(): lax.dot_general(pair[0], pair[1], (((0,), (0,)), ((), ())), preferred_ele...  85.2 us
    all_gather x1, waiting for transfers between devices, body(): act_full = lax.all_gather(acts, ('seq', 'col'), axis=0, tiled=True)  78.5 us
    dot_general x1, matrix products, body(): jnp.dot(lax.all_gather(grads, 'row', axis=0, tiled=True), out_basis, pref...  61.7 us
    all_gather x1, waiting for transfers between devices, body(): lax.all_gather(grads, 'row', axis=0, tiled=True)  40.5 us
    div x1, other arithmetic, body(): return total / (seq_count * SEQ_LEN)  21.9 us
  transfers between devices with their start and end apart: 6, of which 5 were waited for; matrix products, arithmetic and copies ran while one was open for 8% of the time, Pallas kernels for 0%

commit v1 on v0

v1 whole, which is shorter than its diff:
```python
import jax
import jax.numpy as jnp
from jax import lax
from jax.experimental import pallas as pl
from jax.experimental.pallas import tpu as pltpu
from jax.sharding import PartitionSpec as P


SEQ_LEN = 256
WINDOWS = 3
F32 = jnp.float32
BF16 = jnp.bfloat16
PLAN = (1, 2, 2, 2, 2, 2, 2, 1)
PARTS = 14
ORDER = (
    (0, 0), (1, 0), (0, 1), (2, 0), (1, 1), (0, 2), (3, 0), (0, 3), (2, 1), (3, 1),
    (1, 2), (4, 0), (0, 4), (1, 3), (2, 2), (4, 1), (0, 5), (5, 0), (3, 2), (1, 4),
    (2, 3), (5, 1), (6, 0), (4, 2), (1, 5), (0, 6), (3, 3), (6, 1), (0, 7), (2, 4),
    (4, 3), (7, 0), (3, 4), (7, 1), (5, 2), (2, 5), (1, 6), (1, 7), (4, 4), (3, 5),
    (6, 2), (5, 3), (7, 2), (4, 5), (6, 3), (2, 6), (2, 7), (5, 4), (7, 3), (3, 6),
    (6, 4), (3, 7), (5, 5), (7, 4), (4, 6), (4, 7), (6, 5), (7, 5), (5, 6), (5, 7),
    (6, 6), (6, 7), (7, 6), (7, 7),
)


def block_of(width, offset):
    for size in (512, 256, 128):
        if width % size == 0 and offset % size == 0:
            return size
    return width


def dot(lhs, rhs):
    return jnp.dot(lhs, rhs, preferred_element_type=F32)


def cost(flops, moved):
    return pl.CostEstimate(flops=flops, transcendentals=0, bytes_accessed=moved)


def project(where, lhs, basis, offset, width):
    rows = lhs.shape[0] // 4
    depth = lhs.shape[1]
    size = block_of(width, offset)
    start = offset // size

    def kernel(where_ref, lhs_ref, rhs_ref, send_ref, away_ref, own_ref, acc_ref):
        core, side = where_ref[0], where_ref[1]
        acc_ref[...] = dot(lhs_ref[...], rhs_ref[...])

        def quarter(c, s):
            at = pl.multiple_of((2 * c + s) * rows, rows)
            return acc_ref[pl.ds(at, rows), :]

        send_ref[:rows, :] = quarter(1 - core, 1 - side).astype(BF16)
        send_ref[rows:, :] = quarter(1 - core, side).astype(BF16)
        away_ref[...] = quarter(core, 1 - side).astype(BF16)
        own_ref[...] = quarter(core, side).astype(BF16)

    return pl.pallas_call(
        kernel,
        grid_spec=pltpu.PrefetchScalarGridSpec(
            num_scalar_prefetch=1,
            grid=(width // size,),
            in_specs=[
                pl.BlockSpec((4 * rows, depth), lambda i, w: (0, 0)),
                pl.BlockSpec((depth, size), lambda i, w: (0, start + i)),
            ],
            out_specs=[
                pl.BlockSpec((2 * rows, size), lambda i, w: (0, i)),
                pl.BlockSpec((rows, size), lambda i, w: (0, i)),
                pl.BlockSpec((rows, size), lambda i, w: (0, i)),
            ],
            scratch_shapes=[pltpu.VMEM((4 * rows, size), F32)],
        ),
        out_shape=[
            jax.ShapeDtypeStruct((2 * rows, width), BF16),
            jax.ShapeDtypeStruct((rows, width), BF16),
            jax.ShapeDtypeStruct((rows, width), BF16),
        ],
        cost_estimate=cost(8 * rows * depth * width, 2 * depth * width + 8 * rows * width),
    )(where, lhs, basis)


def finish(where, pieces, acts, out, shape, offset, width, scale):
    size = block_of(width, offset)
    start = offset // size
    window = acts[0].shape[0]
    part = window // 8
    columns = shape[1]
    in_specs = [pl.BlockSpec((p.shape[0], size), lambda i, w: (0, i)) for p in pieces]
    in_specs += [pl.BlockSpec(a.shape, lambda i, w: (0, 0)) for a in acts]
    args = [where, *pieces, *acts]
    alias = {}
    if out is not None:
        in_specs.append(pl.BlockSpec(memory_space=pl.ANY))
        alias = {len(args): 0}
        args.append(out)

    def kernel(where_ref, *refs):
        out_ref, proj_ref = refs[-2:]
        core, side, spot = where_ref[0], where_ref[1], where_ref[2]
        for number, piece in enumerate(refs[:4]):
            place = 2 * jnp.bitwise_xor(core, number // 2) + jnp.bitwise_xor(side, number % 2)
            for n in range(2 * WINDOWS):
                half = jnp.bitwise_xor(spot, 1 - n // WINDOWS)
                at = (n % WINDOWS) * window + (2 * place + half) * part
                proj_ref[pl.ds(pl.multiple_of(at, part), part), :] = piece[
                    n * part : (n + 1) * part, :
                ]
        total = None
        for (low, high), act_ref in zip(((0, 1), (0, 2), (1, 3), (2, 3)), refs[4:8]):
            one = lax.dot_general(
                proj_ref[low * window : high * window, :],
                act_ref[...],
                (((0,), (0,)), ((), ())),
                preferred_element_type=F32,
            )
            total = one * one if total is None else total + one * one
        out_ref[...] = total * scale

    return pl.pallas_call(
        kernel,
        grid_spec=pltpu.PrefetchScalarGridSpec(
            num_scalar_prefetch=1,
            grid=(width // size,),
            in_specs=in_specs,
            out_specs=pl.BlockSpec((size, columns), lambda i, w: (start + i, 0)),
            scratch_shapes=[pltpu.VMEM((WINDOWS * window, size), BF16)],
        ),
        out_shape=jax.ShapeDtypeStruct(shape, F32),
        input_output_aliases=alias,
        cost_estimate=cost(
            12 * window * width * columns, 4 * width * columns + 6 * window * width
        ),
    )(*args)


def body(grads, acts, out_basis, in_basis, lengths):
    col = lax.axis_index("col")
    core, side = col % 2, col // 2
    spot = lax.axis_index("seq")
    where = jnp.stack([core, side, spot % 2]).astype(jnp.int32)
    row_size = lax.axis_size("row")
    row = lax.axis_index("row")
    tokens = acts.shape[0] * lax.axis_size("seq") * lax.axis_size("col")
    live = WINDOWS * SEQ_LEN
    part = SEQ_LEN // 4

    def across_core(x):
        return lax.ppermute(x, "col", [(0, 1), (1, 0), (2, 3), (3, 2)])

    def across_side(x):
        return lax.ppermute(x, "col", [(0, 2), (2, 0), (1, 3), (3, 1)])

    def across_pair(x):
        return lax.ppermute(x, "seq", [(0, 1), (1, 0), (2, 3), (3, 2)])

    def across_half(x):
        return lax.ppermute(x, "seq", [(0, 2), (2, 0), (1, 3), (3, 1)])

    ends = jnp.cumsum(lengths)
    order = jnp.arange(live, dtype=jnp.int32)
    past = order[:, None] >= ends[None, :]
    owner = jnp.sum(past.astype(jnp.int32), axis=1)
    token_of = order + jnp.sum(jnp.where(past, SEQ_LEN - lengths[None, :], 0), axis=1)
    split = token_of.reshape(WINDOWS, 4, 2, part // 2).transpose(1, 2, 0, 3)
    split = jnp.where(spot % 2 == 0, split[:, ::-1], split)
    grouped = split.reshape(live)

    def pick(chosen, first, count):
        ids = first + jnp.arange(count, dtype=jnp.int32)
        return (chosen[:, None] == ids[None, :]).astype(BF16)

    share = grads.shape[0]
    if row_size == 2:
        other = lax.ppermute(grads, "row", [(0, 1), (1, 0)])
        packed = dot(pick(grouped, row * share, share), grads) + dot(
            pick(grouped, (1 - row) * share, share), other
        )
    else:
        packed = dot(
            pick(grouped, 0, tokens), lax.all_gather(grads, "row", axis=0, tiled=True)
        )
    packed = packed.astype(BF16)

    def act_sets():
        held_rows = acts.shape[0]
        up, down = [acts], [acts]
        for step in range(3):
            up.append(lax.ppermute(up[-1], "seq", [(i, i + 1) for i in range(step, 3)]))
            down.append(lax.ppermute(down[-1], "seq", [(i + 1, i) for i in range(3 - step)]))
        blocks = [acts]
        for ahead in (1, 2, 3):
            blocks.append(jnp.where(spot + ahead < 4, down[ahead], up[4 - ahead]))
        first = jnp.concatenate([across_side(blocks[0]), across_side(blocks[2])], axis=0)
        second = across_side(jnp.concatenate([blocks[1], blocks[3]], axis=0))
        mine = jnp.concatenate([blocks[0], blocks[2], blocks[1], blocks[3]], axis=0)
        theirs = jnp.concatenate([first, second], axis=0)
        pieces = (mine, theirs, across_core(mine), across_core(theirs))
        place = (spot + jnp.array([0, 2, 1, 3], jnp.int32)) % 4
        ids = jnp.concatenate(
            [
                (
                    (place[:, None] * 4 + 2 * jnp.bitwise_xor(side, n % 2))
                    + jnp.bitwise_xor(core, n // 2)
                )
                * held_rows
                + jnp.arange(held_rows, dtype=jnp.int32)[None, :]
                for n in range(4)
            ]
        ).reshape(tokens)
        act_part = jnp.concatenate([dot(piece, in_basis) for piece in pieces], axis=0)
        if row_size == 2:
            act_sum = act_part + lax.ppermute(act_part, "row", [(0, 1), (1, 0)])
        else:
            act_sum = lax.psum(act_part, "row")
        chosen = (token_of[:, None] == ids[None, :]).astype(BF16)
        act_live = dot(chosen, act_sum.astype(BF16))

        def act_of(seq, low, high):
            span = slice(low * SEQ_LEN, high * SEQ_LEN)
            return jnp.where(owner[span, None] == seq, act_live[span], 0.0).astype(BF16)

        return act_of(0, 0, 1), act_of(1, 0, 2), act_of(2, 1, 3), act_of(3, 2, 3)

    sets = act_sets()
    unit = out_basis.shape[1] // PARTS
    shape = (out_basis.shape[1], in_basis.shape[1])
    rows = live // 4
    half = rows // 2
    held = [{} for _ in PLAN]
    out = None

    def total(*parts):
        value = parts[0].astype(F32)
        for more in parts[1:]:
            value = value + more.astype(F32)
        return value.astype(BF16)

    for chunk, stage in ORDER:
        h = held[chunk]
        width = PLAN[chunk] * unit
        offset = sum(PLAN[:chunk]) * unit
        if stage == 0:
            send, h["away"], h["own"] = project(where, packed, out_basis, offset, width)
        elif stage == 1:
            send = total(h["away"], h["core"][:rows])
        elif stage == 2:
            send = total(h["own"][:half], h["core"][rows : rows + half], h["side"][:half])
        elif stage == 3:
            h["own"] = (h["own"][half:], h["core"][rows + half :], h["side"][half:], h["pair"])
            send = total(*h["own"])
        elif stage == 4:
            send = h["mine"] = total(*h["own"], h["far_pair"])
        elif stage == 5:
            send = h["full"] = jnp.concatenate([h["theirs"], h["mine"]], axis=0)
        elif stage == 7:
            pieces = (h["full"], h["beside"], h["far"], h["last"])
            out = finish(where, pieces, sets, out, shape, offset, width, 1.0 / tokens)
        if stage == 0:
            h["core"] = across_core(send)
        elif stage == 1:
            h["side"] = across_side(send)
        elif stage == 2:
            h["pair"] = across_pair(send)
        elif stage == 3:
            h["far_pair"] = across_half(send)
        elif stage == 4:
            h["theirs"] = across_pair(send)
        elif stage == 5:
            h["beside"] = across_side(send)
            h["far"] = across_core(send)
        elif stage == 6:
            h["last"] = across_core(h["beside"])
    return out


def solution(mesh):
    in_specs = (
        P("row", ("seq", "col")),
        P(("seq", "col"), "row"),
        P(("seq", "col"), "row"),
        P("row", ("seq", "col")),
        P(),
    )
    out_specs = P("row", ("seq", "col"))

    return jax.shard_map(body, mesh=mesh, in_specs=in_specs, out_specs=out_specs, check_vma=False)
```

time: 1030 us -> 634 us (0.62)
  waiting for transfers between devices: 827 us -> 390 us
  Pallas kernels: 0 us -> 140 us
  matrix products: 157 us -> 17.1 us
  starting transfers between devices: 0.2 us -> 57.1 us
  between operations: 13.5 us -> 1.47 us
    reduce_scatter x2 -> x0, waiting for transfers between devices: 539 us -> none  [the longest x1 539 us: body(): lax.psum_scatter(partial_value, ('seq', 'col'), scatter_dimension=0, tile...]
    ppermute x0 -> x77, waiting for transfers between devices: none -> 390 us  [the longest x19 151 us: across_side(): return lax.ppermute(x, 'col', [(0, 2), (2, 0), (1, 3), (3, 1)])]
    all_gather x4 -> x0, waiting for transfers between devices: 287 us -> none  [the longest x1 150 us: body(): grad_proj = lax.all_gather(shared, ('seq', 'col'), axis=0, tiled=True)]
    dot_general x6 -> x7, matrix products: 157 us -> 17.1 us  [dot(): return jnp.dot(lhs, rhs, preferred_element_type=F32)]
    pallas_call x0 -> x16, Pallas kernels: none -> 140 us  [the longest x8 78.7 us: project(): pl.pallas_call(kernel, grid_spec=pltpu.PrefetchScalarGridSpec(num_scalar_...]
    ppermute x0 -> x77, starting transfers between devices: none -> 57.1 us  [the longest x19 21.8 us: across_side(): return lax.ppermute(x, 'col', [(0, 2), (2, 0), (1, 3), (3, 1)])]
    div x1 -> x0, other arithmetic: 21.9 us -> none  [body(): return total / (seq_count * SEQ_LEN)]
  transfers between devices with their start and end apart: 6 -> 77, of which waited for: 5 -> 36; matrix products, arithmetic and copies ran while one was open for 8% -> 6% of each run, Pallas kernels for 0% -> 21%
where the time goes in v1:
time: 634 us; the launch traced here: 630 us
  waiting for transfers between devices  390 us (62%)
  Pallas kernels  140 us (22%)
  starting transfers between devices  57.1 us (9%)
  other arithmetic  18.4 us (3%)
  matrix products  17.1 us (3%)
    ppermute x19, waiting for transfers between devices, across_side(): return lax.ppermute(x, 'col', [(0, 2), (2, 0), (1, 3), (3, 1)])  151 us
    ppermute x16, waiting for transfers between devices, across_pair(): return lax.ppermute(x, 'seq', [(0, 1), (1, 0), (2, 3), (3, 2)])  115 us
    ppermute x8, waiting for transfers between devices, across_half(): return lax.ppermute(x, 'seq', [(0, 2), (2, 0), (1, 3), (3, 1)])  102 us
    pallas_call x8, Pallas kernels, project(): pl.pallas_call(kernel, grid_spec=pltpu.PrefetchScalarGridSpec(num_scalar_...  78.7 us
    pallas_call x8, Pallas kernels, finish(): pl.pallas_call(kernel, grid_spec=pltpu.PrefetchScalarGridSpec(num_scalar_...  61.1 us
    ppermute x3, waiting for transfers between devices, act_sets(): lax.ppermute(down[-1], 'seq', [(i + 1, i) for i in range(3 - step)])  22.2 us
    ppermute x19, starting transfers between devices, across_side(): return lax.ppermute(x, 'col', [(0, 2), (2, 0), (1, 3), (3, 1)])  21.8 us
    dot_general x7, matrix products, dot(): return jnp.dot(lhs, rhs, preferred_element_type=F32)  17.1 us
  transfers between devices with their start and end apart: 77, of which 36 were waited for; matrix products, arithmetic and copies ran while one was open for 6% of the time, Pallas kernels for 21%

profile of v1, /device:TPU:0, one launch (start us, length us, event | category | flops | bytes accessed | tf_op | source)
XLA Modules:
  0.0 629.5 jit_solution(290525934435296300)
XLA Ops:
  21.4 11.8 %collective-permute-done.10 = bf16[64,4096]{1,0:T(8,128)(2,1)S(1)} collective-permute-done((bf16[64,4096]{1,0:T(8,128)(2,1)S(1)}, bf16[64,4096]{1,0:T(8,128)(2,1)S(1)}, u32[]{:S(2)}, u32[]{:S(2)}) %collective-permute-start.10) | collective-permute-done | bytes 524320 | tf_op jit(solution)/shard_map/ppermute | solution.py:192
  36.3 10.5 %collective-permute-done.14 = bf16[64,4096]{1,0:T(8,128)(2,1)S(1)} collective-permute-done((bf16[64,4096]{1,0:T(8,128)(2,1)S(1)}, bf16[64,4096]{1,0:T(8,128)(2,1)S(1)}, u32[]{:S(2)}, u32[]{:S(2)}) %collective-permute-start.14) | collective-permute-done | bytes 524320 | tf_op jit(solution)/shard_map/ppermute | solution.py:192
  63.4 10.7 %shard_map.70 = (bf16[384,2048]{1,0:T(8,128)(2,1)}, bf16[192,2048]{1,0:T(8,128)(2,1)}, bf16[192,2048]{1,0:T(8,128)(2,1)}) custom-call(s32[3]{0:T(128)} %pad_add_fusion.1.where_ref, bf16[768,1792]{1,0:T(8,128)(2,1)} %add_convert_fusion.lhs_ref, bf16[1792,14336]{1,0:T(8,128)(2,1)} %rhs_ref.15), custom_call_target="tpu_custom_call" | custom-call | flops 5637144576 | bytes 10485760 | tf_op jit(solution)/shard_map/pallas_call | solution.py:60
  74.0 10.7 %shard_map.69 = (bf16[384,2048]{1,0:T(8,128)(2,1)}, bf16[192,2048]{1,0:T(8,128)(2,1)}, bf16[192,2048]{1,0:T(8,128)(2,1)}) custom-call(s32[3]{0:T(128)} %pad_add_fusion.1.where_ref, bf16[768,1792]{1,0:T(8,128)(2,1)} %add_convert_fusion.lhs_ref, bf16[1792,14336]{1,0:T(8,128)(2,1)} %rhs_ref.15), custom_call_target="tpu_custom_call" | custom-call | flops 5637144576 | bytes 10485760 | tf_op jit(solution)/shard_map/pallas_call | solution.py:60
  84.7 10.7 %shard_map.68 = (bf16[384,2048]{1,0:T(8,128)(2,1)}, bf16[192,2048]{1,0:T(8,128)(2,1)}, bf16[192,2048]{1,0:T(8,128)(2,1)}) custom-call(s32[3]{0:T(128)} %pad_add_fusion.1.where_ref, bf16[768,1792]{1,0:T(8,128)(2,1)} %add_convert_fusion.lhs_ref, bf16[1792,14336]{1,0:T(8,128)(2,1)} %rhs_ref.15), custom_call_target="tpu_custom_call" | custom-call | flops 5637144576 | bytes 10485760 | tf_op jit(solution)/shard_map/pallas_call | solution.py:60
  95.3 10.7 %shard_map.67 = (bf16[384,2048]{1,0:T(8,128)(2,1)}, bf16[192,2048]{1,0:T(8,128)(2,1)}, bf16[192,2048]{1,0:T(8,128)(2,1)}) custom-call(s32[3]{0:T(128)} %pad_add_fusion.1.where_ref, bf16[768,1792]{1,0:T(8,128)(2,1)} %add_convert_fusion.lhs_ref, bf16[1792,14336]{1,0:T(8,128)(2,1)} %rhs_ref.15), custom_call_target="tpu_custom_call" | custom-call | flops 5637144576 | bytes 10485760 | tf_op jit(solution)/shard_map/pallas_call | solution.py:60
  113.8 10.7 %shard_map.66 = (bf16[384,2048]{1,0:T(8,128)(2,1)}, bf16[192,2048]{1,0:T(8,128)(2,1)}, bf16[192,2048]{1,0:T(8,128)(2,1)}) custom-call(s32[3]{0:T(128)} %pad_add_fusion.1.where_ref, bf16[768,1792]{1,0:T(8,128)(2,1)} %add_convert_fusion.lhs_ref, bf16[1792,14336]{1,0:T(8,128)(2,1)} %rhs_ref.15), custom_call_target="tpu_custom_call" | custom-call | flops 5637144576 | bytes 10485760 | tf_op jit(solution)/shard_map/pallas_call | solution.py:60
  124.5 10.9 %shard_map.65 = (bf16[384,2048]{1,0:T(8,128)(2,1)}, bf16[192,2048]{1,0:T(8,128)(2,1)}, bf16[192,2048]{1,0:T(8,128)(2,1)}) custom-call(s32[3]{0:T(128)} %pad_add_fusion.1.where_ref, bf16[768,1792]{1,0:T(8,128)(2,1)} %add_convert_fusion.lhs_ref, bf16[1792,14336]{1,0:T(8,128)(2,1)} %rhs_ref.15), custom_call_target="tpu_custom_call" | custom-call | flops 5637144576 | bytes 10485760 | tf_op jit(solution)/shard_map/pallas_call | solution.py:60
  173.5 9.5 %collective-permute-done.72 = bf16[96,1024]{1,0:T(8,128)(2,1)S(1)} collective-permute-done((bf16[96,1024]{1,0:T(8,128)(2,1)S(1)}, bf16[96,1024]{1,0:T(8,128)(2,1)S(1)}, u32[]{:S(2)}, u32[]{:S(2)}) %collective-permute-start.72) | collective-permute-done | bytes 196640 | tf_op jit(solution)/shard_map/ppermute | solution.py:160
  209.9 15.5 %collective-permute-done.54 = bf16[192,2048]{1,0:T(8,128)(2,1)S(1)} collective-permute-done((bf16[192,2048]{1,0:T(8,128)(2,1)S(1)}, bf16[192,2048]{1,0:T(8,128)(2,1)S(1)}, u32[]{:S(2)}, u32[]{:S(2)}) %collective-permute-start.54) | collective-permute-done | bytes 786464 | tf_op jit(solution)/shard_map/ppermute | solution.py:154
  226.7 15.5 %collective-permute-done.46 = bf16[192,2048]{1,0:T(8,128)(2,1)S(1)} collective-permute-done((bf16[192,2048]{1,0:T(8,128)(2,1)S(1)}, bf16[192,2048]{1,0:T(8,128)(2,1)S(1)}, u32[]{:S(2)}, u32[]{:S(2)}) %collective-permute-start.46) | collective-permute-done | bytes 786464 | tf_op jit(solution)/shard_map/ppermute | solution.py:154
  242.4 16.7 %collective-permute-done.38 = bf16[192,2048]{1,0:T(8,128)(2,1)S(1)} collective-permute-done((bf16[192,2048]{1,0:T(8,128)(2,1)S(1)}, bf16[192,2048]{1,0:T(8,128)(2,1)S(1)}, u32[]{:S(2)}, u32[]{:S(2)}) %collective-permute-start.38) | collective-permute-done | bytes 786464 | tf_op jit(solution)/shard_map/ppermute | solution.py:154
  260.4 39.7 %collective-permute-done.74.refs_1_ = bf16[192,1024]{1,0:T(8,128)(2,1)S(1)} collective-permute-done((bf16[192,1024]{1,0:T(8,128)(2,1)S(1)}, bf16[192,1024]{1,0:T(8,128)(2,1)S(1)}, u32[]{:S(2)}, u32[]{:S(2)}) %collective-permute-start.74) | collective-permute-done | bytes 393248 | tf_op jit(solution)/shard_map/ppermute | solution.py:154
  301.3 10.6 %collective-permute-done.63 = bf16[96,2048]{1,0:T(8,128)(2,1)S(1)} collective-permute-done((bf16[96,2048]{1,0:T(8,128)(2,1)S(1)}, bf16[96,2048]{1,0:T(8,128)(2,1)S(1)}, u32[]{:S(2)}, u32[]{:S(2)}) %collective-permute-start.63) | collective-permute-done | bytes 393248 | tf_op jit(solution)/shard_map/ppermute | solution.py:157
  312.5 9.7 %collective-permute-done.55 = bf16[96,2048]{1,0:T(8,128)(2,1)S(1)} collective-permute-done((bf16[96,2048]{1,0:T(8,128)(2,1)S(1)}, bf16[96,2048]{1,0:T(8,128)(2,1)S(1)}, u32[]{:S(2)}, u32[]{:S(2)}) %collective-permute-start.55) | collective-permute-done | bytes 393248 | tf_op jit(solution)/shard_map/ppermute | solution.py:157
  322.8 8.8 %collective-permute-done.47 = bf16[96,2048]{1,0:T(8,128)(2,1)S(1)} collective-permute-done((bf16[96,2048]{1,0:T(8,128)(2,1)S(1)}, bf16[96,2048]{1,0:T(8,128)(2,1)S(1)}, u32[]{:S(2)}, u32[]{:S(2)}) %collective-permute-start.47) | collective-permute-done | bytes 393248 | tf_op jit(solution)/shard_map/ppermute | solution.py:157
  332.2 8.7 %collective-permute-done.39 = bf16[96,2048]{1,0:T(8,128)(2,1)S(1)} collective-permute-done((bf16[96,2048]{1,0:T(8,128)(2,1)S(1)}, bf16[96,2048]{1,0:T(8,128)(2,1)S(1)}, u32[]{:S(2)}, u32[]{:S(2)}) %collective-permute-start.39) | collective-permute-done | bytes 393248 | tf_op jit(solution)/shard_map/ppermute | solution.py:157
  341.4 9.1 %collective-permute-done.31 = bf16[96,2048]{1,0:T(8,128)(2,1)S(1)} collective-permute-done((bf16[96,2048]{1,0:T(8,128)(2,1)S(1)}, bf16[96,2048]{1,0:T(8,128)(2,1)S(1)}, u32[]{:S(2)}, u32[]{:S(2)}) %collective-permute-start.31) | collective-permute-done | bytes 393248 | tf_op jit(solution)/shard_map/ppermute | solution.py:157
  351.1 9.4 %collective-permute-done.23 = bf16[96,2048]{1,0:T(8,128)(2,1)S(1)} collective-permute-done((bf16[96,2048]{1,0:T(8,128)(2,1)S(1)}, bf16[96,2048]{1,0:T(8,128)(2,1)S(1)}, u32[]{:S(2)}, u32[]{:S(2)}) %collective-permute-start.23) | collective-permute-done | bytes 393248 | tf_op jit(solution)/shard_map/ppermute | solution.py:157
  365.2 30.9 %collective-permute-done.64 = bf16[96,2048]{1,0:T(8,128)(2,1)S(1)} collective-permute-done((bf16[96,2048]{1,0:T(8,128)(2,1)S(1)}, bf16[96,2048]{1,0:T(8,128)(2,1)S(1)}, u32[]{:S(2)}, u32[]{:S(2)}) %collective-permute-start.64) | collective-permute-done | bytes 393248 | tf_op jit(solution)/shard_map/ppermute | solution.py:160
  396.4 25.0 %collective-permute-done.56 = bf16[96,2048]{1,0:T(8,128)(2,1)S(1)} collective-permute-done((bf16[96,2048]{1,0:T(8,128)(2,1)S(1)}, bf16[96,2048]{1,0:T(8,128)(2,1)S(1)}, u32[]{:S(2)}, u32[]{:S(2)}) %collective-permute-start.56) | collective-permute-done | bytes 393248 | tf_op jit(solution)/shard_map/ppermute | solution.py:160
  421.7 12.3 %collective-permute-done.48 = bf16[96,2048]{1,0:T(8,128)(2,1)S(1)} collective-permute-done((bf16[96,2048]{1,0:T(8,128)(2,1)S(1)}, bf16[96,2048]{1,0:T(8,128)(2,1)S(1)}, u32[]{:S(2)}, u32[]{:S(2)}) %collective-permute-start.48) | collective-permute-done | bytes 393248 | tf_op jit(solution)/shard_map/ppermute | solution.py:160
  465.7 8.4 %collective-permute-done.57 = bf16[96,2048]{1,0:T(8,128)(2,1)S(1)} collective-permute-done((bf16[96,2048]{1,0:T(8,128)(2,1)S(1)}, bf16[96,2048]{1,0:T(8,128)(2,1)S(1)}, u32[]{:S(2)}, u32[]{:S(2)}) %collective-permute-start.57) | collective-permute-done | bytes 393248 | tf_op jit(solution)/shard_map/ppermute | solution.py:157
  474.2 8.3 %collective-permute-done.49 = bf16[96,2048]{1,0:T(8,128)(2,1)S(1)} collective-permute-done((bf16[96,2048]{1,0:T(8,128)(2,1)S(1)}, bf16[96,2048]{1,0:T(8,128)(2,1)S(1)}, u32[]{:S(2)}, u32[]{:S(2)}) %collective-permute-start.49) | collective-permute-done | bytes 393248 | tf_op jit(solution)/shard_map/ppermute | solution.py:157
  491.1 8.3 %collective-permute-done.33 = bf16[96,2048]{1,0:T(8,128)(2,1)S(1)} collective-permute-done((bf16[96,2048]{1,0:T(8,128)(2,1)S(1)}, bf16[96,2048]{1,0:T(8,128)(2,1)S(1)}, u32[]{:S(2)}, u32[]{:S(2)}) %collective-permute-start.33) | collective-permute-done | bytes 393248 | tf_op jit(solution)/shard_map/ppermute | solution.py:157
  509.6 10.4 %collective-permute-done.58.refs_1_ = bf16[192,2048]{1,0:T(8,128)(2,1)} collective-permute-done((bf16[192,2048]{1,0:T(8,128)(2,1)S(1)}, bf16[192,2048]{1,0:T(8,128)(2,1)}, u32[]{:S(2)}, u32[]{:S(2)}) %collective-permute-start.58) | collective-permute-done | bytes 786464 | tf_op jit(solution)/shard_map/ppermute | solution.py:154
  522.9 13.9 %collective-permute-done.50.refs_1_ = bf16[192,2048]{1,0:T(8,128)(2,1)} collective-permute-done((bf16[192,2048]{1,0:T(8,128)(2,1)S(1)}, bf16[192,2048]{1,0:T(8,128)(2,1)}, u32[]{:S(2)}, u32[]{:S(2)}) %collective-permute-start.50) | collective-permute-done | bytes 786464 | tf_op jit(solution)/shard_map/ppermute | solution.py:154
  539.3 14.3 %collective-permute-done.42.refs_1_ = bf16[192,2048]{1,0:T(8,128)(2,1)} collective-permute-done((bf16[192,2048]{1,0:T(8,128)(2,1)S(1)}, bf16[192,2048]{1,0:T(8,128)(2,1)}, u32[]{:S(2)}, u32[]{:S(2)}) %collective-permute-start.42) | collective-permute-done | bytes 786464 | tf_op jit(solution)/shard_map/ppermute | solution.py:154
  571.0 8.3 %shard_map.74.refs_8_ = f32[14336,512]{1,0:T(8,128)} custom-call(s32[3]{0:T(128)} %pad_add_fusion.1.where_ref, bf16[192,2048]{1,0:T(8,128)(2,1)} %copy-done.4, bf16[192,2048]{1,0:T(8,128)(2,1)} %collective-permute-done.58.refs_1_, bf16[192,2048]{1,0:T(8,128)(2,1)} %copy-done.18, ...), custom_call_target="tpu_custom_call", output_to_operand_aliasing={{}: (9, {})} | custom-call | flops 3221225472 | bytes 7340032 | tf_op jit(solution)/shard_map/pallas_call | solution.py:122
  596.6 8.3 %shard_map.76.refs_8_ = f32[14336,512]{1,0:T(8,128)} custom-call(s32[3]{0:T(128)} %pad_add_fusion.1.where_ref, bf16[192,2048]{1,0:T(8,128)(2,1)} %copy-done.1, bf16[192,2048]{1,0:T(8,128)(2,1)} %collective-permute-done.42.refs_1_, bf16[192,2048]{1,0:T(8,128)(2,1)} %copy-done.20, ...), custom_call_target="tpu_custom_call", output_to_operand_aliasing={{}: (9, {})} | custom-call | flops 3221225472 | bytes 7340032 | tf_op jit(solution)/shard_map/pallas_call | solution.py:122
  605.5 8.3 %shard_map.77.refs_8_ = f32[14336,512]{1,0:T(8,128)} custom-call(s32[3]{0:T(128)} %pad_add_fusion.1.where_ref, bf16[192,2048]{1,0:T(8,128)(2,1)} %copy-done, bf16[192,2048]{1,0:T(8,128)(2,1)} %collective-permute-done.34.refs_1_, bf16[192,2048]{1,0:T(8,128)(2,1)} %collective-permute-done.35.refs_2_, ...), custom_call_target="tpu_custom_call", output_to_operand_aliasing={{}: (9, {})} | custom-call | flops 3221225472 | bytes 7340032 | tf_op jit(solution)/shard_map/pallas_call | solution.py:122
  613.8 8.3 %shard_map.78.refs_8_ = f32[14336,512]{1,0:T(8,128)} custom-call(s32[3]{0:T(128)} %pad_add_fusion.1.where_ref, bf16[192,2048]{1,0:T(8,128)(2,1)} %copy-done.3, bf16[192,2048]{1,0:T(8,128)(2,1)} %copy-done.21, bf16[192,2048]{1,0:T(8,128)(2,1)} %collective-permute-done.27.refs_2_, ...), custom_call_target="tpu_custom_call", output_to_operand_aliasing={{}: (9, {})} | custom-call | flops 3221225472 | bytes 7340032 | tf_op jit(solution)/shard_map/pallas_call | solution.py:122
  (321 shorter events, 223.1 us)
Async XLA Ops:
  8.9 44.0 %collective-permute-start = (bf16[512,1792]{1,0:T(8,128)(2,1)}, bf16[512,1792]{1,0:T(8,128)(2,1)S(1)}, u32[]{:S(2)}, u32[]{:S(2)}) collective-permute-start(bf16[512,1792]{1,0:T(8,128)(2,1)} %param.6), channel_id=1, source_target_pairs={{0,4},{4,0},{1,5},{5,1},{2,6},{6,2},{3,7},{7,3},{8,12},{12,8},{9,1... | collective-permute-start | bytes 5505032 | tf_op jit(solution)/shard_map/ppermute | solution.py:177
  48.0 90.1 %collective-permute-start.17 = (bf16[128,4096]{1,0:T(8,128)(2,1)}, bf16[128,4096]{1,0:T(8,128)(2,1)}, u32[]{:S(2)}, u32[]{:S(2)}) collective-permute-start(bf16[128,4096]{1,0:T(8,128)(2,1)} %pad_maximum_fusion.2), channel_id=1, source_target_pairs={{0,2},{2,0},{1,3},{3,1},{4,6},{6,4},{5,7},{7,5},{8,10},{10,8},{9,1... | collective-permute-start | bytes 3145736 | tf_op jit(solution)/shard_map/ppermute | solution.py:154
  50.0 148.1 %collective-permute-start.18 = (bf16[256,4096]{1,0:T(8,128)(2,1)}, bf16[256,4096]{1,0:T(8,128)(2,1)}, u32[]{:S(2)}, u32[]{:S(2)}) collective-permute-start(bf16[256,4096]{1,0:T(8,128)(2,1)} %pad_maximum_fusion), channel_id=1, source_target_pairs={{0,1},{1,0},{2,3},{3,2},{4,5},{5,4},{6,7},{7,6},{8,9},{9,8},{10,11... | collective-permute-start | bytes 6291464 | tf_op jit(solution)/shard_map/ppermute | solution.py:151
  124.5 43.2 %collective-permute-start.61 = (bf16[384,2048]{1,0:T(8,128)(2,1)}, bf16[384,2048]{1,0:T(8,128)(2,1)S(1)}, u32[]{:S(2)}, u32[]{:S(2)}) collective-permute-start(bf16[384,2048]{1,0:T(8,128)(2,1)} %get-tuple-element.48), channel_id=1, source_target_pairs={{0,1},{1,0},{2,3},{3,2},{4,5},{5,4},{6,7},{7,6},{8,9},{9,8},{10,11... | collective-permute-start | bytes 4718600 | tf_op jit(solution)/shard_map/ppermute | solution.py:151
  135.5 33.0 %collective-permute-start.53 = (bf16[384,2048]{1,0:T(8,128)(2,1)}, bf16[384,2048]{1,0:T(8,128)(2,1)S(1)}, u32[]{:S(2)}, u32[]{:S(2)}) collective-permute-start(bf16[384,2048]{1,0:T(8,128)(2,1)} %get-tuple-element.45), channel_id=1, source_target_pairs={{0,1},{1,0},{2,3},{3,2},{4,5},{5,4},{6,7},{7,6},{8,9},{9,8},{10,11... | collective-permute-start | bytes 4718600 | tf_op jit(solution)/shard_map/ppermute | solution.py:151
  183.0 178.1 %collective-permute-start.19 = (bf16[256,4096]{1,0:T(8,128)(2,1)S(1)}, bf16[256,4096]{1,0:T(8,128)(2,1)S(1)}, u32[]{:S(2)}, u32[]{:S(2)}) collective-permute-start(bf16[256,4096]{1,0:T(8,128)(2,1)S(1)} %constant_dynamic-update-slice_fusion), channel_id=1, source_target_pairs={{0,1},{1,0},{2,3},{3,2},{4,5},{5,4},{6,7},{7,6},{8,9},{9,8},{10,11... | collective-permute-start | bytes 6291464 | tf_op jit(solution)/shard_map/ppermute | solution.py:151
  195.8 29.6 %collective-permute-start.54 = (bf16[192,2048]{1,0:T(8,128)(2,1)S(1)}, bf16[192,2048]{1,0:T(8,128)(2,1)S(1)}, u32[]{:S(2)}, u32[]{:S(2)}) collective-permute-start(bf16[192,2048]{1,0:T(8,128)(2,1)S(1)} %add_convert_fusion.3), channel_id=1, source_target_pairs={{0,2},{2,0},{1,3},{3,1},{4,6},{6,4},{5,7},{7,5},{8,10},{10,8},{9,1... | collective-permute-start | bytes 2359304 | tf_op jit(solution)/shard_map/ppermute | solution.py:154
  197.1 45.1 %collective-permute-start.46 = (bf16[192,2048]{1,0:T(8,128)(2,1)S(1)}, bf16[192,2048]{1,0:T(8,128)(2,1)S(1)}, u32[]{:S(2)}, u32[]{:S(2)}) collective-permute-start(bf16[192,2048]{1,0:T(8,128)(2,1)S(1)} %add_convert_fusion.4), channel_id=1, source_target_pairs={{0,2},{2,0},{1,3},{3,1},{4,6},{6,4},{5,7},{7,5},{8,10},{10,8},{9,1... | collective-permute-start | bytes 2359304 | tf_op jit(solution)/shard_map/ppermute | solution.py:154
  198.1 61.0 %collective-permute-start.38 = (bf16[192,2048]{1,0:T(8,128)(2,1)S(1)}, bf16[192,2048]{1,0:T(8,128)(2,1)S(1)}, u32[]{:S(2)}, u32[]{:S(2)}) collective-permute-start(bf16[192,2048]{1,0:T(8,128)(2,1)S(1)} %add_convert_fusion.5), channel_id=1, source_target_pairs={{0,2},{2,0},{1,3},{3,1},{4,6},{6,4},{5,7},{7,5},{8,10},{10,8},{9,1... | collective-permute-start | bytes 2359304 | tf_op jit(solution)/shard_map/ppermute | solution.py:154
  208.5 91.6 %collective-permute-start.30 = (bf16[192,2048]{1,0:T(8,128)(2,1)S(1)}, bf16[192,2048]{1,0:T(8,128)(2,1)S(1)}, u32[]{:S(2)}, u32[]{:S(2)}) collective-permute-start(bf16[192,2048]{1,0:T(8,128)(2,1)S(1)} %add_convert_fusion.6), channel_id=1, source_target_pairs={{0,2},{2,0},{1,3},{3,1},{4,6},{6,4},{5,7},{7,5},{8,10},{10,8},{9,1... | collective-permute-start | bytes 2359304 | tf_op jit(solution)/shard_map/ppermute | solution.py:154
  225.4 75.4 %collective-permute-start.22 = (bf16[192,2048]{1,0:T(8,128)(2,1)S(1)}, bf16[192,2048]{1,0:T(8,128)(2,1)S(1)}, u32[]{:S(2)}, u32[]{:S(2)}) collective-permute-start(bf16[192,2048]{1,0:T(8,128)(2,1)S(1)} %add_convert_fusion.7), channel_id=1, source_target_pairs={{0,2},{2,0},{1,3},{3,1},{4,6},{6,4},{5,7},{7,5},{8,10},{10,8},{9,1... | collective-permute-start | bytes 2359304 | tf_op jit(solution)/shard_map/ppermute | solution.py:154
  242.2 210.7 %collective-permute-start.5 = (bf16[96,1024]{1,0:T(8,128)(2,1)S(1)}, bf16[96,1024]{1,0:T(8,128)(2,1)S(1)}, u32[]{:S(2)}, u32[]{:S(2)}) collective-permute-start(bf16[96,1024]{1,0:T(8,128)(2,1)S(1)} %add_convert_fusion.25), channel_id=1, source_target_pairs={{0,8},{8,0},{16,24},{24,16},{1,9},{9,1},{17,25},{25,17},{2,10},{10... | collective-permute-start | bytes 589832 | tf_op jit(solution)/shard_map/ppermute | solution.py:157
  259.1 41.0 %collective-permute-start.74 = (bf16[192,1024]{1,0:T(8,128)(2,1)S(1)}, bf16[192,1024]{1,0:T(8,128)(2,1)S(1)}, u32[]{:S(2)}, u32[]{:S(2)}) collective-permute-start(bf16[192,1024]{1,0:T(8,128)(2,1)S(1)} %pad_maximum_fusion.10.refs_0_), channel_id=1, source_target_pairs={{0,2},{2,0},{1,3},{3,1},{4,6},{6,4},{5,7},{7,5},{8,10},{10,8},{9,1... | collective-permute-start | bytes 1179656 | tf_op jit(solution)/shard_map/ppermute | solution.py:154
  300.1 152.9 %collective-permute-start.75 = (bf16[192,1024]{1,0:T(8,128)(2,1)S(1)}, bf16[192,1024]{1,0:T(8,128)(2,1)S(1)}, u32[]{:S(2)}, u32[]{:S(2)}) collective-permute-start(bf16[192,1024]{1,0:T(8,128)(2,1)S(1)} %pad_maximum_fusion.10.refs_0_), channel_id=1, source_target_pairs={{0,1},{1,0},{2,3},{3,2},{4,5},{5,4},{6,7},{7,6},{8,9},{9,8},{10,11... | collective-permute-start | bytes 1179656 | tf_op jit(solution)/shard_map/ppermute | solution.py:151
  300.2 154.9 %collective-permute-start.76 = (bf16[192,1024]{1,0:T(8,128)(2,1)S(1)}, bf16[192,1024]{1,0:T(8,128)(2,1)S(1)}, u32[]{:S(2)}, u32[]{:S(2)}) collective-permute-start(bf16[192,1024]{1,0:T(8,128)(2,1)S(1)} %collective-permute-done.74.refs_1_), channel_id=1, source_target_pairs={{0,1},{1,0},{2,3},{3,2},{4,5},{5,4},{6,7},{7,6},{8,9},{9,8},{10,11... | collective-permute-start | bytes 1179656 | tf_op jit(solution)/shard_map/ppermute | solution.py:151
  360.5 35.6 %collective-permute-start.64 = (bf16[96,2048]{1,0:T(8,128)(2,1)S(1)}, bf16[96,2048]{1,0:T(8,128)(2,1)S(1)}, u32[]{:S(2)}, u32[]{:S(2)}) collective-permute-start(bf16[96,2048]{1,0:T(8,128)(2,1)S(1)} %fusion.20), channel_id=1, source_target_pairs={{0,16},{16,0},{8,24},{24,8},{1,17},{17,1},{9,25},{25,9},{2,18},{18... | collective-permute-start | bytes 1179656 | tf_op jit(solution)/shard_map/ppermute | solution.py:160
  361.1 60.3 %collective-permute-start.56 = (bf16[96,2048]{1,0:T(8,128)(2,1)S(1)}, bf16[96,2048]{1,0:T(8,128)(2,1)S(1)}, u32[]{:S(2)}, u32[]{:S(2)}) collective-permute-start(bf16[96,2048]{1,0:T(8,128)(2,1)S(1)} %fusion.19), channel_id=1, source_target_pairs={{0,16},{16,0},{8,24},{24,8},{1,17},{17,1},{9,25},{25,9},{2,18},{18... | collective-permute-start | bytes 1179656 | tf_op jit(solution)/shard_map/ppermute | solution.py:160
  396.1 37.9 %collective-permute-start.48 = (bf16[96,2048]{1,0:T(8,128)(2,1)S(1)}, bf16[96,2048]{1,0:T(8,128)(2,1)S(1)}, u32[]{:S(2)}, u32[]{:S(2)}) collective-permute-start(bf16[96,2048]{1,0:T(8,128)(2,1)S(1)} %fusion.18), channel_id=1, source_target_pairs={{0,16},{16,0},{8,24},{24,8},{1,17},{17,1},{9,25},{25,9},{2,18},{18... | collective-permute-start | bytes 1179656 | tf_op jit(solution)/shard_map/ppermute | solution.py:160
  450.9 70.2 %collective-permute-start.20 = (f32[1024,512]{1,0:T(8,128)S(1)}, f32[1024,512]{1,0:T(8,128)S(1)}, u32[]{:S(2)}, u32[]{:S(2)}) collective-permute-start(f32[1024,512]{1,0:T(8,128)S(1)} %pad_maximum_fusion.1), channel_id=1, source_target_pairs={{0,4},{4,0},{1,5},{5,1},{2,6},{6,2},{3,7},{7,3},{8,12},{12,8},{9,1... | collective-permute-start | bytes 6291464 | tf_op jit(solution)/shard_map/ppermute | solution.py:215
  457.3 33.7 %collective-permute-start.41 = (bf16[96,2048]{1,0:T(8,128)(2,1)S(1)}, bf16[96,2048]{1,0:T(8,128)(2,1)S(1)}, u32[]{:S(2)}, u32[]{:S(2)}) collective-permute-start(bf16[96,2048]{1,0:T(8,128)(2,1)S(1)} %add_convert_fusion.16), channel_id=1, source_target_pairs={{0,8},{8,0},{16,24},{24,16},{1,9},{9,1},{17,25},{25,17},{2,10},{10... | collective-permute-start | bytes 1179656 | tf_op jit(solution)/shard_map/ppermute | solution.py:157
  465.7 33.7 %collective-permute-start.33 = (bf16[96,2048]{1,0:T(8,128)(2,1)S(1)}, bf16[96,2048]{1,0:T(8,128)(2,1)S(1)}, u32[]{:S(2)}, u32[]{:S(2)}) collective-permute-start(bf16[96,2048]{1,0:T(8,128)(2,1)S(1)} %add_convert_fusion.18), channel_id=1, source_target_pairs={{0,8},{8,0},{16,24},{24,16},{1,9},{9,1},{17,25},{25,17},{2,10},{10... | collective-permute-start | bytes 1179656 | tf_op jit(solution)/shard_map/ppermute | solution.py:157
  474.1 33.6 %collective-permute-start.25 = (bf16[96,2048]{1,0:T(8,128)(2,1)S(1)}, bf16[96,2048]{1,0:T(8,128)(2,1)S(1)}, u32[]{:S(2)}, u32[]{:S(2)}) collective-permute-start(bf16[96,2048]{1,0:T(8,128)(2,1)S(1)} %add_convert_fusion.20), channel_id=1, source_target_pairs={{0,8},{8,0},{16,24},{24,16},{1,9},{9,1},{17,25},{25,17},{2,10},{10... | collective-permute-start | bytes 1179656 | tf_op jit(solution)/shard_map/ppermute | solution.py:157
  519.9 33.7 %collective-permute-start.42 = (bf16[192,2048]{1,0:T(8,128)(2,1)S(1)}, bf16[192,2048]{1,0:T(8,128)(2,1)}, u32[]{:S(2)}, u32[]{:S(2)}) collective-permute-start(bf16[192,2048]{1,0:T(8,128)(2,1)S(1)} %pad_maximum_fusion.5.refs_0_), channel_id=1, source_target_pairs={{0,2},{2,0},{1,3},{3,1},{4,6},{6,4},{5,7},{7,5},{8,10},{10,8},{9,1... | collective-permute-start | bytes 2359304 | tf_op jit(solution)/shard_map/ppermute | solution.py:154
  521.1 33.7 %collective-permute-start.43 = (bf16[192,2048]{1,0:T(8,128)(2,1)S(1)}, bf16[192,2048]{1,0:T(8,128)(2,1)S(1)}, u32[]{:S(2)}, u32[]{:S(2)}) collective-permute-start(bf16[192,2048]{1,0:T(8,128)(2,1)S(1)} %pad_maximum_fusion.5.refs_0_), channel_id=1, source_target_pairs={{0,1},{1,0},{2,3},{3,2},{4,5},{5,4},{6,7},{7,6},{8,9},{9,8},{10,11... | collective-permute-start | bytes 2359304 | tf_op jit(solution)/shard_map/ppermute | solution.py:151
  521.1 33.7 %collective-permute-start.68 = (bf16[192,2048]{1,0:T(8,128)(2,1)S(1)}, bf16[192,2048]{1,0:T(8,128)(2,1)S(1)}, u32[]{:S(2)}, u32[]{:S(2)}) collective-permute-start(bf16[192,2048]{1,0:T(8,128)(2,1)S(1)} %collective-permute-done.66.refs_1_), channel_id=1, source_target_pairs={{0,1},{1,0},{2,3},{3,2},{4,5},{5,4},{6,7},{7,6},{8,9},{9,8},{10,11... | collective-permute-start | bytes 2359304 | tf_op jit(solution)/shard_map/ppermute | solution.py:151
  536.8 33.7 %collective-permute-start.34 = (bf16[192,2048]{1,0:T(8,128)(2,1)S(1)}, bf16[192,2048]{1,0:T(8,128)(2,1)}, u32[]{:S(2)}, u32[]{:S(2)}) collective-permute-start(bf16[192,2048]{1,0:T(8,128)(2,1)S(1)} %pad_maximum_fusion.4.refs_0_), channel_id=1, source_target_pairs={{0,2},{2,0},{1,3},{3,1},{4,6},{6,4},{5,7},{7,5},{8,10},{10,8},{9,1... | collective-permute-start | bytes 2359304 | tf_op jit(solution)/shard_map/ppermute | solution.py:154
  538.0 32.5 %collective-permute-start.60 = (bf16[192,2048]{1,0:T(8,128)(2,1)}, bf16[192,2048]{1,0:T(8,128)(2,1)}, u32[]{:S(2)}, u32[]{:S(2)}) collective-permute-start(bf16[192,2048]{1,0:T(8,128)(2,1)} %collective-permute-done.58.refs_1_), channel_id=1, source_target_pairs={{0,1},{1,0},{2,3},{3,2},{4,5},{5,4},{6,7},{7,6},{8,9},{9,8},{10,11... | collective-permute-start | bytes 2359304 | tf_op jit(solution)/shard_map/ppermute | solution.py:151
  553.6 32.6 %collective-permute-start.26 = (bf16[192,2048]{1,0:T(8,128)(2,1)S(1)}, bf16[192,2048]{1,0:T(8,128)(2,1)S(1)}, u32[]{:S(2)}, u32[]{:S(2)}) collective-permute-start(bf16[192,2048]{1,0:T(8,128)(2,1)S(1)} %pad_maximum_fusion.3.refs_0_), channel_id=1, source_target_pairs={{0,2},{2,0},{1,3},{3,1},{4,6},{6,4},{5,7},{7,5},{8,10},{10,8},{9,1... | collective-permute-start | bytes 2359304 | tf_op jit(solution)/shard_map/ppermute | solution.py:154
  554.8 32.6 %collective-permute-start.52 = (bf16[192,2048]{1,0:T(8,128)(2,1)}, bf16[192,2048]{1,0:T(8,128)(2,1)S(1)}, u32[]{:S(2)}, u32[]{:S(2)}) collective-permute-start(bf16[192,2048]{1,0:T(8,128)(2,1)} %collective-permute-done.50.refs_1_), channel_id=1, source_target_pairs={{0,1},{1,0},{2,3},{3,2},{4,5},{5,4},{6,7},{7,6},{8,9},{9,8},{10,11... | collective-permute-start | bytes 2359304 | tf_op jit(solution)/shard_map/ppermute | solution.py:151
  554.9 32.6 %collective-permute-start.44 = (bf16[192,2048]{1,0:T(8,128)(2,1)}, bf16[192,2048]{1,0:T(8,128)(2,1)}, u32[]{:S(2)}, u32[]{:S(2)}) collective-permute-start(bf16[192,2048]{1,0:T(8,128)(2,1)} %collective-permute-done.42.refs_1_), channel_id=1, source_target_pairs={{0,1},{1,0},{2,3},{3,2},{4,5},{5,4},{6,7},{7,6},{8,9},{9,8},{10,11... | collective-permute-start | bytes 2359304 | tf_op jit(solution)/shard_map/ppermute | solution.py:151
  570.5 34.5 %collective-permute-start.35 = (bf16[192,2048]{1,0:T(8,128)(2,1)S(1)}, bf16[192,2048]{1,0:T(8,128)(2,1)}, u32[]{:S(2)}, u32[]{:S(2)}) collective-permute-start(bf16[192,2048]{1,0:T(8,128)(2,1)S(1)} %pad_maximum_fusion.4.refs_0_), channel_id=1, source_target_pairs={{0,1},{1,0},{2,3},{3,2},{4,5},{5,4},{6,7},{7,6},{8,9},{9,8},{10,11... | collective-permute-start | bytes 2359304 | tf_op jit(solution)/shard_map/ppermute | solution.py:151
  570.5 35.0 %collective-permute-start.36 = (bf16[192,2048]{1,0:T(8,128)(2,1)}, bf16[192,2048]{1,0:T(8,128)(2,1)}, u32[]{:S(2)}, u32[]{:S(2)}) collective-permute-start(bf16[192,2048]{1,0:T(8,128)(2,1)} %collective-permute-done.34.refs_1_), channel_id=1, source_target_pairs={{0,1},{1,0},{2,3},{3,2},{4,5},{5,4},{6,7},{7,6},{8,9},{9,8},{10,11... | collective-permute-start | bytes 2359304 | tf_op jit(solution)/shard_map/ppermute | solution.py:151
  (97 other events, 1906.1 us)

commit v2 on v1

--- a/solution.py
+++ b/solution.py
@@ -78,6 +78,7 @@
             jax.ShapeDtypeStruct((rows, width), BF16),
             jax.ShapeDtypeStruct((rows, width), BF16),
         ],
+        compiler_params=pltpu.CompilerParams(vmem_limit_bytes=20 * 2**20),
         cost_estimate=cost(8 * rows * depth * width, 2 * depth * width + 8 * rows * width),
     )(where, lhs, basis)
 
@@ -108,10 +109,11 @@
                 proj_ref[pl.ds(pl.multiple_of(at, part), part), :] = piece[
                     n * part : (n + 1) * part, :
                 ]
+        last = pl.multiple_of(where_ref[3], 16)
         total = None
-        for (low, high), act_ref in zip(((0, 1), (0, 2), (1, 3), (2, 3)), refs[4:8]):
+        for low, act_ref in zip((0, window, 2 * window, last), refs[4:8]):
             one = lax.dot_general(
-                proj_ref[low * window : high * window, :],
+                proj_ref[pl.ds(low, window), :],
                 act_ref[...],
                 (((0,), (0,)), ((), ())),
                 preferred_element_type=F32,
@@ -130,8 +132,9 @@
         ),
         out_shape=jax.ShapeDtypeStruct(shape, F32),
         input_output_aliases=alias,
+        compiler_params=pltpu.CompilerParams(vmem_limit_bytes=16 * 2**20),
         cost_estimate=cost(
-            12 * window * width * columns, 4 * width * columns + 6 * window * width
+            8 * window * width * columns, 4 * width * columns + 6 * window * width
         ),
     )(*args)
 
@@ -140,7 +143,6 @@
     col = lax.axis_index("col")
     core, side = col % 2, col // 2
     spot = lax.axis_index("seq")
-    where = jnp.stack([core, side, spot % 2]).astype(jnp.int32)
     row_size = lax.axis_size("row")
     row = lax.axis_index("row")
     tokens = acts.shape[0] * lax.axis_size("seq") * lax.axis_size("col")
@@ -159,11 +161,24 @@
     def across_half(x):
         return lax.ppermute(x, "seq", [(0, 2), (2, 0), (1, 3), (3, 1)])
 
-    ends = jnp.cumsum(lengths)
+    ids = jnp.arange(lengths.shape[0], dtype=jnp.int32)
+    longer = (lengths[None, :] > lengths[:, None]) | (
+        (lengths[None, :] == lengths[:, None]) & (ids[None, :] < ids[:, None])
+    )
+    rank = jnp.sum(longer.astype(jnp.int32), axis=1)
+    slot = jnp.where(rank == 2, 3, jnp.where(rank == 3, 2, rank))
+    held_by = slot[None, :] == ids[:, None]
+    size_of = jnp.sum(jnp.where(held_by, lengths[None, :], 0), axis=1)
+    seq_of = jnp.sum(jnp.where(held_by, ids[None, :], 0), axis=1)
+    stop = jnp.sum(jnp.where(ids[None, :] <= ids[:, None], size_of[None, :], 0), axis=1)
     order = jnp.arange(live, dtype=jnp.int32)
-    past = order[:, None] >= ends[None, :]
-    owner = jnp.sum(past.astype(jnp.int32), axis=1)
-    token_of = order + jnp.sum(jnp.where(past, SEQ_LEN - lengths[None, :], 0), axis=1)
+    past = (order[:, None] >= stop[None, :]).astype(jnp.int32)
+    owner = jnp.sum(past, axis=1)
+    shift = seq_of * SEQ_LEN - (stop - size_of)
+    inside = owner[:, None] == ids[None, :]
+    token_of = order + jnp.sum(jnp.where(inside, shift[None, :], 0), axis=1)
+    third = stop[1] // 16 * 16
+    where = jnp.stack([core, side, spot % 2, third]).astype(jnp.int32)
     split = token_of.reshape(WINDOWS, 4, 2, part // 2).transpose(1, 2, 0, 3)
     split = jnp.where(spot % 2 == 0, split[:, ::-1], split)
     grouped = split.reshape(live)
@@ -193,13 +208,14 @@
         blocks = [acts]
         for ahead in (1, 2, 3):
             blocks.append(jnp.where(spot + ahead < 4, down[ahead], up[4 - ahead]))
-        first = jnp.concatenate([across_side(blocks[0]), across_side(blocks[2])], axis=0)
+        first = across_side(blocks[0])
+        first = jnp.concatenate([first, across_side(blocks[2])], axis=0)
         second = across_side(jnp.concatenate([blocks[1], blocks[3]], axis=0))
         mine = jnp.concatenate([blocks[0], blocks[2], blocks[1], blocks[3]], axis=0)
         theirs = jnp.concatenate([first, second], axis=0)
         pieces = (mine, theirs, across_core(mine), across_core(theirs))
         place = (spot + jnp.array([0, 2, 1, 3], jnp.int32)) % 4
-        ids = jnp.concatenate(
+        token_ids = jnp.concatenate(
             [
                 (
                     (place[:, None] * 4 + 2 * jnp.bitwise_xor(side, n % 2))
@@ -215,14 +231,15 @@
             act_sum = act_part + lax.ppermute(act_part, "row", [(0, 1), (1, 0)])
         else:
             act_sum = lax.psum(act_part, "row")
-        chosen = (token_of[:, None] == ids[None, :]).astype(BF16)
+        chosen = (token_of[:, None] == token_ids[None, :]).astype(BF16)
         act_live = dot(chosen, act_sum.astype(BF16))
 
-        def act_of(seq, low, high):
-            span = slice(low * SEQ_LEN, high * SEQ_LEN)
-            return jnp.where(owner[span, None] == seq, act_live[span], 0.0).astype(BF16)
-
-        return act_of(0, 0, 1), act_of(1, 0, 2), act_of(2, 1, 3), act_of(3, 2, 3)
+        def act_of(slot, low):
+            mine = lax.dynamic_slice_in_dim(owner, low, SEQ_LEN)[:, None] == slot
+            rows = lax.dynamic_slice_in_dim(act_live, low, SEQ_LEN)
+            return jnp.where(mine, rows, 0.0).astype(BF16)
+
+        return act_of(0, 0), act_of(1, SEQ_LEN), act_of(3, 2 * SEQ_LEN), act_of(2, third)
 
     sets = act_sets()
     unit = out_basis.shape[1] // PARTS

time: 634 us -> 618 us (0.975)
  Pallas kernels: 140 us -> 106 us
  waiting for transfers between devices: 390 us -> 408 us
    pallas_call x8, Pallas kernels: 61.1 us -> 41.1 us  [finish(): pl.pallas_call(kernel, grid_spec=pltpu.PrefetchScalarGridSpec(num_scalar_...]
    ppermute x19, waiting for transfers between devices: 151 us -> 170 us  [across_side(): return lax.ppermute(x, 'col', [(0, 2), (2, 0), (1, 3), (3, 1)])]
    pallas_call x8, Pallas kernels: 78.7 us -> 65.2 us  [project(): pl.pallas_call(kernel, grid_spec=pltpu.PrefetchScalarGridSpec(num_scalar_...]
  transfers between devices with their start and end apart: 77 -> 77, of which waited for: 36 -> 35; matrix products, arithmetic and copies ran while one was open for 6% -> 5% of each run, Pallas kernels for 21% -> 17%
where the time goes in v2:
time: 618 us; the launch traced here: 615 us
  waiting for transfers between devices  408 us (66%)
  Pallas kernels  106 us (17%)
  starting transfers between devices  60.8 us (10%)
  other arithmetic  17.2 us (3%)
  matrix products  14.1 us (2%)
    ppermute x19, waiting for transfers between devices, across_side(): return lax.ppermute(x, 'col', [(0, 2), (2, 0), (1, 3), (3, 1)])  170 us
    ppermute x16, waiting for transfers between devices, across_pair(): return lax.ppermute(x, 'seq', [(0, 1), (1, 0), (2, 3), (3, 2)])  116 us
    ppermute x8, waiting for transfers between devices, across_half(): return lax.ppermute(x, 'seq', [(0, 2), (2, 0), (1, 3), (3, 1)])  98.9 us
    pallas_call x8, Pallas kernels, project(): pl.pallas_call(kernel, grid_spec=pltpu.PrefetchScalarGridSpec(num_scalar_...  65.2 us
    pallas_call x8, Pallas kernels, finish(): pl.pallas_call(kernel, grid_spec=pltpu.PrefetchScalarGridSpec(num_scalar_...  41.1 us
    ppermute x3, waiting for transfers between devices, act_sets(): lax.ppermute(down[-1], 'seq', [(i + 1, i) for i in range(3 - step)])  22.8 us
    ppermute x19, starting transfers between devices, across_side(): return lax.ppermute(x, 'col', [(0, 2), (2, 0), (1, 3), (3, 1)])  21.3 us
    dot_general x7, matrix products, dot(): return jnp.dot(lhs, rhs, preferred_element_type=F32)  14.1 us
  transfers between devices with their start and end apart: 77, of which 35 were waited for; matrix products, arithmetic and copies ran while one was open for 5% of the time, Pallas kernels for 17%

profile of v2, /device:TPU:0, one launch (start us, length us, event | category | flops | bytes accessed | tf_op | source)
XLA Modules:
  0.0 614.6 jit_solution(11388022219451043141)
XLA Ops:
  24.3 12.3 %collective-permute-done.10 = bf16[64,4096]{1,0:T(8,128)(2,1)S(1)} collective-permute-done((bf16[64,4096]{1,0:T(8,128)(2,1)S(1)}, bf16[64,4096]{1,0:T(8,128)(2,1)S(1)}, u32[]{:S(2)}, u32[]{:S(2)}) %collective-permute-start.10) | collective-permute-done | bytes 524320 | tf_op jit(solution)/shard_map/ppermute | solution.py:207
  39.7 10.5 %collective-permute-done.14 = bf16[64,4096]{1,0:T(8,128)(2,1)S(1)} collective-permute-done((bf16[64,4096]{1,0:T(8,128)(2,1)S(1)}, bf16[64,4096]{1,0:T(8,128)(2,1)S(1)}, u32[]{:S(2)}, u32[]{:S(2)}) %collective-permute-start.14) | collective-permute-done | bytes 524320 | tf_op jit(solution)/shard_map/ppermute | solution.py:207
  61.2 9.0 %shard_map.70 = (bf16[384,2048]{1,0:T(8,128)(2,1)S(1)}, bf16[192,2048]{1,0:T(8,128)(2,1)S(1)}, bf16[192,2048]{1,0:T(8,128)(2,1)S(1)}) custom-call(s32[4]{0:T(128)S(1)} %pad_add_fusion.1.where_ref, bf16[768,1792]{1,0:T(8,128)(2,1)S(1)} %add_convert_fusion.lhs_ref, bf16[1792,14336]{1,0:T(8,128)(2,1)} %rhs_ref.15), custom_call_target="tpu_custom_call" | custom-call | flops 5637144576 | bytes 10485760 | tf_op jit(solution)/shard_map/pallas_call | solution.py:60
  70.2 9.0 %shard_map.69 = (bf16[384,2048]{1,0:T(8,128)(2,1)S(1)}, bf16[192,2048]{1,0:T(8,128)(2,1)S(1)}, bf16[192,2048]{1,0:T(8,128)(2,1)S(1)}) custom-call(s32[4]{0:T(128)S(1)} %pad_add_fusion.1.where_ref, bf16[768,1792]{1,0:T(8,128)(2,1)S(1)} %add_convert_fusion.lhs_ref, bf16[1792,14336]{1,0:T(8,128)(2,1)} %rhs_ref.15), custom_call_target="tpu_custom_call" | custom-call | flops 5637144576 | bytes 10485760 | tf_op jit(solution)/shard_map/pallas_call | solution.py:60
  79.3 9.0 %shard_map.68 = (bf16[384,2048]{1,0:T(8,128)(2,1)S(1)}, bf16[192,2048]{1,0:T(8,128)(2,1)S(1)}, bf16[192,2048]{1,0:T(8,128)(2,1)S(1)}) custom-call(s32[4]{0:T(128)S(1)} %pad_add_fusion.1.where_ref, bf16[768,1792]{1,0:T(8,128)(2,1)S(1)} %add_convert_fusion.lhs_ref, bf16[1792,14336]{1,0:T(8,128)(2,1)} %rhs_ref.15), custom_call_target="tpu_custom_call" | custom-call | flops 5637144576 | bytes 10485760 | tf_op jit(solution)/shard_map/pallas_call | solution.py:60
  88.3 9.0 %shard_map.67 = (bf16[384,2048]{1,0:T(8,128)(2,1)S(1)}, bf16[192,2048]{1,0:T(8,128)(2,1)S(1)}, bf16[192,2048]{1,0:T(8,128)(2,1)S(1)}) custom-call(s32[4]{0:T(128)S(1)} %pad_add_fusion.1.where_ref, bf16[768,1792]{1,0:T(8,128)(2,1)S(1)} %add_convert_fusion.lhs_ref, bf16[1792,14336]{1,0:T(8,128)(2,1)} %rhs_ref.15), custom_call_target="tpu_custom_call" | custom-call | flops 5637144576 | bytes 10485760 | tf_op jit(solution)/shard_map/pallas_call | solution.py:60
  103.4 9.0 %shard_map.66 = (bf16[384,2048]{1,0:T(8,128)(2,1)S(1)}, bf16[192,2048]{1,0:T(8,128)(2,1)S(1)}, bf16[192,2048]{1,0:T(8,128)(2,1)S(1)}) custom-call(s32[4]{0:T(128)S(1)} %pad_add_fusion.1.where_ref, bf16[768,1792]{1,0:T(8,128)(2,1)S(1)} %add_convert_fusion.lhs_ref, bf16[1792,14336]{1,0:T(8,128)(2,1)} %rhs_ref.15), custom_call_target="tpu_custom_call" | custom-call | flops 5637144576 | bytes 10485760 | tf_op jit(solution)/shard_map/pallas_call | solution.py:60
  112.5 9.2 %shard_map.65 = (bf16[384,2048]{1,0:T(8,128)(2,1)S(1)}, bf16[192,2048]{1,0:T(8,128)(2,1)S(1)}, bf16[192,2048]{1,0:T(8,128)(2,1)S(1)}) custom-call(s32[4]{0:T(128)S(1)} %pad_add_fusion.1.where_ref, bf16[768,1792]{1,0:T(8,128)(2,1)S(1)} %add_convert_fusion.lhs_ref, bf16[1792,14336]{1,0:T(8,128)(2,1)} %rhs_ref.15), custom_call_target="tpu_custom_call" | custom-call | flops 5637144576 | bytes 10485760 | tf_op jit(solution)/shard_map/pallas_call | solution.py:60
  126.0 8.4 %collective-permute-done.70 = bf16[192,1024]{1,0:T(8,128)(2,1)S(1)} collective-permute-done((bf16[192,1024]{1,0:T(8,128)(2,1)S(1)}, bf16[192,1024]{1,0:T(8,128)(2,1)S(1)}, u32[]{:S(2)}, u32[]{:S(2)}) %collective-permute-start.70) | collective-permute-done | bytes 393248 | tf_op jit(solution)/shard_map/ppermute | solution.py:156
  159.2 9.5 %collective-permute-done.72 = bf16[96,1024]{1,0:T(8,128)(2,1)S(1)} collective-permute-done((bf16[96,1024]{1,0:T(8,128)(2,1)S(1)}, bf16[96,1024]{1,0:T(8,128)(2,1)S(1)}, u32[]{:S(2)}, u32[]{:S(2)}) %collective-permute-start.72) | collective-permute-done | bytes 196640 | tf_op jit(solution)/shard_map/ppermute | solution.py:162
  195.5 15.5 %collective-permute-done.54 = bf16[192,2048]{1,0:T(8,128)(2,1)S(1)} collective-permute-done((bf16[192,2048]{1,0:T(8,128)(2,1)S(1)}, bf16[192,2048]{1,0:T(8,128)(2,1)S(1)}, u32[]{:S(2)}, u32[]{:S(2)}) %collective-permute-start.54) | collective-permute-done | bytes 786464 | tf_op jit(solution)/shard_map/ppermute | solution.py:156
  212.3 15.5 %collective-permute-done.46 = bf16[192,2048]{1,0:T(8,128)(2,1)S(1)} collective-permute-done((bf16[192,2048]{1,0:T(8,128)(2,1)S(1)}, bf16[192,2048]{1,0:T(8,128)(2,1)S(1)}, u32[]{:S(2)}, u32[]{:S(2)}) %collective-permute-start.46) | collective-permute-done | bytes 786464 | tf_op jit(solution)/shard_map/ppermute | solution.py:156
  228.1 16.7 %collective-permute-done.38 = bf16[192,2048]{1,0:T(8,128)(2,1)S(1)} collective-permute-done((bf16[192,2048]{1,0:T(8,128)(2,1)S(1)}, bf16[192,2048]{1,0:T(8,128)(2,1)S(1)}, u32[]{:S(2)}, u32[]{:S(2)}) %collective-permute-start.38) | collective-permute-done | bytes 786464 | tf_op jit(solution)/shard_map/ppermute | solution.py:156
  246.0 39.7 %collective-permute-done.74.refs_1_ = bf16[192,1024]{1,0:T(8,128)(2,1)S(1)} collective-permute-done((bf16[192,1024]{1,0:T(8,128)(2,1)S(1)}, bf16[192,1024]{1,0:T(8,128)(2,1)S(1)}, u32[]{:S(2)}, u32[]{:S(2)}) %collective-permute-start.74) | collective-permute-done | bytes 393248 | tf_op jit(solution)/shard_map/ppermute | solution.py:156
  287.0 10.6 %collective-permute-done.63 = bf16[96,2048]{1,0:T(8,128)(2,1)S(1)} collective-permute-done((bf16[96,2048]{1,0:T(8,128)(2,1)S(1)}, bf16[96,2048]{1,0:T(8,128)(2,1)S(1)}, u32[]{:S(2)}, u32[]{:S(2)}) %collective-permute-start.63) | collective-permute-done | bytes 393248 | tf_op jit(solution)/shard_map/ppermute | solution.py:159
  298.2 9.7 %collective-permute-done.55 = bf16[96,2048]{1,0:T(8,128)(2,1)S(1)} collective-permute-done((bf16[96,2048]{1,0:T(8,128)(2,1)S(1)}, bf16[96,2048]{1,0:T(8,128)(2,1)S(1)}, u32[]{:S(2)}, u32[]{:S(2)}) %collective-permute-start.55) | collective-permute-done | bytes 393248 | tf_op jit(solution)/shard_map/ppermute | solution.py:159
  308.4 8.8 %collective-permute-done.47 = bf16[96,2048]{1,0:T(8,128)(2,1)S(1)} collective-permute-done((bf16[96,2048]{1,0:T(8,128)(2,1)S(1)}, bf16[96,2048]{1,0:T(8,128)(2,1)S(1)}, u32[]{:S(2)}, u32[]{:S(2)}) %collective-permute-start.47) | collective-permute-done | bytes 393248 | tf_op jit(solution)/shard_map/ppermute | solution.py:159
  317.8 8.7 %collective-permute-done.39 = bf16[96,2048]{1,0:T(8,128)(2,1)S(1)} collective-permute-done((bf16[96,2048]{1,0:T(8,128)(2,1)S(1)}, bf16[96,2048]{1,0:T(8,128)(2,1)S(1)}, u32[]{:S(2)}, u32[]{:S(2)}) %collective-permute-start.39) | collective-permute-done | bytes 393248 | tf_op jit(solution)/shard_map/ppermute | solution.py:159
  327.1 9.1 %collective-permute-done.31 = bf16[96,2048]{1,0:T(8,128)(2,1)S(1)} collective-permute-done((bf16[96,2048]{1,0:T(8,128)(2,1)S(1)}, bf16[96,2048]{1,0:T(8,128)(2,1)S(1)}, u32[]{:S(2)}, u32[]{:S(2)}) %collective-permute-start.31) | collective-permute-done | bytes 393248 | tf_op jit(solution)/shard_map/ppermute | solution.py:159
  336.7 9.4 %collective-permute-done.23 = bf16[96,2048]{1,0:T(8,128)(2,1)S(1)} collective-permute-done((bf16[96,2048]{1,0:T(8,128)(2,1)S(1)}, bf16[96,2048]{1,0:T(8,128)(2,1)S(1)}, u32[]{:S(2)}, u32[]{:S(2)}) %collective-permute-start.23) | collective-permute-done | bytes 393248 | tf_op jit(solution)/shard_map/ppermute | solution.py:159
  352.1 29.6 %collective-permute-done.64 = bf16[96,2048]{1,0:T(8,128)(2,1)S(1)} collective-permute-done((bf16[96,2048]{1,0:T(8,128)(2,1)S(1)}, bf16[96,2048]{1,0:T(8,128)(2,1)S(1)}, u32[]{:S(2)}, u32[]{:S(2)}) %collective-permute-start.64) | collective-permute-done | bytes 393248 | tf_op jit(solution)/shard_map/ppermute | solution.py:162
  382.0 25.0 %collective-permute-done.56 = bf16[96,2048]{1,0:T(8,128)(2,1)S(1)} collective-permute-done((bf16[96,2048]{1,0:T(8,128)(2,1)S(1)}, bf16[96,2048]{1,0:T(8,128)(2,1)S(1)}, u32[]{:S(2)}, u32[]{:S(2)}) %collective-permute-start.56) | collective-permute-done | bytes 393248 | tf_op jit(solution)/shard_map/ppermute | solution.py:162
  407.3 12.3 %collective-permute-done.48 = bf16[96,2048]{1,0:T(8,128)(2,1)S(1)} collective-permute-done((bf16[96,2048]{1,0:T(8,128)(2,1)S(1)}, bf16[96,2048]{1,0:T(8,128)(2,1)S(1)}, u32[]{:S(2)}, u32[]{:S(2)}) %collective-permute-start.48) | collective-permute-done | bytes 393248 | tf_op jit(solution)/shard_map/ppermute | solution.py:162
  419.9 8.1 %collective-permute-done.40 = bf16[96,2048]{1,0:T(8,128)(2,1)S(1)} collective-permute-done((bf16[96,2048]{1,0:T(8,128)(2,1)S(1)}, bf16[96,2048]{1,0:T(8,128)(2,1)S(1)}, u32[]{:S(2)}, u32[]{:S(2)}) %collective-permute-start.40) | collective-permute-done | bytes 393248 | tf_op jit(solution)/shard_map/ppermute | solution.py:162
  428.4 8.2 %collective-permute-done.32 = bf16[96,2048]{1,0:T(8,128)(2,1)S(1)} collective-permute-done((bf16[96,2048]{1,0:T(8,128)(2,1)S(1)}, bf16[96,2048]{1,0:T(8,128)(2,1)S(1)}, u32[]{:S(2)}, u32[]{:S(2)}) %collective-permute-start.32) | collective-permute-done | bytes 393248 | tf_op jit(solution)/shard_map/ppermute | solution.py:162
  436.9 14.3 %collective-permute-done.65 = bf16[96,2048]{1,0:T(8,128)(2,1)S(1)} collective-permute-done((bf16[96,2048]{1,0:T(8,128)(2,1)S(1)}, bf16[96,2048]{1,0:T(8,128)(2,1)S(1)}, u32[]{:S(2)}, u32[]{:S(2)}) %collective-permute-start.65) | collective-permute-done | bytes 393248 | tf_op jit(solution)/shard_map/ppermute | solution.py:159
  472.0 8.3 %collective-permute-done.41 = bf16[96,2048]{1,0:T(8,128)(2,1)S(1)} collective-permute-done((bf16[96,2048]{1,0:T(8,128)(2,1)S(1)}, bf16[96,2048]{1,0:T(8,128)(2,1)S(1)}, u32[]{:S(2)}, u32[]{:S(2)}) %collective-permute-start.41) | collective-permute-done | bytes 393248 | tf_op jit(solution)/shard_map/ppermute | solution.py:159
  480.3 8.4 %collective-permute-done.33 = bf16[96,2048]{1,0:T(8,128)(2,1)S(1)} collective-permute-done((bf16[96,2048]{1,0:T(8,128)(2,1)S(1)}, bf16[96,2048]{1,0:T(8,128)(2,1)S(1)}, u32[]{:S(2)}, u32[]{:S(2)}) %collective-permute-start.33) | collective-permute-done | bytes 393248 | tf_op jit(solution)/shard_map/ppermute | solution.py:159
  500.5 8.8 %collective-permute-done.58.refs_1_ = bf16[192,2048]{1,0:T(8,128)(2,1)} collective-permute-done((bf16[192,2048]{1,0:T(8,128)(2,1)S(1)}, bf16[192,2048]{1,0:T(8,128)(2,1)}, u32[]{:S(2)}, u32[]{:S(2)}) %collective-permute-start.58) | collective-permute-done | bytes 786464 | tf_op jit(solution)/shard_map/ppermute | solution.py:156
  511.7 14.4 %collective-permute-done.50.refs_1_ = bf16[192,2048]{1,0:T(8,128)(2,1)} collective-permute-done((bf16[192,2048]{1,0:T(8,128)(2,1)S(1)}, bf16[192,2048]{1,0:T(8,128)(2,1)}, u32[]{:S(2)}, u32[]{:S(2)}) %collective-permute-start.50) | collective-permute-done | bytes 786464 | tf_op jit(solution)/shard_map/ppermute | solution.py:156
  528.4 14.5 %collective-permute-done.42.refs_1_ = bf16[192,2048]{1,0:T(8,128)(2,1)S(1)} collective-permute-done((bf16[192,2048]{1,0:T(8,128)(2,1)S(1)}, bf16[192,2048]{1,0:T(8,128)(2,1)S(1)}, u32[]{:S(2)}, u32[]{:S(2)}) %collective-permute-start.42) | collective-permute-done | bytes 786464 | tf_op jit(solution)/shard_map/ppermute | solution.py:156
  543.4 16.2 %collective-permute-done.34.refs_1_ = bf16[192,2048]{1,0:T(8,128)(2,1)S(1)} collective-permute-done((bf16[192,2048]{1,0:T(8,128)(2,1)S(1)}, bf16[192,2048]{1,0:T(8,128)(2,1)S(1)}, u32[]{:S(2)}, u32[]{:S(2)}) %collective-permute-start.34) | collective-permute-done | bytes 786464 | tf_op jit(solution)/shard_map/ppermute | solution.py:156
  (292 shorter events, 203.8 us)
Async XLA Ops:
  8.9 45.0 %collective-permute-start = (bf16[512,1792]{1,0:T(8,128)(2,1)}, bf16[512,1792]{1,0:T(8,128)(2,1)S(1)}, u32[]{:S(2)}, u32[]{:S(2)}) collective-permute-start(bf16[512,1792]{1,0:T(8,128)(2,1)} %param.6), channel_id=1, source_target_pairs={{0,4},{4,0},{1,5},{5,1},{2,6},{6,2},{3,7},{7,3},{8,12},{12,8},{9,1... | collective-permute-start | bytes 5505032 | tf_op jit(solution)/shard_map/ppermute | solution.py:192
  50.5 72.6 %collective-permute-start.17 = (bf16[128,4096]{1,0:T(8,128)(2,1)S(1)}, bf16[128,4096]{1,0:T(8,128)(2,1)S(1)}, u32[]{:S(2)}, u32[]{:S(2)}) collective-permute-start(bf16[128,4096]{1,0:T(8,128)(2,1)S(1)} %pad_maximum_fusion.2), channel_id=1, source_target_pairs={{0,2},{2,0},{1,3},{3,1},{4,6},{6,4},{5,7},{7,5},{8,10},{10,8},{9,1... | collective-permute-start | bytes 3145736 | tf_op jit(solution)/shard_map/ppermute | solution.py:156
  51.5 132.2 %collective-permute-start.18 = (bf16[256,4096]{1,0:T(8,128)(2,1)S(1)}, bf16[256,4096]{1,0:T(8,128)(2,1)}, u32[]{:S(2)}, u32[]{:S(2)}) collective-permute-start(bf16[256,4096]{1,0:T(8,128)(2,1)S(1)} %pad_maximum_fusion), channel_id=1, source_target_pairs={{0,1},{1,0},{2,3},{3,2},{4,5},{5,4},{6,7},{7,6},{8,9},{9,8},{10,11... | collective-permute-start | bytes 6291464 | tf_op jit(solution)/shard_map/ppermute | solution.py:153
  112.4 41.6 %collective-permute-start.61 = (bf16[384,2048]{1,0:T(8,128)(2,1)S(1)}, bf16[384,2048]{1,0:T(8,128)(2,1)S(1)}, u32[]{:S(2)}, u32[]{:S(2)}) collective-permute-start(bf16[384,2048]{1,0:T(8,128)(2,1)S(1)} %get-tuple-element.48), channel_id=1, source_target_pairs={{0,1},{1,0},{2,3},{3,2},{4,5},{5,4},{6,7},{7,6},{8,9},{9,8},{10,11... | collective-permute-start | bytes 4718600 | tf_op jit(solution)/shard_map/ppermute | solution.py:153
  121.7 33.1 %collective-permute-start.53 = (bf16[384,2048]{1,0:T(8,128)(2,1)S(1)}, bf16[384,2048]{1,0:T(8,128)(2,1)S(1)}, u32[]{:S(2)}, u32[]{:S(2)}) collective-permute-start(bf16[384,2048]{1,0:T(8,128)(2,1)S(1)} %get-tuple-element.45), channel_id=1, source_target_pairs={{0,1},{1,0},{2,3},{3,2},{4,5},{5,4},{6,7},{7,6},{8,9},{9,8},{10,11... | collective-permute-start | bytes 4718600 | tf_op jit(solution)/shard_map/ppermute | solution.py:153
  168.7 178.0 %collective-permute-start.19 = (bf16[256,4096]{1,0:T(8,128)(2,1)S(1)}, bf16[256,4096]{1,0:T(8,128)(2,1)S(1)}, u32[]{:S(2)}, u32[]{:S(2)}) collective-permute-start(bf16[256,4096]{1,0:T(8,128)(2,1)S(1)} %constant_dynamic-update-slice_fusion), channel_id=1, source_target_pairs={{0,1},{1,0},{2,3},{3,2},{4,5},{5,4},{6,7},{7,6},{8,9},{9,8},{10,11... | collective-permute-start | bytes 6291464 | tf_op jit(solution)/shard_map/ppermute | solution.py:153
  181.4 29.6 %collective-permute-start.54 = (bf16[192,2048]{1,0:T(8,128)(2,1)S(1)}, bf16[192,2048]{1,0:T(8,128)(2,1)S(1)}, u32[]{:S(2)}, u32[]{:S(2)}) collective-permute-start(bf16[192,2048]{1,0:T(8,128)(2,1)S(1)} %add_convert_fusion.3), channel_id=1, source_target_pairs={{0,2},{2,0},{1,3},{3,1},{4,6},{6,4},{5,7},{7,5},{8,10},{10,8},{9,1... | collective-permute-start | bytes 2359304 | tf_op jit(solution)/shard_map/ppermute | solution.py:156
  182.8 45.1 %collective-permute-start.46 = (bf16[192,2048]{1,0:T(8,128)(2,1)S(1)}, bf16[192,2048]{1,0:T(8,128)(2,1)S(1)}, u32[]{:S(2)}, u32[]{:S(2)}) collective-permute-start(bf16[192,2048]{1,0:T(8,128)(2,1)S(1)} %add_convert_fusion.4), channel_id=1, source_target_pairs={{0,2},{2,0},{1,3},{3,1},{4,6},{6,4},{5,7},{7,5},{8,10},{10,8},{9,1... | collective-permute-start | bytes 2359304 | tf_op jit(solution)/shard_map/ppermute | solution.py:156
  183.7 61.0 %collective-permute-start.38 = (bf16[192,2048]{1,0:T(8,128)(2,1)S(1)}, bf16[192,2048]{1,0:T(8,128)(2,1)S(1)}, u32[]{:S(2)}, u32[]{:S(2)}) collective-permute-start(bf16[192,2048]{1,0:T(8,128)(2,1)S(1)} %add_convert_fusion.5), channel_id=1, source_target_pairs={{0,2},{2,0},{1,3},{3,1},{4,6},{6,4},{5,7},{7,5},{8,10},{10,8},{9,1... | collective-permute-start | bytes 2359304 | tf_op jit(solution)/shard_map/ppermute | solution.py:156
  194.2 91.6 %collective-permute-start.30 = (bf16[192,2048]{1,0:T(8,128)(2,1)S(1)}, bf16[192,2048]{1,0:T(8,128)(2,1)S(1)}, u32[]{:S(2)}, u32[]{:S(2)}) collective-permute-start(bf16[192,2048]{1,0:T(8,128)(2,1)S(1)} %add_convert_fusion.6), channel_id=1, source_target_pairs={{0,2},{2,0},{1,3},{3,1},{4,6},{6,4},{5,7},{7,5},{8,10},{10,8},{9,1... | collective-permute-start | bytes 2359304 | tf_op jit(solution)/shard_map/ppermute | solution.py:156
  211.0 75.4 %collective-permute-start.22 = (bf16[192,2048]{1,0:T(8,128)(2,1)S(1)}, bf16[192,2048]{1,0:T(8,128)(2,1)S(1)}, u32[]{:S(2)}, u32[]{:S(2)}) collective-permute-start(bf16[192,2048]{1,0:T(8,128)(2,1)S(1)} %add_convert_fusion.7), channel_id=1, source_target_pairs={{0,2},{2,0},{1,3},{3,1},{4,6},{6,4},{5,7},{7,5},{8,10},{10,8},{9,1... | collective-permute-start | bytes 2359304 | tf_op jit(solution)/shard_map/ppermute | solution.py:156
  227.9 223.6 %collective-permute-start.5 = (bf16[96,1024]{1,0:T(8,128)(2,1)S(1)}, bf16[96,1024]{1,0:T(8,128)(2,1)S(1)}, u32[]{:S(2)}, u32[]{:S(2)}) collective-permute-start(bf16[96,1024]{1,0:T(8,128)(2,1)S(1)} %add_convert_fusion.25), channel_id=1, source_target_pairs={{0,8},{8,0},{16,24},{24,16},{1,9},{9,1},{17,25},{25,17},{2,10},{10... | collective-permute-start | bytes 589832 | tf_op jit(solution)/shard_map/ppermute | solution.py:159
  244.7 41.0 %collective-permute-start.74 = (bf16[192,1024]{1,0:T(8,128)(2,1)S(1)}, bf16[192,1024]{1,0:T(8,128)(2,1)S(1)}, u32[]{:S(2)}, u32[]{:S(2)}) collective-permute-start(bf16[192,1024]{1,0:T(8,128)(2,1)S(1)} %pad_maximum_fusion.10.refs_0_), channel_id=1, source_target_pairs={{0,2},{2,0},{1,3},{3,1},{4,6},{6,4},{5,7},{7,5},{8,10},{10,8},{9,1... | collective-permute-start | bytes 1179656 | tf_op jit(solution)/shard_map/ppermute | solution.py:156
  285.8 167.8 %collective-permute-start.75 = (bf16[192,1024]{1,0:T(8,128)(2,1)S(1)}, bf16[192,1024]{1,0:T(8,128)(2,1)S(1)}, u32[]{:S(2)}, u32[]{:S(2)}) collective-permute-start(bf16[192,1024]{1,0:T(8,128)(2,1)S(1)} %pad_maximum_fusion.10.refs_0_), channel_id=1, source_target_pairs={{0,1},{1,0},{2,3},{3,2},{4,5},{5,4},{6,7},{7,6},{8,9},{9,8},{10,11... | collective-permute-start | bytes 1179656 | tf_op jit(solution)/shard_map/ppermute | solution.py:153
  285.8 167.9 %collective-permute-start.76 = (bf16[192,1024]{1,0:T(8,128)(2,1)S(1)}, bf16[192,1024]{1,0:T(8,128)(2,1)S(1)}, u32[]{:S(2)}, u32[]{:S(2)}) collective-permute-start(bf16[192,1024]{1,0:T(8,128)(2,1)S(1)} %collective-permute-done.74.refs_1_), channel_id=1, source_target_pairs={{0,1},{1,0},{2,3},{3,2},{4,5},{5,4},{6,7},{7,6},{8,9},{9,8},{10,11... | collective-permute-start | bytes 1179656 | tf_op jit(solution)/shard_map/ppermute | solution.py:153
  346.1 35.6 %collective-permute-start.64 = (bf16[96,2048]{1,0:T(8,128)(2,1)S(1)}, bf16[96,2048]{1,0:T(8,128)(2,1)S(1)}, u32[]{:S(2)}, u32[]{:S(2)}) collective-permute-start(bf16[96,2048]{1,0:T(8,128)(2,1)S(1)} %fusion.19), channel_id=1, source_target_pairs={{0,16},{16,0},{8,24},{24,8},{1,17},{17,1},{9,25},{25,9},{2,18},{18... | collective-permute-start | bytes 1179656 | tf_op jit(solution)/shard_map/ppermute | solution.py:162
  346.7 60.3 %collective-permute-start.56 = (bf16[96,2048]{1,0:T(8,128)(2,1)S(1)}, bf16[96,2048]{1,0:T(8,128)(2,1)S(1)}, u32[]{:S(2)}, u32[]{:S(2)}) collective-permute-start(bf16[96,2048]{1,0:T(8,128)(2,1)S(1)} %fusion.18), channel_id=1, source_target_pairs={{0,16},{16,0},{8,24},{24,8},{1,17},{17,1},{9,25},{25,9},{2,18},{18... | collective-permute-start | bytes 1179656 | tf_op jit(solution)/shard_map/ppermute | solution.py:162
  381.7 37.9 %collective-permute-start.48 = (bf16[96,2048]{1,0:T(8,128)(2,1)S(1)}, bf16[96,2048]{1,0:T(8,128)(2,1)S(1)}, u32[]{:S(2)}, u32[]{:S(2)}) collective-permute-start(bf16[96,2048]{1,0:T(8,128)(2,1)S(1)} %fusion.17), channel_id=1, source_target_pairs={{0,16},{16,0},{8,24},{24,8},{1,17},{17,1},{9,25},{25,9},{2,18},{18... | collective-permute-start | bytes 1179656 | tf_op jit(solution)/shard_map/ppermute | solution.py:162
  428.1 27.6 %collective-permute-start.24 = (bf16[96,2048]{1,0:T(8,128)(2,1)S(1)}, bf16[96,2048]{1,0:T(8,128)(2,1)S(1)}, u32[]{:S(2)}, u32[]{:S(2)}) collective-permute-start(bf16[96,2048]{1,0:T(8,128)(2,1)S(1)} %fusion.14), channel_id=1, source_target_pairs={{0,16},{16,0},{8,24},{24,8},{1,17},{17,1},{9,25},{25,9},{2,18},{18... | collective-permute-start | bytes 1179656 | tf_op jit(solution)/shard_map/ppermute | solution.py:162
  453.7 35.0 %collective-permute-start.33 = (bf16[96,2048]{1,0:T(8,128)(2,1)S(1)}, bf16[96,2048]{1,0:T(8,128)(2,1)S(1)}, u32[]{:S(2)}, u32[]{:S(2)}) collective-permute-start(bf16[96,2048]{1,0:T(8,128)(2,1)S(1)} %add_convert_fusion.18), channel_id=1, source_target_pairs={{0,8},{8,0},{16,24},{24,16},{1,9},{9,1},{17,25},{25,17},{2,10},{10... | collective-permute-start | bytes 1179656 | tf_op jit(solution)/shard_map/ppermute | solution.py:159
  455.6 40.5 %collective-permute-start.66 = (bf16[192,2048]{1,0:T(8,128)(2,1)S(1)}, bf16[192,2048]{1,0:T(8,128)(2,1)S(1)}, u32[]{:S(2)}, u32[]{:S(2)}) collective-permute-start(bf16[192,2048]{1,0:T(8,128)(2,1)S(1)} %pad_maximum_fusion.8.refs_0_), channel_id=1, source_target_pairs={{0,2},{2,0},{1,3},{3,1},{4,6},{6,4},{5,7},{7,5},{8,10},{10,8},{9,1... | collective-permute-start | bytes 2359304 | tf_op jit(solution)/shard_map/ppermute | solution.py:156
  463.4 96.3 %collective-permute-start.20 = (f32[1024,512]{1,0:T(8,128)}, f32[1024,512]{1,0:T(8,128)}, u32[]{:S(2)}, u32[]{:S(2)}) collective-permute-start(f32[1024,512]{1,0:T(8,128)} %pad_maximum_fusion.1), channel_id=1, source_target_pairs={{0,4},{4,0},{1,5},{5,1},{2,6},{6,2},{3,7},{7,3},{8,12},{12,8},{9,1... | collective-permute-start | bytes 6291464 | tf_op jit(solution)/shard_map/ppermute | solution.py:231
  496.2 29.9 %collective-permute-start.50 = (bf16[192,2048]{1,0:T(8,128)(2,1)S(1)}, bf16[192,2048]{1,0:T(8,128)(2,1)}, u32[]{:S(2)}, u32[]{:S(2)}) collective-permute-start(bf16[192,2048]{1,0:T(8,128)(2,1)S(1)} %pad_maximum_fusion.6.refs_0_), channel_id=1, source_target_pairs={{0,2},{2,0},{1,3},{3,1},{4,6},{6,4},{5,7},{7,5},{8,10},{10,8},{9,1... | collective-permute-start | bytes 2359304 | tf_op jit(solution)/shard_map/ppermute | solution.py:156
  500.2 27.2 %collective-permute-start.51 = (bf16[192,2048]{1,0:T(8,128)(2,1)S(1)}, bf16[192,2048]{1,0:T(8,128)(2,1)S(1)}, u32[]{:S(2)}, u32[]{:S(2)}) collective-permute-start(bf16[192,2048]{1,0:T(8,128)(2,1)S(1)} %pad_maximum_fusion.6.refs_0_), channel_id=1, source_target_pairs={{0,1},{1,0},{2,3},{3,2},{4,5},{5,4},{6,7},{7,6},{8,9},{9,8},{10,11... | collective-permute-start | bytes 2359304 | tf_op jit(solution)/shard_map/ppermute | solution.py:153
  509.2 33.6 %collective-permute-start.42 = (bf16[192,2048]{1,0:T(8,128)(2,1)S(1)}, bf16[192,2048]{1,0:T(8,128)(2,1)S(1)}, u32[]{:S(2)}, u32[]{:S(2)}) collective-permute-start(bf16[192,2048]{1,0:T(8,128)(2,1)S(1)} %pad_maximum_fusion.5.refs_0_), channel_id=1, source_target_pairs={{0,2},{2,0},{1,3},{3,1},{4,6},{6,4},{5,7},{7,5},{8,10},{10,8},{9,1... | collective-permute-start | bytes 2359304 | tf_op jit(solution)/shard_map/ppermute | solution.py:156
  511.6 31.3 %collective-permute-start.43 = (bf16[192,2048]{1,0:T(8,128)(2,1)S(1)}, bf16[192,2048]{1,0:T(8,128)(2,1)S(1)}, u32[]{:S(2)}, u32[]{:S(2)}) collective-permute-start(bf16[192,2048]{1,0:T(8,128)(2,1)S(1)} %pad_maximum_fusion.5.refs_0_), channel_id=1, source_target_pairs={{0,1},{1,0},{2,3},{3,2},{4,5},{5,4},{6,7},{7,6},{8,9},{9,8},{10,11... | collective-permute-start | bytes 2359304 | tf_op jit(solution)/shard_map/ppermute | solution.py:153
  526.1 33.6 %collective-permute-start.34 = (bf16[192,2048]{1,0:T(8,128)(2,1)S(1)}, bf16[192,2048]{1,0:T(8,128)(2,1)S(1)}, u32[]{:S(2)}, u32[]{:S(2)}) collective-permute-start(bf16[192,2048]{1,0:T(8,128)(2,1)S(1)} %pad_maximum_fusion.4.refs_0_), channel_id=1, source_target_pairs={{0,2},{2,0},{1,3},{3,1},{4,6},{6,4},{5,7},{7,5},{8,10},{10,8},{9,1... | collective-permute-start | bytes 2359304 | tf_op jit(solution)/shard_map/ppermute | solution.py:156
  527.4 46.5 %collective-permute-start.26 = (bf16[192,2048]{1,0:T(8,128)(2,1)S(1)}, bf16[192,2048]{1,0:T(8,128)(2,1)S(1)}, u32[]{:S(2)}, u32[]{:S(2)}) collective-permute-start(bf16[192,2048]{1,0:T(8,128)(2,1)S(1)} %pad_maximum_fusion.3.refs_0_), channel_id=1, source_target_pairs={{0,2},{2,0},{1,3},{3,1},{4,6},{6,4},{5,7},{7,5},{8,10},{10,8},{9,1... | collective-permute-start | bytes 2359304 | tf_op jit(solution)/shard_map/ppermute | solution.py:156
  542.8 31.1 %collective-permute-start.68 = (bf16[192,2048]{1,0:T(8,128)(2,1)S(1)}, bf16[192,2048]{1,0:T(8,128)(2,1)S(1)}, u32[]{:S(2)}, u32[]{:S(2)}) collective-permute-start(bf16[192,2048]{1,0:T(8,128)(2,1)S(1)} %collective-permute-done.66.refs_1_), channel_id=1, source_target_pairs={{0,1},{1,0},{2,3},{3,2},{4,5},{5,4},{6,7},{7,6},{8,9},{9,8},{10,11... | collective-permute-start | bytes 2359304 | tf_op jit(solution)/shard_map/ppermute | solution.py:153
  542.9 37.8 %collective-permute-start.60 = (bf16[192,2048]{1,0:T(8,128)(2,1)}, bf16[192,2048]{1,0:T(8,128)(2,1)S(1)}, u32[]{:S(2)}, u32[]{:S(2)}) collective-permute-start(bf16[192,2048]{1,0:T(8,128)(2,1)} %collective-permute-done.58.refs_1_), channel_id=1, source_target_pairs={{0,1},{1,0},{2,3},{3,2},{4,5},{5,4},{6,7},{7,6},{8,9},{9,8},{10,11... | collective-permute-start | bytes 2359304 | tf_op jit(solution)/shard_map/ppermute | solution.py:153
  559.7 28.0 %collective-permute-start.44 = (bf16[192,2048]{1,0:T(8,128)(2,1)S(1)}, bf16[192,2048]{1,0:T(8,128)(2,1)S(1)}, u32[]{:S(2)}, u32[]{:S(2)}) collective-permute-start(bf16[192,2048]{1,0:T(8,128)(2,1)S(1)} %collective-permute-done.42.refs_1_), channel_id=1, source_target_pairs={{0,1},{1,0},{2,3},{3,2},{4,5},{5,4},{6,7},{7,6},{8,9},{9,8},{10,11... | collective-permute-start | bytes 2359304 | tf_op jit(solution)/shard_map/ppermute | solution.py:153
  573.9 26.9 %collective-permute-start.36 = (bf16[192,2048]{1,0:T(8,128)(2,1)S(1)}, bf16[192,2048]{1,0:T(8,128)(2,1)S(1)}, u32[]{:S(2)}, u32[]{:S(2)}) collective-permute-start(bf16[192,2048]{1,0:T(8,128)(2,1)S(1)} %collective-permute-done.34.refs_1_), channel_id=1, source_target_pairs={{0,1},{1,0},{2,3},{3,2},{4,5},{5,4},{6,7},{7,6},{8,9},{9,8},{10,11... | collective-permute-start | bytes 2359304 | tf_op jit(solution)/shard_map/ppermute | solution.py:153
  (81 other events, 2345.1 us)

commit v3 on v2

--- a/solution.py
+++ b/solution.py
@@ -10,16 +10,16 @@
 WINDOWS = 3
 F32 = jnp.float32
 BF16 = jnp.bfloat16
-PLAN = (1, 2, 2, 2, 2, 2, 2, 1)
+PLAN = (2, 2, 2, 2, 2, 2, 2)
+KINDS = (1, 1, 1, 1, 2, 1, 2)
 PARTS = 14
 ORDER = (
-    (0, 0), (1, 0), (0, 1), (2, 0), (1, 1), (0, 2), (3, 0), (0, 3), (2, 1), (3, 1),
-    (1, 2), (4, 0), (0, 4), (1, 3), (2, 2), (4, 1), (0, 5), (5, 0), (3, 2), (1, 4),
-    (2, 3), (5, 1), (6, 0), (4, 2), (1, 5), (0, 6), (3, 3), (6, 1), (0, 7), (2, 4),
-    (4, 3), (7, 0), (3, 4), (7, 1), (5, 2), (2, 5), (1, 6), (1, 7), (4, 4), (3, 5),
-    (6, 2), (5, 3), (7, 2), (4, 5), (6, 3), (2, 6), (2, 7), (5, 4), (7, 3), (3, 6),
-    (6, 4), (3, 7), (5, 5), (7, 4), (4, 6), (4, 7), (6, 5), (7, 5), (5, 6), (5, 7),
-    (6, 6), (6, 7), (7, 6), (7, 7),
+    (0, 0), (1, 0), (0, 1), (2, 0), (1, 1), (2, 1), (3, 0), (3, 1), (0, 2), (4, 0),
+    (0, 3), (1, 2), (5, 0), (2, 2), (4, 1), (5, 1), (1, 3), (0, 4), (6, 0), (3, 2),
+    (2, 3), (6, 1), (1, 4), (0, 5), (4, 2), (3, 3), (2, 4), (5, 2), (1, 5), (4, 3),
+    (6, 2), (3, 4), (2, 5), (0, 6), (0, 7), (5, 3), (4, 4), (1, 6), (1, 7), (6, 3),
+    (3, 5), (2, 6), (2, 7), (5, 4), (4, 5), (6, 4), (5, 5), (3, 6), (3, 7), (6, 5),
+    (4, 6), (4, 7), (5, 6), (5, 7), (6, 6), (6, 7),
 )
 
 
@@ -83,7 +83,7 @@
     )(where, lhs, basis)
 
 
-def finish(where, pieces, acts, out, shape, offset, width, scale):
+def finish(kind, where, pieces, acts, out, shape, offset, width, scale):
     size = block_of(width, offset)
     start = offset // size
     window = acts[0].shape[0]
@@ -102,10 +102,14 @@
         out_ref, proj_ref = refs[-2:]
         core, side, spot = where_ref[0], where_ref[1], where_ref[2]
         for number, piece in enumerate(refs[:4]):
-            place = 2 * jnp.bitwise_xor(core, number // 2) + jnp.bitwise_xor(side, number % 2)
+            its_core = jnp.bitwise_xor(core, number // 2)
             for n in range(2 * WINDOWS):
-                half = jnp.bitwise_xor(spot, 1 - n // WINDOWS)
-                at = (n % WINDOWS) * window + (2 * place + half) * part
+                group = n // WINDOWS
+                if kind == 1:
+                    its_side, half = side ^ (number % 2), spot ^ (1 - group)
+                else:
+                    its_side, half = side ^ group, spot ^ (number % 2)
+                at = (n % WINDOWS) * window + (4 * its_core + 2 * its_side + half) * part
                 proj_ref[pl.ds(pl.multiple_of(at, part), part), :] = piece[
                     n * part : (n + 1) * part, :
                 ]
@@ -209,26 +213,25 @@
         for ahead in (1, 2, 3):
             blocks.append(jnp.where(spot + ahead < 4, down[ahead], up[4 - ahead]))
         first = across_side(blocks[0])
-        first = jnp.concatenate([first, across_side(blocks[2])], axis=0)
-        second = across_side(jnp.concatenate([blocks[1], blocks[3]], axis=0))
+        second = across_side(blocks[2])
+        third_part = across_side(jnp.concatenate([blocks[1], blocks[3]], axis=0))
         mine = jnp.concatenate([blocks[0], blocks[2], blocks[1], blocks[3]], axis=0)
-        theirs = jnp.concatenate([first, second], axis=0)
-        pieces = (mine, theirs, across_core(mine), across_core(theirs))
-        place = (spot + jnp.array([0, 2, 1, 3], jnp.int32)) % 4
-        token_ids = jnp.concatenate(
-            [
-                (
-                    (place[:, None] * 4 + 2 * jnp.bitwise_xor(side, n % 2))
-                    + jnp.bitwise_xor(core, n // 2)
-                )
-                * held_rows
-                + jnp.arange(held_rows, dtype=jnp.int32)[None, :]
-                for n in range(4)
-            ]
+        theirs = jnp.concatenate([first, second, third_part], axis=0)
+        mine_far = across_core(mine)
+        theirs_far = across_core(theirs)
+        pieces = (mine, theirs, mine_far, theirs_far)
+        seats = []
+        for n in range(4):
+            for ahead in (0, 2, 1, 3):
+                seats.append((spot + ahead) % 4 * 4 + 2 * (side ^ (n % 2)) + (core ^ (n // 2)))
+        token_ids = (
+            jnp.stack(seats)[:, None] * held_rows
+            + jnp.arange(held_rows, dtype=jnp.int32)[None, :]
         ).reshape(tokens)
         act_part = jnp.concatenate([dot(piece, in_basis) for piece in pieces], axis=0)
         if row_size == 2:
-            act_sum = act_part + lax.ppermute(act_part, "row", [(0, 1), (1, 0)])
+            other = lax.ppermute(act_part, "row", [(0, 1), (1, 0)])
+            act_sum = act_part + other
         else:
             act_sum = lax.psum(act_part, "row")
         chosen = (token_of[:, None] == token_ids[None, :]).astype(BF16)
@@ -257,6 +260,7 @@
 
     for chunk, stage in ORDER:
         h = held[chunk]
+        kind = KINDS[chunk]
         width = PLAN[chunk] * unit
         offset = sum(PLAN[:chunk]) * unit
         if stage == 0:
@@ -270,11 +274,15 @@
             send = total(*h["own"])
         elif stage == 4:
             send = h["mine"] = total(*h["own"], h["far_pair"])
+        elif stage == 5 and kind == 1:
+            send = h["full"] = jnp.concatenate([h["theirs"], h["mine"]], axis=0)
         elif stage == 5:
-            send = h["full"] = jnp.concatenate([h["theirs"], h["mine"]], axis=0)
+            send = h["full"] = jnp.concatenate([h["mine"], h["theirs"]], axis=0)
         elif stage == 7:
             pieces = (h["full"], h["beside"], h["far"], h["last"])
-            out = finish(where, pieces, sets, out, shape, offset, width, 1.0 / tokens)
+            out = finish(
+                kind, where, pieces, sets, out, shape, offset, width, 1.0 / tokens
+            )
         if stage == 0:
             h["core"] = across_core(send)
         elif stage == 1:
@@ -284,9 +292,11 @@
         elif stage == 3:
             h["far_pair"] = across_half(send)
         elif stage == 4:
-            h["theirs"] = across_pair(send)
+            move = across_pair if kind == 1 else across_side
+            h["theirs"] = move(send)
         elif stage == 5:
-            h["beside"] = across_side(send)
+            move = across_side if kind == 1 else across_pair
+            h["beside"] = move(send)
             h["far"] = across_core(send)
         elif stage == 6:
             h["last"] = across_core(h["beside"])

time: 618 us -> 553 us (0.89)
  waiting for transfers between devices: 408 us -> 326 us
  starting transfers between devices: 60.8 us -> 75.4 us
    ppermute x8 -> x7, waiting for transfers between devices: 98.9 us -> 54 us  [across_half(): return lax.ppermute(x, 'seq', [(0, 2), (2, 0), (1, 3), (3, 1)])]
    ppermute x16 -> x14, waiting for transfers between devices: 116 us -> 76.5 us  [across_pair(): return lax.ppermute(x, 'seq', [(0, 1), (1, 0), (2, 3), (3, 2)])]
    ppermute x16 -> x14, starting transfers between devices: 14.1 us -> 30.1 us  [across_pair(): return lax.ppermute(x, 'seq', [(0, 1), (1, 0), (2, 3), (3, 2)])]
    ppermute x26 -> x23, waiting for transfers between devices: 0.07 us -> 6.99 us  [across_core(): return lax.ppermute(x, 'col', [(0, 1), (1, 0), (2, 3), (3, 2)])]
    ppermute x19 -> x17, starting transfers between devices: 21.3 us -> 14.4 us  [across_side(): return lax.ppermute(x, 'col', [(0, 2), (2, 0), (1, 3), (3, 1)])]
    ppermute x8 -> x7, starting transfers between devices: 6.74 us -> 12.7 us  [across_half(): return lax.ppermute(x, 'seq', [(0, 2), (2, 0), (1, 3), (3, 1)])]
    ppermute x19 -> x17, waiting for transfers between devices: 170 us -> 166 us  [across_side(): return lax.ppermute(x, 'col', [(0, 2), (2, 0), (1, 3), (3, 1)])]
    pallas_call x8 -> x7, Pallas kernels: 65.2 us -> 63.2 us  [project(): pl.pallas_call(kernel, grid_spec=pltpu.PrefetchScalarGridSpec(num_scalar_...]
  transfers between devices with their start and end apart: 77 -> 69, of which waited for: 35 -> 32; matrix products, arithmetic and copies ran while one was open for 5% -> 6% of each run, Pallas kernels for 17% -> 18%
where the time goes in v3:
time: 553 us; the launch traced here: 548 us
  waiting for transfers between devices  326 us (59%)
  Pallas kernels  105 us (19%)
  starting transfers between devices  75.4 us (14%)
  other arithmetic  16.2 us (3%)
  matrix products  14.7 us (3%)
  local copies, waits for them, and re-layouts  6.96 us (1%)
    ppermute x17, waiting for transfers between devices, across_side(): return lax.ppermute(x, 'col', [(0, 2), (2, 0), (1, 3), (3, 1)])  166 us
    ppermute x14, waiting for transfers between devices, across_pair(): return lax.ppermute(x, 'seq', [(0, 1), (1, 0), (2, 3), (3, 2)])  76.5 us
    pallas_call x7, Pallas kernels, project(): pl.pallas_call(kernel, grid_spec=pltpu.PrefetchScalarGridSpec(num_scalar_...  63.2 us
    ppermute x7, waiting for transfers between devices, across_half(): return lax.ppermute(x, 'seq', [(0, 2), (2, 0), (1, 3), (3, 1)])  54 us
    pallas_call x7, Pallas kernels, finish(): pl.pallas_call(kernel, grid_spec=pltpu.PrefetchScalarGridSpec(num_scalar_...  41.8 us
    ppermute x14, starting transfers between devices, across_pair(): return lax.ppermute(x, 'seq', [(0, 1), (1, 0), (2, 3), (3, 2)])  30.1 us
    ppermute x3, waiting for transfers between devices, act_sets(): lax.ppermute(down[-1], 'seq', [(i + 1, i) for i in range(3 - step)])  23.1 us
    dot_general x7, matrix products, dot(): return jnp.dot(lhs, rhs, preferred_element_type=F32)  14.7 us
  transfers between devices with their start and end apart: 69, of which 32 were waited for; matrix products, arithmetic and copies ran while one was open for 6% of the time, Pallas kernels for 18%

profile of v3, /device:TPU:0, one launch (start us, length us, event | category | flops | bytes accessed | tf_op | source)
XLA Modules:
  0.0 547.9 jit_solution(13439902489904665262)
XLA Ops:
  21.3 12.3 %collective-permute-done.10 = bf16[64,4096]{1,0:T(8,128)(2,1)S(1)} collective-permute-done((bf16[64,4096]{1,0:T(8,128)(2,1)S(1)}, bf16[64,4096]{1,0:T(8,128)(2,1)S(1)}, u32[]{:S(2)}, u32[]{:S(2)}) %collective-permute-start.10) | collective-permute-done | bytes 524320 | tf_op jit(solution)/shard_map/ppermute | solution.py:211
  36.4 10.8 %collective-permute-done.14 = bf16[64,4096]{1,0:T(8,128)(2,1)S(1)} collective-permute-done((bf16[64,4096]{1,0:T(8,128)(2,1)S(1)}, bf16[64,4096]{1,0:T(8,128)(2,1)S(1)}, u32[]{:S(2)}, u32[]{:S(2)}) %collective-permute-start.14) | collective-permute-done | bytes 524320 | tf_op jit(solution)/shard_map/ppermute | solution.py:211
  52.6 9.0 %shard_map.61 = (bf16[384,2048]{1,0:T(8,128)(2,1)S(1)}, bf16[192,2048]{1,0:T(8,128)(2,1)S(1)}, bf16[192,2048]{1,0:T(8,128)(2,1)S(1)}) custom-call(s32[4]{0:T(128)S(1)} %pad_add_fusion.where_ref, bf16[768,1792]{1,0:T(8,128)(2,1)S(1)} %add_convert_fusion.lhs_ref, bf16[1792,14336]{1,0:T(8,128)(2,1)} %rhs_ref.13), custom_call_target="tpu_custom_call" | custom-call | flops 5637144576 | bytes 10485760 | tf_op jit(solution)/shard_map/pallas_call | solution.py:60
  61.6 9.0 %shard_map.60 = (bf16[384,2048]{1,0:T(8,128)(2,1)S(1)}, bf16[192,2048]{1,0:T(8,128)(2,1)S(1)}, bf16[192,2048]{1,0:T(8,128)(2,1)S(1)}) custom-call(s32[4]{0:T(128)S(1)} %pad_add_fusion.where_ref, bf16[768,1792]{1,0:T(8,128)(2,1)S(1)} %add_convert_fusion.lhs_ref, bf16[1792,14336]{1,0:T(8,128)(2,1)} %rhs_ref.13), custom_call_target="tpu_custom_call" | custom-call | flops 5637144576 | bytes 10485760 | tf_op jit(solution)/shard_map/pallas_call | solution.py:60
  70.6 9.0 %shard_map.59 = (bf16[384,2048]{1,0:T(8,128)(2,1)S(1)}, bf16[192,2048]{1,0:T(8,128)(2,1)S(1)}, bf16[192,2048]{1,0:T(8,128)(2,1)S(1)}) custom-call(s32[4]{0:T(128)S(1)} %pad_add_fusion.where_ref, bf16[768,1792]{1,0:T(8,128)(2,1)S(1)} %add_convert_fusion.lhs_ref, bf16[1792,14336]{1,0:T(8,128)(2,1)} %rhs_ref.13), custom_call_target="tpu_custom_call" | custom-call | flops 5637144576 | bytes 10485760 | tf_op jit(solution)/shard_map/pallas_call | solution.py:60
  79.6 9.0 %shard_map.58 = (bf16[384,2048]{1,0:T(8,128)(2,1)S(1)}, bf16[192,2048]{1,0:T(8,128)(2,1)S(1)}, bf16[192,2048]{1,0:T(8,128)(2,1)S(1)}) custom-call(s32[4]{0:T(128)S(1)} %pad_add_fusion.where_ref, bf16[768,1792]{1,0:T(8,128)(2,1)S(1)} %add_convert_fusion.lhs_ref, bf16[1792,14336]{1,0:T(8,128)(2,1)} %rhs_ref.13), custom_call_target="tpu_custom_call" | custom-call | flops 5637144576 | bytes 10485760 | tf_op jit(solution)/shard_map/pallas_call | solution.py:60
  88.6 9.0 %shard_map.57 = (bf16[384,2048]{1,0:T(8,128)(2,1)S(1)}, bf16[192,2048]{1,0:T(8,128)(2,1)S(1)}, bf16[192,2048]{1,0:T(8,128)(2,1)S(1)}) custom-call(s32[4]{0:T(128)S(1)} %pad_add_fusion.where_ref, bf16[768,1792]{1,0:T(8,128)(2,1)S(1)} %add_convert_fusion.lhs_ref, bf16[1792,14336]{1,0:T(8,128)(2,1)} %rhs_ref.13), custom_call_target="tpu_custom_call" | custom-call | flops 5637144576 | bytes 10485760 | tf_op jit(solution)/shard_map/pallas_call | solution.py:60
  97.7 9.0 %shard_map.56 = (bf16[384,2048]{1,0:T(8,128)(2,1)S(1)}, bf16[192,2048]{1,0:T(8,128)(2,1)S(1)}, bf16[192,2048]{1,0:T(8,128)(2,1)S(1)}) custom-call(s32[4]{0:T(128)S(1)} %pad_add_fusion.where_ref, bf16[768,1792]{1,0:T(8,128)(2,1)S(1)} %add_convert_fusion.lhs_ref, bf16[1792,14336]{1,0:T(8,128)(2,1)} %rhs_ref.13), custom_call_target="tpu_custom_call" | custom-call | flops 5637144576 | bytes 10485760 | tf_op jit(solution)/shard_map/pallas_call | solution.py:60
  107.3 9.2 %shard_map.55 = (bf16[384,2048]{1,0:T(8,128)(2,1)S(1)}, bf16[192,2048]{1,0:T(8,128)(2,1)S(1)}, bf16[192,2048]{1,0:T(8,128)(2,1)S(1)}) custom-call(s32[4]{0:T(128)S(1)} %pad_add_fusion.where_ref, bf16[768,1792]{1,0:T(8,128)(2,1)S(1)} %add_convert_fusion.lhs_ref, bf16[1792,14336]{1,0:T(8,128)(2,1)} %rhs_ref.13), custom_call_target="tpu_custom_call" | custom-call | flops 5637144576 | bytes 10485760 | tf_op jit(solution)/shard_map/pallas_call | solution.py:60
  134.2 10.6 %collective-permute-done.62 = bf16[192,2048]{1,0:T(8,128)(2,1)S(1)} collective-permute-done((bf16[192,2048]{1,0:T(8,128)(2,1)S(1)}, bf16[192,2048]{1,0:T(8,128)(2,1)S(1)}, u32[]{:S(2)}, u32[]{:S(2)}) %collective-permute-start.62) | collective-permute-done | bytes 786464 | tf_op jit(solution)/shard_map/ppermute | solution.py:160
  145.5 16.2 %collective-permute-done.54 = bf16[192,2048]{1,0:T(8,128)(2,1)S(1)} collective-permute-done((bf16[192,2048]{1,0:T(8,128)(2,1)S(1)}, bf16[192,2048]{1,0:T(8,128)(2,1)S(1)}, u32[]{:S(2)}, u32[]{:S(2)}) %collective-permute-start.54) | collective-permute-done | bytes 786464 | tf_op jit(solution)/shard_map/ppermute | solution.py:160
  162.4 16.2 %collective-permute-done.46 = bf16[192,2048]{1,0:T(8,128)(2,1)S(1)} collective-permute-done((bf16[192,2048]{1,0:T(8,128)(2,1)S(1)}, bf16[192,2048]{1,0:T(8,128)(2,1)S(1)}, u32[]{:S(2)}, u32[]{:S(2)}) %collective-permute-start.46) | collective-permute-done | bytes 786464 | tf_op jit(solution)/shard_map/ppermute | solution.py:160
  179.2 16.2 %collective-permute-done.38 = bf16[192,2048]{1,0:T(8,128)(2,1)S(1)} collective-permute-done((bf16[192,2048]{1,0:T(8,128)(2,1)S(1)}, bf16[192,2048]{1,0:T(8,128)(2,1)S(1)}, u32[]{:S(2)}, u32[]{:S(2)}) %collective-permute-start.38) | collective-permute-done | bytes 786464 | tf_op jit(solution)/shard_map/ppermute | solution.py:160
  197.6 14.7 %collective-permute-done.30 = bf16[192,2048]{1,0:T(8,128)(2,1)S(1)} collective-permute-done((bf16[192,2048]{1,0:T(8,128)(2,1)S(1)}, bf16[192,2048]{1,0:T(8,128)(2,1)S(1)}, u32[]{:S(2)}, u32[]{:S(2)}) %collective-permute-start.30) | collective-permute-done | bytes 786464 | tf_op jit(solution)/shard_map/ppermute | solution.py:160
  214.4 14.7 %collective-permute-done.22 = bf16[192,2048]{1,0:T(8,128)(2,1)S(1)} collective-permute-done((bf16[192,2048]{1,0:T(8,128)(2,1)S(1)}, bf16[192,2048]{1,0:T(8,128)(2,1)S(1)}, u32[]{:S(2)}, u32[]{:S(2)}) %collective-permute-start.22) | collective-permute-done | bytes 786464 | tf_op jit(solution)/shard_map/ppermute | solution.py:160
  231.3 13.9 %collective-permute-done.2 = bf16[192,2048]{1,0:T(8,128)(2,1)S(1)} collective-permute-done((bf16[192,2048]{1,0:T(8,128)(2,1)S(1)}, bf16[192,2048]{1,0:T(8,128)(2,1)S(1)}, u32[]{:S(2)}, u32[]{:S(2)}) %collective-permute-start.2) | collective-permute-done | bytes 786464 | tf_op jit(solution)/shard_map/ppermute | solution.py:160
  250.3 6.8 %collective-permute-done.39 = bf16[96,2048]{1,0:T(8,128)(2,1)S(1)} collective-permute-done((bf16[96,2048]{1,0:T(8,128)(2,1)S(1)}, bf16[96,2048]{1,0:T(8,128)(2,1)S(1)}, u32[]{:S(2)}, u32[]{:S(2)}) %collective-permute-start.39) | collective-permute-done | bytes 393248 | tf_op jit(solution)/shard_map/ppermute | solution.py:163
  260.9 13.1 %collective-permute-done.31 = bf16[96,2048]{1,0:T(8,128)(2,1)S(1)} collective-permute-done((bf16[96,2048]{1,0:T(8,128)(2,1)S(1)}, bf16[96,2048]{1,0:T(8,128)(2,1)S(1)}, u32[]{:S(2)}, u32[]{:S(2)}) %collective-permute-start.31) | collective-permute-done | bytes 393248 | tf_op jit(solution)/shard_map/ppermute | solution.py:163
  277.3 13.5 %collective-permute-done.23 = bf16[96,2048]{1,0:T(8,128)(2,1)S(1)} collective-permute-done((bf16[96,2048]{1,0:T(8,128)(2,1)S(1)}, bf16[96,2048]{1,0:T(8,128)(2,1)S(1)}, u32[]{:S(2)}, u32[]{:S(2)}) %collective-permute-start.23) | collective-permute-done | bytes 393248 | tf_op jit(solution)/shard_map/ppermute | solution.py:163
  291.1 6.8 %collective-permute-done.3 = bf16[96,2048]{1,0:T(8,128)(2,1)S(1)} collective-permute-done((bf16[96,2048]{1,0:T(8,128)(2,1)S(1)}, bf16[96,2048]{1,0:T(8,128)(2,1)S(1)}, u32[]{:S(2)}, u32[]{:S(2)}) %collective-permute-start.3) | collective-permute-done | bytes 393248 | tf_op jit(solution)/shard_map/ppermute | solution.py:163
  306.1 41.2 %collective-permute-done.48 = bf16[96,2048]{1,0:T(8,128)(2,1)S(1)} collective-permute-done((bf16[96,2048]{1,0:T(8,128)(2,1)S(1)}, bf16[96,2048]{1,0:T(8,128)(2,1)S(1)}, u32[]{:S(2)}, u32[]{:S(2)}) %collective-permute-start.48) | collective-permute-done | bytes 393248 | tf_op jit(solution)/shard_map/ppermute | solution.py:166
  347.3 8.1 %collective-permute-start.65 = (bf16[96,2048]{1,0:T(8,128)(2,1)S(1)}, bf16[96,2048]{1,0:T(8,128)(2,1)S(1)}, u32[]{:S(2)}, u32[]{:S(2)}) collective-permute-start(bf16[96,2048]{1,0:T(8,128)(2,1)S(1)} %add_convert_fusion.10), channel_id=1, source_target_pairs={{0,8},{8,0},{16,24},{24,16},{1,9},{9,1},{17,25},{25,17},{2,10},{10... | collective-permute-start | bytes 1179656 | tf_op jit(solution)/shard_map/ppermute | solution.py:163
  381.0 11.9 %collective-permute-done.65 = bf16[96,2048]{1,0:T(8,128)(2,1)S(1)} collective-permute-done((bf16[96,2048]{1,0:T(8,128)(2,1)S(1)}, bf16[96,2048]{1,0:T(8,128)(2,1)S(1)}, u32[]{:S(2)}, u32[]{:S(2)}) %collective-permute-start.65) | collective-permute-done | bytes 393248 | tf_op jit(solution)/shard_map/ppermute | solution.py:163
  393.8 7.6 %collective-permute-done.57 = bf16[96,2048]{1,0:T(8,128)(2,1)S(1)} collective-permute-done((bf16[96,2048]{1,0:T(8,128)(2,1)S(1)}, bf16[96,2048]{1,0:T(8,128)(2,1)S(1)}, u32[]{:S(2)}, u32[]{:S(2)}) %collective-permute-start.57) | collective-permute-done | bytes 393248 | tf_op jit(solution)/shard_map/ppermute | solution.py:163
  402.3 7.5 %collective-permute-done.49 = bf16[96,2048]{1,0:T(8,128)(2,1)S(1)} collective-permute-done((bf16[96,2048]{1,0:T(8,128)(2,1)S(1)}, bf16[96,2048]{1,0:T(8,128)(2,1)S(1)}, u32[]{:S(2)}, u32[]{:S(2)}) %collective-permute-start.49) | collective-permute-done | bytes 393248 | tf_op jit(solution)/shard_map/ppermute | solution.py:163
  409.8 8.4 %collective-permute-done.41 = bf16[96,2048]{1,0:T(8,128)(2,1)S(1)} collective-permute-done((bf16[96,2048]{1,0:T(8,128)(2,1)S(1)}, bf16[96,2048]{1,0:T(8,128)(2,1)S(1)}, u32[]{:S(2)}, u32[]{:S(2)}) %collective-permute-start.41) | collective-permute-done | bytes 393248 | tf_op jit(solution)/shard_map/ppermute | solution.py:163
  424.6 18.3 %collective-permute-done.5 = bf16[96,2048]{1,0:T(8,128)(2,1)S(1)} collective-permute-done((bf16[96,2048]{1,0:T(8,128)(2,1)S(1)}, bf16[96,2048]{1,0:T(8,128)(2,1)S(1)}, u32[]{:S(2)}, u32[]{:S(2)}) %collective-permute-start.5) | collective-permute-done | bytes 393248 | tf_op jit(solution)/shard_map/ppermute | solution.py:160
  452.2 12.1 %collective-permute-done.50.refs_1_ = bf16[192,2048]{1,0:T(8,128)(2,1)} collective-permute-done((bf16[192,2048]{1,0:T(8,128)(2,1)S(1)}, bf16[192,2048]{1,0:T(8,128)(2,1)}, u32[]{:S(2)}, u32[]{:S(2)}) %collective-permute-start.50) | collective-permute-done | bytes 786464 | tf_op jit(solution)/shard_map/ppermute | solution.py:160
  464.3 16.4 %collective-permute-done.42.refs_1_ = bf16[192,2048]{1,0:T(8,128)(2,1)} collective-permute-done((bf16[192,2048]{1,0:T(8,128)(2,1)S(1)}, bf16[192,2048]{1,0:T(8,128)(2,1)}, u32[]{:S(2)}, u32[]{:S(2)}) %collective-permute-start.42) | collective-permute-done | bytes 786464 | tf_op jit(solution)/shard_map/ppermute | solution.py:160
  483.6 16.2 %collective-permute-done.26.refs_1_ = bf16[192,2048]{1,0:T(8,128)(2,1)} collective-permute-done((bf16[192,2048]{1,0:T(8,128)(2,1)S(1)}, bf16[192,2048]{1,0:T(8,128)(2,1)}, u32[]{:S(2)}, u32[]{:S(2)}) %collective-permute-start.26) | collective-permute-done | bytes 786464 | tf_op jit(solution)/shard_map/ppermute | solution.py:160
  523.1 6.6 %shard_map.65.refs_8_ = f32[14336,512]{1,0:T(8,128)} custom-call(s32[4]{0:T(128)S(1)} %pad_add_fusion.where_ref, bf16[192,2048]{1,0:T(8,128)(2,1)S(1)} %pad_maximum_fusion.6.refs_0_, bf16[192,2048]{1,0:T(8,128)(2,1)} %collective-permute-done.42.refs_1_, bf16[192,2048]{1,0:T(8,128)(2,1)} %collective-permute-done.43.refs_2_, ...), custom_call_target="tpu_custom_call", output_to_operand_aliasing={{}: (9, {})} | custom-call | flops 2147483648 | bytes 7340032 | tf_op jit(solution)/shard_map/pallas_call | solution.py:128
  529.7 6.7 %shard_map.66.refs_8_ = f32[14336,512]{1,0:T(8,128)} custom-call(s32[4]{0:T(128)S(1)} %pad_add_fusion.where_ref, bf16[192,2048]{1,0:T(8,128)(2,1)} %pad_maximum_fusion.5.refs_0_, bf16[192,2048]{1,0:T(8,128)(2,1)} %collective-permute-done.34.refs_1_, bf16[192,2048]{1,0:T(8,128)(2,1)} %collective-permute-done.35.refs_2_, ...), custom_call_target="tpu_custom_call", output_to_operand_aliasing={{}: (9, {})} | custom-call | flops 2147483648 | bytes 7340032 | tf_op jit(solution)/shard_map/pallas_call | solution.py:128
  (237 shorter events, 154.4 us)
Async XLA Ops:
  8.9 41.9 %collective-permute-start = (bf16[512,1792]{1,0:T(8,128)(2,1)}, bf16[512,1792]{1,0:T(8,128)(2,1)S(1)}, u32[]{:S(2)}, u32[]{:S(2)}) collective-permute-start(bf16[512,1792]{1,0:T(8,128)(2,1)} %param.5), channel_id=1, source_target_pairs={{0,4},{4,0},{1,5},{5,1},{2,6},{6,2},{3,7},{7,3},{8,12},{12,8},{9,1... | collective-permute-start | bytes 5505032 | tf_op jit(solution)/shard_map/ppermute | solution.py:196
  47.4 69.2 %collective-permute-start.17 = (bf16[128,4096]{1,0:T(8,128)(2,1)S(1)}, bf16[128,4096]{1,0:T(8,128)(2,1)S(1)}, u32[]{:S(2)}, u32[]{:S(2)}) collective-permute-start(bf16[128,4096]{1,0:T(8,128)(2,1)S(1)} %pad_maximum_fusion.2), channel_id=1, source_target_pairs={{0,2},{2,0},{1,3},{3,1},{4,6},{6,4},{5,7},{7,5},{8,10},{10,8},{9,1... | collective-permute-start | bytes 3145736 | tf_op jit(solution)/shard_map/ppermute | solution.py:160
  48.5 81.3 %collective-permute-start.18 = (bf16[256,4096]{1,0:T(8,128)(2,1)S(1)}, bf16[256,4096]{1,0:T(8,128)(2,1)}, u32[]{:S(2)}, u32[]{:S(2)}) collective-permute-start(bf16[256,4096]{1,0:T(8,128)(2,1)S(1)} %pad_maximum_fusion), channel_id=1, source_target_pairs={{0,1},{1,0},{2,3},{3,2},{4,5},{5,4},{6,7},{7,6},{8,9},{9,8},{10,11... | collective-permute-start | bytes 6291464 | tf_op jit(solution)/shard_map/ppermute | solution.py:157
  122.2 176.0 %collective-permute-start.19 = (bf16[256,4096]{1,0:T(8,128)(2,1)S(1)}, bf16[256,4096]{1,0:T(8,128)(2,1)S(1)}, u32[]{:S(2)}, u32[]{:S(2)}) collective-permute-start(bf16[256,4096]{1,0:T(8,128)(2,1)S(1)} %constant_dynamic-update-slice_fusion), channel_id=1, source_target_pairs={{0,1},{1,0},{2,3},{3,2},{4,5},{5,4},{6,7},{7,6},{8,9},{9,8},{10,11... | collective-permute-start | bytes 6291464 | tf_op jit(solution)/shard_map/ppermute | solution.py:157
  126.7 35.0 %collective-permute-start.54 = (bf16[192,2048]{1,0:T(8,128)(2,1)S(1)}, bf16[192,2048]{1,0:T(8,128)(2,1)S(1)}, u32[]{:S(2)}, u32[]{:S(2)}) collective-permute-start(bf16[192,2048]{1,0:T(8,128)(2,1)S(1)} %add_convert_fusion.3), channel_id=1, source_target_pairs={{0,2},{2,0},{1,3},{3,1},{4,6},{6,4},{5,7},{7,5},{8,10},{10,8},{9,1... | collective-permute-start | bytes 2359304 | tf_op jit(solution)/shard_map/ppermute | solution.py:160
  129.0 49.6 %collective-permute-start.46 = (bf16[192,2048]{1,0:T(8,128)(2,1)S(1)}, bf16[192,2048]{1,0:T(8,128)(2,1)S(1)}, u32[]{:S(2)}, u32[]{:S(2)}) collective-permute-start(bf16[192,2048]{1,0:T(8,128)(2,1)S(1)} %add_convert_fusion.4), channel_id=1, source_target_pairs={{0,2},{2,0},{1,3},{3,1},{4,6},{6,4},{5,7},{7,5},{8,10},{10,8},{9,1... | collective-permute-start | bytes 2359304 | tf_op jit(solution)/shard_map/ppermute | solution.py:160
  129.7 65.7 %collective-permute-start.38 = (bf16[192,2048]{1,0:T(8,128)(2,1)S(1)}, bf16[192,2048]{1,0:T(8,128)(2,1)S(1)}, u32[]{:S(2)}, u32[]{:S(2)}) collective-permute-start(bf16[192,2048]{1,0:T(8,128)(2,1)S(1)} %add_convert_fusion.5), channel_id=1, source_target_pairs={{0,2},{2,0},{1,3},{3,1},{4,6},{6,4},{5,7},{7,5},{8,10},{10,8},{9,1... | collective-permute-start | bytes 2359304 | tf_op jit(solution)/shard_map/ppermute | solution.py:160
  144.9 67.4 %collective-permute-start.30 = (bf16[192,2048]{1,0:T(8,128)(2,1)S(1)}, bf16[192,2048]{1,0:T(8,128)(2,1)S(1)}, u32[]{:S(2)}, u32[]{:S(2)}) collective-permute-start(bf16[192,2048]{1,0:T(8,128)(2,1)S(1)} %add_convert_fusion.6), channel_id=1, source_target_pairs={{0,2},{2,0},{1,3},{3,1},{4,6},{6,4},{5,7},{7,5},{8,10},{10,8},{9,1... | collective-permute-start | bytes 2359304 | tf_op jit(solution)/shard_map/ppermute | solution.py:160
  161.7 67.4 %collective-permute-start.22 = (bf16[192,2048]{1,0:T(8,128)(2,1)S(1)}, bf16[192,2048]{1,0:T(8,128)(2,1)S(1)}, u32[]{:S(2)}, u32[]{:S(2)}) collective-permute-start(bf16[192,2048]{1,0:T(8,128)(2,1)S(1)} %add_convert_fusion.7), channel_id=1, source_target_pairs={{0,2},{2,0},{1,3},{3,1},{4,6},{6,4},{5,7},{7,5},{8,10},{10,8},{9,1... | collective-permute-start | bytes 2359304 | tf_op jit(solution)/shard_map/ppermute | solution.py:160
  178.6 66.6 %collective-permute-start.2 = (bf16[192,2048]{1,0:T(8,128)(2,1)S(1)}, bf16[192,2048]{1,0:T(8,128)(2,1)S(1)}, u32[]{:S(2)}, u32[]{:S(2)}) collective-permute-start(bf16[192,2048]{1,0:T(8,128)(2,1)S(1)} %add_convert_fusion.8), channel_id=1, source_target_pairs={{0,2},{2,0},{1,3},{3,1},{4,6},{6,4},{5,7},{7,5},{8,10},{10,8},{9,1... | collective-permute-start | bytes 2359304 | tf_op jit(solution)/shard_map/ppermute | solution.py:160
  195.4 51.9 %collective-permute-start.63 = (bf16[96,2048]{1,0:T(8,128)(2,1)S(1)}, bf16[96,2048]{1,0:T(8,128)(2,1)S(1)}, u32[]{:S(2)}, u32[]{:S(2)}) collective-permute-start(bf16[96,2048]{1,0:T(8,128)(2,1)S(1)} %add_convert_fusion.11), channel_id=1, source_target_pairs={{0,8},{8,0},{16,24},{24,16},{1,9},{9,1},{17,25},{25,17},{2,10},{10... | collective-permute-start | bytes 1179656 | tf_op jit(solution)/shard_map/ppermute | solution.py:163
  212.3 35.4 %collective-permute-start.55 = (bf16[96,2048]{1,0:T(8,128)(2,1)S(1)}, bf16[96,2048]{1,0:T(8,128)(2,1)S(1)}, u32[]{:S(2)}, u32[]{:S(2)}) collective-permute-start(bf16[96,2048]{1,0:T(8,128)(2,1)S(1)} %add_convert_fusion.13), channel_id=1, source_target_pairs={{0,8},{8,0},{16,24},{24,16},{1,9},{9,1},{17,25},{25,17},{2,10},{10... | collective-permute-start | bytes 1179656 | tf_op jit(solution)/shard_map/ppermute | solution.py:163
  247.7 43.2 %collective-permute-start.23 = (bf16[96,2048]{1,0:T(8,128)(2,1)S(1)}, bf16[96,2048]{1,0:T(8,128)(2,1)S(1)}, u32[]{:S(2)}, u32[]{:S(2)}) collective-permute-start(bf16[96,2048]{1,0:T(8,128)(2,1)S(1)} %add_convert_fusion.21), channel_id=1, source_target_pairs={{0,8},{8,0},{16,24},{24,16},{1,9},{9,1},{17,25},{25,17},{2,10},{10... | collective-permute-start | bytes 1179656 | tf_op jit(solution)/shard_map/ppermute | solution.py:163
  250.0 48.0 %collective-permute-start.3 = (bf16[96,2048]{1,0:T(8,128)(2,1)S(1)}, bf16[96,2048]{1,0:T(8,128)(2,1)S(1)}, u32[]{:S(2)}, u32[]{:S(2)}) collective-permute-start(bf16[96,2048]{1,0:T(8,128)(2,1)S(1)} %add_convert_fusion.23), channel_id=1, source_target_pairs={{0,8},{8,0},{16,24},{24,16},{1,9},{9,1},{17,25},{25,17},{2,10},{10... | collective-permute-start | bytes 1179656 | tf_op jit(solution)/shard_map/ppermute | solution.py:163
  257.2 45.3 %collective-permute-start.64 = (bf16[96,2048]{1,0:T(8,128)(2,1)S(1)}, bf16[96,2048]{1,0:T(8,128)(2,1)S(1)}, u32[]{:S(2)}, u32[]{:S(2)}) collective-permute-start(bf16[96,2048]{1,0:T(8,128)(2,1)S(1)} %fusion.20), channel_id=1, source_target_pairs={{0,16},{16,0},{8,24},{24,8},{1,17},{17,1},{9,25},{25,9},{2,18},{18... | collective-permute-start | bytes 1179656 | tf_op jit(solution)/shard_map/ppermute | solution.py:166
  274.0 28.8 %collective-permute-start.56 = (bf16[96,2048]{1,0:T(8,128)(2,1)S(1)}, bf16[96,2048]{1,0:T(8,128)(2,1)S(1)}, u32[]{:S(2)}, u32[]{:S(2)}) collective-permute-start(bf16[96,2048]{1,0:T(8,128)(2,1)S(1)} %fusion.19), channel_id=1, source_target_pairs={{0,16},{16,0},{8,24},{24,8},{1,17},{17,1},{9,25},{25,9},{2,18},{18... | collective-permute-start | bytes 1179656 | tf_op jit(solution)/shard_map/ppermute | solution.py:166
  290.9 56.4 %collective-permute-start.48 = (bf16[96,2048]{1,0:T(8,128)(2,1)S(1)}, bf16[96,2048]{1,0:T(8,128)(2,1)S(1)}, u32[]{:S(2)}, u32[]{:S(2)}) collective-permute-start(bf16[96,2048]{1,0:T(8,128)(2,1)S(1)} %fusion.18), channel_id=1, source_target_pairs={{0,16},{16,0},{8,24},{24,8},{1,17},{17,1},{9,25},{25,9},{2,18},{18... | collective-permute-start | bytes 1179656 | tf_op jit(solution)/shard_map/ppermute | solution.py:166
  297.9 62.1 %collective-permute-start.40 = (bf16[96,2048]{1,0:T(8,128)(2,1)S(1)}, bf16[96,2048]{1,0:T(8,128)(2,1)S(1)}, u32[]{:S(2)}, u32[]{:S(2)}) collective-permute-start(bf16[96,2048]{1,0:T(8,128)(2,1)S(1)} %fusion.17), channel_id=1, source_target_pairs={{0,16},{16,0},{8,24},{24,8},{1,17},{17,1},{9,25},{25,9},{2,18},{18... | collective-permute-start | bytes 1179656 | tf_op jit(solution)/shard_map/ppermute | solution.py:166
  298.2 70.3 %collective-permute-start.32 = (bf16[96,2048]{1,0:T(8,128)(2,1)S(1)}, bf16[96,2048]{1,0:T(8,128)(2,1)S(1)}, u32[]{:S(2)}, u32[]{:S(2)}) collective-permute-start(bf16[96,2048]{1,0:T(8,128)(2,1)S(1)} %fusion.16), channel_id=1, source_target_pairs={{0,16},{16,0},{8,24},{24,8},{1,17},{17,1},{9,25},{25,9},{2,18},{18... | collective-permute-start | bytes 1179656 | tf_op jit(solution)/shard_map/ppermute | solution.py:166
  302.4 74.4 %collective-permute-start.24 = (bf16[96,2048]{1,0:T(8,128)(2,1)S(1)}, bf16[96,2048]{1,0:T(8,128)(2,1)S(1)}, u32[]{:S(2)}, u32[]{:S(2)}) collective-permute-start(bf16[96,2048]{1,0:T(8,128)(2,1)S(1)} %fusion.15), channel_id=1, source_target_pairs={{0,16},{16,0},{8,24},{24,8},{1,17},{17,1},{9,25},{25,9},{2,18},{18... | collective-permute-start | bytes 1179656 | tf_op jit(solution)/shard_map/ppermute | solution.py:166
  302.9 98.6 %collective-permute-start.4 = (bf16[96,2048]{1,0:T(8,128)(2,1)S(1)}, bf16[96,2048]{1,0:T(8,128)(2,1)S(1)}, u32[]{:S(2)}, u32[]{:S(2)}) collective-permute-start(bf16[96,2048]{1,0:T(8,128)(2,1)S(1)} %fusion.14), channel_id=1, source_target_pairs={{0,16},{16,0},{8,24},{24,8},{1,17},{17,1},{9,25},{25,9},{2,18},{18... | collective-permute-start | bytes 1179656 | tf_op jit(solution)/shard_map/ppermute | solution.py:166
  347.3 45.7 %collective-permute-start.65 = (bf16[96,2048]{1,0:T(8,128)(2,1)S(1)}, bf16[96,2048]{1,0:T(8,128)(2,1)S(1)}, u32[]{:S(2)}, u32[]{:S(2)}) collective-permute-start(bf16[96,2048]{1,0:T(8,128)(2,1)S(1)} %add_convert_fusion.10), channel_id=1, source_target_pairs={{0,8},{8,0},{16,24},{24,16},{1,9},{9,1},{17,25},{25,17},{2,10},{10... | collective-permute-start | bytes 1179656 | tf_op jit(solution)/shard_map/ppermute | solution.py:163
  360.0 41.3 %collective-permute-start.57 = (bf16[96,2048]{1,0:T(8,128)(2,1)S(1)}, bf16[96,2048]{1,0:T(8,128)(2,1)S(1)}, u32[]{:S(2)}, u32[]{:S(2)}) collective-permute-start(bf16[96,2048]{1,0:T(8,128)(2,1)S(1)} %add_convert_fusion.12), channel_id=1, source_target_pairs={{0,8},{8,0},{16,24},{24,16},{1,9},{9,1},{17,25},{25,17},{2,10},{10... | collective-permute-start | bytes 1179656 | tf_op jit(solution)/shard_map/ppermute | solution.py:163
  368.5 41.3 %collective-permute-start.49 = (bf16[96,2048]{1,0:T(8,128)(2,1)S(1)}, bf16[96,2048]{1,0:T(8,128)(2,1)S(1)}, u32[]{:S(2)}, u32[]{:S(2)}) collective-permute-start(bf16[96,2048]{1,0:T(8,128)(2,1)S(1)} %add_convert_fusion.14), channel_id=1, source_target_pairs={{0,8},{8,0},{16,24},{24,16},{1,9},{9,1},{17,25},{25,17},{2,10},{10... | collective-permute-start | bytes 1179656 | tf_op jit(solution)/shard_map/ppermute | solution.py:163
  376.9 41.3 %collective-permute-start.41 = (bf16[96,2048]{1,0:T(8,128)(2,1)S(1)}, bf16[96,2048]{1,0:T(8,128)(2,1)S(1)}, u32[]{:S(2)}, u32[]{:S(2)}) collective-permute-start(bf16[96,2048]{1,0:T(8,128)(2,1)S(1)} %add_convert_fusion.16), channel_id=1, source_target_pairs={{0,8},{8,0},{16,24},{24,16},{1,9},{9,1},{17,25},{25,17},{2,10},{10... | collective-permute-start | bytes 1179656 | tf_op jit(solution)/shard_map/ppermute | solution.py:163
  401.5 42.2 %collective-permute-start.66 = (bf16[192,2048]{1,0:T(8,128)(2,1)S(1)}, bf16[192,2048]{1,0:T(8,128)(2,1)S(1)}, u32[]{:S(2)}, u32[]{:S(2)}) collective-permute-start(bf16[192,2048]{1,0:T(8,128)(2,1)S(1)} %pad_maximum_fusion.9.refs_0_), channel_id=1, source_target_pairs={{0,2},{2,0},{1,3},{3,1},{4,6},{6,4},{5,7},{7,5},{8,10},{10,8},{9,1... | collective-permute-start | bytes 2359304 | tf_op jit(solution)/shard_map/ppermute | solution.py:160
  409.8 34.8 %collective-permute-start.67 = (bf16[192,2048]{1,0:T(8,128)(2,1)S(1)}, bf16[192,2048]{1,0:T(8,128)(2,1)S(1)}, u32[]{:S(2)}, u32[]{:S(2)}) collective-permute-start(bf16[192,2048]{1,0:T(8,128)(2,1)S(1)} %pad_maximum_fusion.9.refs_0_), channel_id=1, source_target_pairs={{0,1},{1,0},{2,3},{3,2},{4,5},{5,4},{6,7},{7,6},{8,9},{9,8},{10,11... | collective-permute-start | bytes 2359304 | tf_op jit(solution)/shard_map/ppermute | solution.py:157
  418.2 27.5 %collective-permute-start.58 = (bf16[192,2048]{1,0:T(8,128)(2,1)S(1)}, bf16[192,2048]{1,0:T(8,128)(2,1)S(1)}, u32[]{:S(2)}, u32[]{:S(2)}) collective-permute-start(bf16[192,2048]{1,0:T(8,128)(2,1)S(1)} %pad_maximum_fusion.8.refs_0_), channel_id=1, source_target_pairs={{0,2},{2,0},{1,3},{3,1},{4,6},{6,4},{5,7},{7,5},{8,10},{10,8},{9,1... | collective-permute-start | bytes 2359304 | tf_op jit(solution)/shard_map/ppermute | solution.py:160
  423.0 76.8 %collective-permute-start.20 = (f32[1024,512]{1,0:T(8,128)}, f32[1024,512]{1,0:T(8,128)}, u32[]{:S(2)}, u32[]{:S(2)}) collective-permute-start(f32[1024,512]{1,0:T(8,128)} %pad_maximum_fusion.1), channel_id=1, source_target_pairs={{0,4},{4,0},{1,5},{5,1},{2,6},{6,2},{3,7},{7,3},{8,12},{12,8},{9,1... | collective-permute-start | bytes 6291464 | tf_op jit(solution)/shard_map/ppermute | solution.py:233
  446.7 34.0 %collective-permute-start.42 = (bf16[192,2048]{1,0:T(8,128)(2,1)S(1)}, bf16[192,2048]{1,0:T(8,128)(2,1)}, u32[]{:S(2)}, u32[]{:S(2)}) collective-permute-start(bf16[192,2048]{1,0:T(8,128)(2,1)S(1)} %pad_maximum_fusion.6.refs_0_), channel_id=1, source_target_pairs={{0,2},{2,0},{1,3},{3,1},{4,6},{6,4},{5,7},{7,5},{8,10},{10,8},{9,1... | collective-permute-start | bytes 2359304 | tf_op jit(solution)/shard_map/ppermute | solution.py:160
  451.0 30.7 %collective-permute-start.43 = (bf16[192,2048]{1,0:T(8,128)(2,1)S(1)}, bf16[192,2048]{1,0:T(8,128)(2,1)}, u32[]{:S(2)}, u32[]{:S(2)}) collective-permute-start(bf16[192,2048]{1,0:T(8,128)(2,1)S(1)} %pad_maximum_fusion.6.refs_0_), channel_id=1, source_target_pairs={{0,1},{1,0},{2,3},{3,2},{4,5},{5,4},{6,7},{7,6},{8,9},{9,8},{10,11... | collective-permute-start | bytes 2359304 | tf_op jit(solution)/shard_map/ppermute | solution.py:157
  483.2 27.0 %collective-permute-start.6 = (bf16[192,2048]{1,0:T(8,128)(2,1)S(1)}, bf16[192,2048]{1,0:T(8,128)(2,1)S(1)}, u32[]{:S(2)}, u32[]{:S(2)}) collective-permute-start(bf16[192,2048]{1,0:T(8,128)(2,1)S(1)} %pad_maximum_fusion.3.refs_0_), channel_id=1, source_target_pairs={{0,8},{8,0},{16,24},{24,16},{1,9},{9,1},{17,25},{25,17},{2,10},{10... | collective-permute-start | bytes 2359304 | tf_op jit(solution)/shard_map/ppermute | solution.py:163
  (58 other events, 1852.4 us)

commit v4 on v3

--- a/solution.py
+++ b/solution.py
@@ -14,9 +14,9 @@
 KINDS = (1, 1, 1, 1, 2, 1, 2)
 PARTS = 14
 ORDER = (
-    (0, 0), (1, 0), (0, 1), (2, 0), (1, 1), (2, 1), (3, 0), (3, 1), (0, 2), (4, 0),
-    (0, 3), (1, 2), (5, 0), (2, 2), (4, 1), (5, 1), (1, 3), (0, 4), (6, 0), (3, 2),
-    (2, 3), (6, 1), (1, 4), (0, 5), (4, 2), (3, 3), (2, 4), (5, 2), (1, 5), (4, 3),
+    (0, 0), (1, 0), (0, 1), (2, 0), (1, 1), (2, 1), (3, 0), (0, 2), (3, 1), (4, 0),
+    (0, 3), (1, 2), (4, 1), (5, 0), (2, 2), (6, 0), (1, 3), (0, 4), (3, 2), (2, 3),
+    (5, 1), (6, 1), (0, 5), (1, 4), (4, 2), (3, 3), (2, 4), (5, 2), (1, 5), (4, 3),
     (6, 2), (3, 4), (2, 5), (0, 6), (0, 7), (5, 3), (4, 4), (1, 6), (1, 7), (6, 3),
     (3, 5), (2, 6), (2, 7), (5, 4), (4, 5), (6, 4), (5, 5), (3, 6), (3, 7), (6, 5),
     (4, 6), (4, 7), (5, 6), (5, 7), (6, 6), (6, 7),

time: 553 us -> 553 us (level)
  no operation moved by 1% of the time
where the time goes in v4:
time: 553 us; the launch traced here: 548 us
  waiting for transfers between devices  326 us (59%)
  Pallas kernels  105 us (19%)
  starting transfers between devices  75.4 us (14%)
  other arithmetic  16.2 us (3%)
  matrix products  14.7 us (3%)
  local copies, waits for them, and re-layouts  6.96 us (1%)
    ppermute x17, waiting for transfers between devices, across_side(): return lax.ppermute(x, 'col', [(0, 2), (2, 0), (1, 3), (3, 1)])  166 us
    ppermute x14, waiting for transfers between devices, across_pair(): return lax.ppermute(x, 'seq', [(0, 1), (1, 0), (2, 3), (3, 2)])  76.5 us
    pallas_call x7, Pallas kernels, project(): pl.pallas_call(kernel, grid_spec=pltpu.PrefetchScalarGridSpec(num_scalar_...  63.2 us
    ppermute x7, waiting for transfers between devices, across_half(): return lax.ppermute(x, 'seq', [(0, 2), (2, 0), (1, 3), (3, 1)])  54 us
    pallas_call x7, Pallas kernels, finish(): pl.pallas_call(kernel, grid_spec=pltpu.PrefetchScalarGridSpec(num_scalar_...  41.8 us
    ppermute x14, starting transfers between devices, across_pair(): return lax.ppermute(x, 'seq', [(0, 1), (1, 0), (2, 3), (3, 2)])  30.1 us
    ppermute x3, waiting for transfers between devices, act_sets(): lax.ppermute(down[-1], 'seq', [(i + 1, i) for i in range(3 - step)])  23.1 us
    dot_general x7, matrix products, dot(): return jnp.dot(lhs, rhs, preferred_element_type=F32)  14.7 us
  transfers between devices with their start and end apart: 69, of which 32 were waited for; matrix products, arithmetic and copies ran while one was open for 6% of the time, Pallas kernels for 18%

profile of v4, /device:TPU:0, one launch (start us, length us, event | category | flops | bytes accessed | tf_op | source)
XLA Modules:
  0.0 547.9 jit_solution(13439902489904665262)
XLA Ops:
  21.3 12.3 %collective-permute-done.10 = bf16[64,4096]{1,0:T(8,128)(2,1)S(1)} collective-permute-done((bf16[64,4096]{1,0:T(8,128)(2,1)S(1)}, bf16[64,4096]{1,0:T(8,128)(2,1)S(1)}, u32[]{:S(2)}, u32[]{:S(2)}) %collective-permute-start.10) | collective-permute-done | bytes 524320 | tf_op jit(solution)/shard_map/ppermute | solution.py:211
  36.4 10.8 %collective-permute-done.14 = bf16[64,4096]{1,0:T(8,128)(2,1)S(1)} collective-permute-done((bf16[64,4096]{1,0:T(8,128)(2,1)S(1)}, bf16[64,4096]{1,0:T(8,128)(2,1)S(1)}, u32[]{:S(2)}, u32[]{:S(2)}) %collective-permute-start.14) | collective-permute-done | bytes 524320 | tf_op jit(solution)/shard_map/ppermute | solution.py:211
  52.6 9.0 %shard_map.61 = (bf16[384,2048]{1,0:T(8,128)(2,1)S(1)}, bf16[192,2048]{1,0:T(8,128)(2,1)S(1)}, bf16[192,2048]{1,0:T(8,128)(2,1)S(1)}) custom-call(s32[4]{0:T(128)S(1)} %pad_add_fusion.where_ref, bf16[768,1792]{1,0:T(8,128)(2,1)S(1)} %add_convert_fusion.lhs_ref, bf16[1792,14336]{1,0:T(8,128)(2,1)} %rhs_ref.13), custom_call_target="tpu_custom_call" | custom-call | flops 5637144576 | bytes 10485760 | tf_op jit(solution)/shard_map/pallas_call | solution.py:60
  61.6 9.0 %shard_map.60 = (bf16[384,2048]{1,0:T(8,128)(2,1)S(1)}, bf16[192,2048]{1,0:T(8,128)(2,1)S(1)}, bf16[192,2048]{1,0:T(8,128)(2,1)S(1)}) custom-call(s32[4]{0:T(128)S(1)} %pad_add_fusion.where_ref, bf16[768,1792]{1,0:T(8,128)(2,1)S(1)} %add_convert_fusion.lhs_ref, bf16[1792,14336]{1,0:T(8,128)(2,1)} %rhs_ref.13), custom_call_target="tpu_custom_call" | custom-call | flops 5637144576 | bytes 10485760 | tf_op jit(solution)/shard_map/pallas_call | solution.py:60
  70.6 9.0 %shard_map.59 = (bf16[384,2048]{1,0:T(8,128)(2,1)S(1)}, bf16[192,2048]{1,0:T(8,128)(2,1)S(1)}, bf16[192,2048]{1,0:T(8,128)(2,1)S(1)}) custom-call(s32[4]{0:T(128)S(1)} %pad_add_fusion.where_ref, bf16[768,1792]{1,0:T(8,128)(2,1)S(1)} %add_convert_fusion.lhs_ref, bf16[1792,14336]{1,0:T(8,128)(2,1)} %rhs_ref.13), custom_call_target="tpu_custom_call" | custom-call | flops 5637144576 | bytes 10485760 | tf_op jit(solution)/shard_map/pallas_call | solution.py:60
  79.6 9.0 %shard_map.58 = (bf16[384,2048]{1,0:T(8,128)(2,1)S(1)}, bf16[192,2048]{1,0:T(8,128)(2,1)S(1)}, bf16[192,2048]{1,0:T(8,128)(2,1)S(1)}) custom-call(s32[4]{0:T(128)S(1)} %pad_add_fusion.where_ref, bf16[768,1792]{1,0:T(8,128)(2,1)S(1)} %add_convert_fusion.lhs_ref, bf16[1792,14336]{1,0:T(8,128)(2,1)} %rhs_ref.13), custom_call_target="tpu_custom_call" | custom-call | flops 5637144576 | bytes 10485760 | tf_op jit(solution)/shard_map/pallas_call | solution.py:60
  88.6 9.0 %shard_map.57 = (bf16[384,2048]{1,0:T(8,128)(2,1)S(1)}, bf16[192,2048]{1,0:T(8,128)(2,1)S(1)}, bf16[192,2048]{1,0:T(8,128)(2,1)S(1)}) custom-call(s32[4]{0:T(128)S(1)} %pad_add_fusion.where_ref, bf16[768,1792]{1,0:T(8,128)(2,1)S(1)} %add_convert_fusion.lhs_ref, bf16[1792,14336]{1,0:T(8,128)(2,1)} %rhs_ref.13), custom_call_target="tpu_custom_call" | custom-call | flops 5637144576 | bytes 10485760 | tf_op jit(solution)/shard_map/pallas_call | solution.py:60
  97.7 9.0 %shard_map.56 = (bf16[384,2048]{1,0:T(8,128)(2,1)S(1)}, bf16[192,2048]{1,0:T(8,128)(2,1)S(1)}, bf16[192,2048]{1,0:T(8,128)(2,1)S(1)}) custom-call(s32[4]{0:T(128)S(1)} %pad_add_fusion.where_ref, bf16[768,1792]{1,0:T(8,128)(2,1)S(1)} %add_convert_fusion.lhs_ref, bf16[1792,14336]{1,0:T(8,128)(2,1)} %rhs_ref.13), custom_call_target="tpu_custom_call" | custom-call | flops 5637144576 | bytes 10485760 | tf_op jit(solution)/shard_map/pallas_call | solution.py:60
  107.3 9.2 %shard_map.55 = (bf16[384,2048]{1,0:T(8,128)(2,1)S(1)}, bf16[192,2048]{1,0:T(8,128)(2,1)S(1)}, bf16[192,2048]{1,0:T(8,128)(2,1)S(1)}) custom-call(s32[4]{0:T(128)S(1)} %pad_add_fusion.where_ref, bf16[768,1792]{1,0:T(8,128)(2,1)S(1)} %add_convert_fusion.lhs_ref, bf16[1792,14336]{1,0:T(8,128)(2,1)} %rhs_ref.13), custom_call_target="tpu_custom_call" | custom-call | flops 5637144576 | bytes 10485760 | tf_op jit(solution)/shard_map/pallas_call | solution.py:60
  134.2 10.6 %collective-permute-done.62 = bf16[192,2048]{1,0:T(8,128)(2,1)S(1)} collective-permute-done((bf16[192,2048]{1,0:T(8,128)(2,1)S(1)}, bf16[192,2048]{1,0:T(8,128)(2,1)S(1)}, u32[]{:S(2)}, u32[]{:S(2)}) %collective-permute-start.62) | collective-permute-done | bytes 786464 | tf_op jit(solution)/shard_map/ppermute | solution.py:160
  145.5 16.2 %collective-permute-done.54 = bf16[192,2048]{1,0:T(8,128)(2,1)S(1)} collective-permute-done((bf16[192,2048]{1,0:T(8,128)(2,1)S(1)}, bf16[192,2048]{1,0:T(8,128)(2,1)S(1)}, u32[]{:S(2)}, u32[]{:S(2)}) %collective-permute-start.54) | collective-permute-done | bytes 786464 | tf_op jit(solution)/shard_map/ppermute | solution.py:160
  162.4 16.2 %collective-permute-done.46 = bf16[192,2048]{1,0:T(8,128)(2,1)S(1)} collective-permute-done((bf16[192,2048]{1,0:T(8,128)(2,1)S(1)}, bf16[192,2048]{1,0:T(8,128)(2,1)S(1)}, u32[]{:S(2)}, u32[]{:S(2)}) %collective-permute-start.46) | collective-permute-done | bytes 786464 | tf_op jit(solution)/shard_map/ppermute | solution.py:160
  179.2 16.2 %collective-permute-done.38 = bf16[192,2048]{1,0:T(8,128)(2,1)S(1)} collective-permute-done((bf16[192,2048]{1,0:T(8,128)(2,1)S(1)}, bf16[192,2048]{1,0:T(8,128)(2,1)S(1)}, u32[]{:S(2)}, u32[]{:S(2)}) %collective-permute-start.38) | collective-permute-done | bytes 786464 | tf_op jit(solution)/shard_map/ppermute | solution.py:160
  197.6 14.7 %collective-permute-done.30 = bf16[192,2048]{1,0:T(8,128)(2,1)S(1)} collective-permute-done((bf16[192,2048]{1,0:T(8,128)(2,1)S(1)}, bf16[192,2048]{1,0:T(8,128)(2,1)S(1)}, u32[]{:S(2)}, u32[]{:S(2)}) %collective-permute-start.30) | collective-permute-done | bytes 786464 | tf_op jit(solution)/shard_map/ppermute | solution.py:160
  214.4 14.7 %collective-permute-done.22 = bf16[192,2048]{1,0:T(8,128)(2,1)S(1)} collective-permute-done((bf16[192,2048]{1,0:T(8,128)(2,1)S(1)}, bf16[192,2048]{1,0:T(8,128)(2,1)S(1)}, u32[]{:S(2)}, u32[]{:S(2)}) %collective-permute-start.22) | collective-permute-done | bytes 786464 | tf_op jit(solution)/shard_map/ppermute | solution.py:160
  231.3 13.9 %collective-permute-done.2 = bf16[192,2048]{1,0:T(8,128)(2,1)S(1)} collective-permute-done((bf16[192,2048]{1,0:T(8,128)(2,1)S(1)}, bf16[192,2048]{1,0:T(8,128)(2,1)S(1)}, u32[]{:S(2)}, u32[]{:S(2)}) %collective-permute-start.2) | collective-permute-done | bytes 786464 | tf_op jit(solution)/shard_map/ppermute | solution.py:160
  250.3 6.8 %collective-permute-done.39 = bf16[96,2048]{1,0:T(8,128)(2,1)S(1)} collective-permute-done((bf16[96,2048]{1,0:T(8,128)(2,1)S(1)}, bf16[96,2048]{1,0:T(8,128)(2,1)S(1)}, u32[]{:S(2)}, u32[]{:S(2)}) %collective-permute-start.39) | collective-permute-done | bytes 393248 | tf_op jit(solution)/shard_map/ppermute | solution.py:163
  260.9 13.1 %collective-permute-done.31 = bf16[96,2048]{1,0:T(8,128)(2,1)S(1)} collective-permute-done((bf16[96,2048]{1,0:T(8,128)(2,1)S(1)}, bf16[96,2048]{1,0:T(8,128)(2,1)S(1)}, u32[]{:S(2)}, u32[]{:S(2)}) %collective-permute-start.31) | collective-permute-done | bytes 393248 | tf_op jit(solution)/shard_map/ppermute | solution.py:163
  277.3 13.5 %collective-permute-done.23 = bf16[96,2048]{1,0:T(8,128)(2,1)S(1)} collective-permute-done((bf16[96,2048]{1,0:T(8,128)(2,1)S(1)}, bf16[96,2048]{1,0:T(8,128)(2,1)S(1)}, u32[]{:S(2)}, u32[]{:S(2)}) %collective-permute-start.23) | collective-permute-done | bytes 393248 | tf_op jit(solution)/shard_map/ppermute | solution.py:163
  291.1 6.8 %collective-permute-done.3 = bf16[96,2048]{1,0:T(8,128)(2,1)S(1)} collective-permute-done((bf16[96,2048]{1,0:T(8,128)(2,1)S(1)}, bf16[96,2048]{1,0:T(8,128)(2,1)S(1)}, u32[]{:S(2)}, u32[]{:S(2)}) %collective-permute-start.3) | collective-permute-done | bytes 393248 | tf_op jit(solution)/shard_map/ppermute | solution.py:163
  306.1 41.2 %collective-permute-done.48 = bf16[96,2048]{1,0:T(8,128)(2,1)S(1)} collective-permute-done((bf16[96,2048]{1,0:T(8,128)(2,1)S(1)}, bf16[96,2048]{1,0:T(8,128)(2,1)S(1)}, u32[]{:S(2)}, u32[]{:S(2)}) %collective-permute-start.48) | collective-permute-done | bytes 393248 | tf_op jit(solution)/shard_map/ppermute | solution.py:166
  347.3 8.1 %collective-permute-start.65 = (bf16[96,2048]{1,0:T(8,128)(2,1)S(1)}, bf16[96,2048]{1,0:T(8,128)(2,1)S(1)}, u32[]{:S(2)}, u32[]{:S(2)}) collective-permute-start(bf16[96,2048]{1,0:T(8,128)(2,1)S(1)} %add_convert_fusion.10), channel_id=1, source_target_pairs={{0,8},{8,0},{16,24},{24,16},{1,9},{9,1},{17,25},{25,17},{2,10},{10... | collective-permute-start | bytes 1179656 | tf_op jit(solution)/shard_map/ppermute | solution.py:163
  381.0 11.9 %collective-permute-done.65 = bf16[96,2048]{1,0:T(8,128)(2,1)S(1)} collective-permute-done((bf16[96,2048]{1,0:T(8,128)(2,1)S(1)}, bf16[96,2048]{1,0:T(8,128)(2,1)S(1)}, u32[]{:S(2)}, u32[]{:S(2)}) %collective-permute-start.65) | collective-permute-done | bytes 393248 | tf_op jit(solution)/shard_map/ppermute | solution.py:163
  393.8 7.6 %collective-permute-done.57 = bf16[96,2048]{1,0:T(8,128)(2,1)S(1)} collective-permute-done((bf16[96,2048]{1,0:T(8,128)(2,1)S(1)}, bf16[96,2048]{1,0:T(8,128)(2,1)S(1)}, u32[]{:S(2)}, u32[]{:S(2)}) %collective-permute-start.57) | collective-permute-done | bytes 393248 | tf_op jit(solution)/shard_map/ppermute | solution.py:163
  402.3 7.5 %collective-permute-done.49 = bf16[96,2048]{1,0:T(8,128)(2,1)S(1)} collective-permute-done((bf16[96,2048]{1,0:T(8,128)(2,1)S(1)}, bf16[96,2048]{1,0:T(8,128)(2,1)S(1)}, u32[]{:S(2)}, u32[]{:S(2)}) %collective-permute-start.49) | collective-permute-done | bytes 393248 | tf_op jit(solution)/shard_map/ppermute | solution.py:163
  409.8 8.4 %collective-permute-done.41 = bf16[96,2048]{1,0:T(8,128)(2,1)S(1)} collective-permute-done((bf16[96,2048]{1,0:T(8,128)(2,1)S(1)}, bf16[96,2048]{1,0:T(8,128)(2,1)S(1)}, u32[]{:S(2)}, u32[]{:S(2)}) %collective-permute-start.41) | collective-permute-done | bytes 393248 | tf_op jit(solution)/shard_map/ppermute | solution.py:163
  424.6 18.3 %collective-permute-done.5 = bf16[96,2048]{1,0:T(8,128)(2,1)S(1)} collective-permute-done((bf16[96,2048]{1,0:T(8,128)(2,1)S(1)}, bf16[96,2048]{1,0:T(8,128)(2,1)S(1)}, u32[]{:S(2)}, u32[]{:S(2)}) %collective-permute-start.5) | collective-permute-done | bytes 393248 | tf_op jit(solution)/shard_map/ppermute | solution.py:160
  452.2 12.1 %collective-permute-done.50.refs_1_ = bf16[192,2048]{1,0:T(8,128)(2,1)} collective-permute-done((bf16[192,2048]{1,0:T(8,128)(2,1)S(1)}, bf16[192,2048]{1,0:T(8,128)(2,1)}, u32[]{:S(2)}, u32[]{:S(2)}) %collective-permute-start.50) | collective-permute-done | bytes 786464 | tf_op jit(solution)/shard_map/ppermute | solution.py:160
  464.3 16.4 %collective-permute-done.42.refs_1_ = bf16[192,2048]{1,0:T(8,128)(2,1)} collective-permute-done((bf16[192,2048]{1,0:T(8,128)(2,1)S(1)}, bf16[192,2048]{1,0:T(8,128)(2,1)}, u32[]{:S(2)}, u32[]{:S(2)}) %collective-permute-start.42) | collective-permute-done | bytes 786464 | tf_op jit(solution)/shard_map/ppermute | solution.py:160
  483.6 16.2 %collective-permute-done.26.refs_1_ = bf16[192,2048]{1,0:T(8,128)(2,1)} collective-permute-done((bf16[192,2048]{1,0:T(8,128)(2,1)S(1)}, bf16[192,2048]{1,0:T(8,128)(2,1)}, u32[]{:S(2)}, u32[]{:S(2)}) %collective-permute-start.26) | collective-permute-done | bytes 786464 | tf_op jit(solution)/shard_map/ppermute | solution.py:160
  523.1 6.6 %shard_map.65.refs_8_ = f32[14336,512]{1,0:T(8,128)} custom-call(s32[4]{0:T(128)S(1)} %pad_add_fusion.where_ref, bf16[192,2048]{1,0:T(8,128)(2,1)S(1)} %pad_maximum_fusion.6.refs_0_, bf16[192,2048]{1,0:T(8,128)(2,1)} %collective-permute-done.42.refs_1_, bf16[192,2048]{1,0:T(8,128)(2,1)} %collective-permute-done.43.refs_2_, ...), custom_call_target="tpu_custom_call", output_to_operand_aliasing={{}: (9, {})} | custom-call | flops 2147483648 | bytes 7340032 | tf_op jit(solution)/shard_map/pallas_call | solution.py:128
  529.7 6.7 %shard_map.66.refs_8_ = f32[14336,512]{1,0:T(8,128)} custom-call(s32[4]{0:T(128)S(1)} %pad_add_fusion.where_ref, bf16[192,2048]{1,0:T(8,128)(2,1)} %pad_maximum_fusion.5.refs_0_, bf16[192,2048]{1,0:T(8,128)(2,1)} %collective-permute-done.34.refs_1_, bf16[192,2048]{1,0:T(8,128)(2,1)} %collective-permute-done.35.refs_2_, ...), custom_call_target="tpu_custom_call", output_to_operand_aliasing={{}: (9, {})} | custom-call | flops 2147483648 | bytes 7340032 | tf_op jit(solution)/shard_map/pallas_call | solution.py:128
  (237 shorter events, 154.4 us)
Async XLA Ops:
  8.9 41.9 %collective-permute-start = (bf16[512,1792]{1,0:T(8,128)(2,1)}, bf16[512,1792]{1,0:T(8,128)(2,1)S(1)}, u32[]{:S(2)}, u32[]{:S(2)}) collective-permute-start(bf16[512,1792]{1,0:T(8,128)(2,1)} %param.5), channel_id=1, source_target_pairs={{0,4},{4,0},{1,5},{5,1},{2,6},{6,2},{3,7},{7,3},{8,12},{12,8},{9,1... | collective-permute-start | bytes 5505032 | tf_op jit(solution)/shard_map/ppermute | solution.py:196
  47.4 69.2 %collective-permute-start.17 = (bf16[128,4096]{1,0:T(8,128)(2,1)S(1)}, bf16[128,4096]{1,0:T(8,128)(2,1)S(1)}, u32[]{:S(2)}, u32[]{:S(2)}) collective-permute-start(bf16[128,4096]{1,0:T(8,128)(2,1)S(1)} %pad_maximum_fusion.2), channel_id=1, source_target_pairs={{0,2},{2,0},{1,3},{3,1},{4,6},{6,4},{5,7},{7,5},{8,10},{10,8},{9,1... | collective-permute-start | bytes 3145736 | tf_op jit(solution)/shard_map/ppermute | solution.py:160
  48.5 81.3 %collective-permute-start.18 = (bf16[256,4096]{1,0:T(8,128)(2,1)S(1)}, bf16[256,4096]{1,0:T(8,128)(2,1)}, u32[]{:S(2)}, u32[]{:S(2)}) collective-permute-start(bf16[256,4096]{1,0:T(8,128)(2,1)S(1)} %pad_maximum_fusion), channel_id=1, source_target_pairs={{0,1},{1,0},{2,3},{3,2},{4,5},{5,4},{6,7},{7,6},{8,9},{9,8},{10,11... | collective-permute-start | bytes 6291464 | tf_op jit(solution)/shard_map/ppermute | solution.py:157
  122.2 176.0 %collective-permute-start.19 = (bf16[256,4096]{1,0:T(8,128)(2,1)S(1)}, bf16[256,4096]{1,0:T(8,128)(2,1)S(1)}, u32[]{:S(2)}, u32[]{:S(2)}) collective-permute-start(bf16[256,4096]{1,0:T(8,128)(2,1)S(1)} %constant_dynamic-update-slice_fusion), channel_id=1, source_target_pairs={{0,1},{1,0},{2,3},{3,2},{4,5},{5,4},{6,7},{7,6},{8,9},{9,8},{10,11... | collective-permute-start | bytes 6291464 | tf_op jit(solution)/shard_map/ppermute | solution.py:157
  126.7 35.0 %collective-permute-start.54 = (bf16[192,2048]{1,0:T(8,128)(2,1)S(1)}, bf16[192,2048]{1,0:T(8,128)(2,1)S(1)}, u32[]{:S(2)}, u32[]{:S(2)}) collective-permute-start(bf16[192,2048]{1,0:T(8,128)(2,1)S(1)} %add_convert_fusion.3), channel_id=1, source_target_pairs={{0,2},{2,0},{1,3},{3,1},{4,6},{6,4},{5,7},{7,5},{8,10},{10,8},{9,1... | collective-permute-start | bytes 2359304 | tf_op jit(solution)/shard_map/ppermute | solution.py:160
  129.0 49.6 %collective-permute-start.46 = (bf16[192,2048]{1,0:T(8,128)(2,1)S(1)}, bf16[192,2048]{1,0:T(8,128)(2,1)S(1)}, u32[]{:S(2)}, u32[]{:S(2)}) collective-permute-start(bf16[192,2048]{1,0:T(8,128)(2,1)S(1)} %add_convert_fusion.4), channel_id=1, source_target_pairs={{0,2},{2,0},{1,3},{3,1},{4,6},{6,4},{5,7},{7,5},{8,10},{10,8},{9,1... | collective-permute-start | bytes 2359304 | tf_op jit(solution)/shard_map/ppermute | solution.py:160
  129.7 65.7 %collective-permute-start.38 = (bf16[192,2048]{1,0:T(8,128)(2,1)S(1)}, bf16[192,2048]{1,0:T(8,128)(2,1)S(1)}, u32[]{:S(2)}, u32[]{:S(2)}) collective-permute-start(bf16[192,2048]{1,0:T(8,128)(2,1)S(1)} %add_convert_fusion.5), channel_id=1, source_target_pairs={{0,2},{2,0},{1,3},{3,1},{4,6},{6,4},{5,7},{7,5},{8,10},{10,8},{9,1... | collective-permute-start | bytes 2359304 | tf_op jit(solution)/shard_map/ppermute | solution.py:160
  144.9 67.4 %collective-permute-start.30 = (bf16[192,2048]{1,0:T(8,128)(2,1)S(1)}, bf16[192,2048]{1,0:T(8,128)(2,1)S(1)}, u32[]{:S(2)}, u32[]{:S(2)}) collective-permute-start(bf16[192,2048]{1,0:T(8,128)(2,1)S(1)} %add_convert_fusion.6), channel_id=1, source_target_pairs={{0,2},{2,0},{1,3},{3,1},{4,6},{6,4},{5,7},{7,5},{8,10},{10,8},{9,1... | collective-permute-start | bytes 2359304 | tf_op jit(solution)/shard_map/ppermute | solution.py:160
  161.7 67.4 %collective-permute-start.22 = (bf16[192,2048]{1,0:T(8,128)(2,1)S(1)}, bf16[192,2048]{1,0:T(8,128)(2,1)S(1)}, u32[]{:S(2)}, u32[]{:S(2)}) collective-permute-start(bf16[192,2048]{1,0:T(8,128)(2,1)S(1)} %add_convert_fusion.7), channel_id=1, source_target_pairs={{0,2},{2,0},{1,3},{3,1},{4,6},{6,4},{5,7},{7,5},{8,10},{10,8},{9,1... | collective-permute-start | bytes 2359304 | tf_op jit(solution)/shard_map/ppermute | solution.py:160
  178.6 66.6 %collective-permute-start.2 = (bf16[192,2048]{1,0:T(8,128)(2,1)S(1)}, bf16[192,2048]{1,0:T(8,128)(2,1)S(1)}, u32[]{:S(2)}, u32[]{:S(2)}) collective-permute-start(bf16[192,2048]{1,0:T(8,128)(2,1)S(1)} %add_convert_fusion.8), channel_id=1, source_target_pairs={{0,2},{2,0},{1,3},{3,1},{4,6},{6,4},{5,7},{7,5},{8,10},{10,8},{9,1... | collective-permute-start | bytes 2359304 | tf_op jit(solution)/shard_map/ppermute | solution.py:160
  195.4 51.9 %collective-permute-start.63 = (bf16[96,2048]{1,0:T(8,128)(2,1)S(1)}, bf16[96,2048]{1,0:T(8,128)(2,1)S(1)}, u32[]{:S(2)}, u32[]{:S(2)}) collective-permute-start(bf16[96,2048]{1,0:T(8,128)(2,1)S(1)} %add_convert_fusion.11), channel_id=1, source_target_pairs={{0,8},{8,0},{16,24},{24,16},{1,9},{9,1},{17,25},{25,17},{2,10},{10... | collective-permute-start | bytes 1179656 | tf_op jit(solution)/shard_map/ppermute | solution.py:163
  212.3 35.4 %collective-permute-start.55 = (bf16[96,2048]{1,0:T(8,128)(2,1)S(1)}, bf16[96,2048]{1,0:T(8,128)(2,1)S(1)}, u32[]{:S(2)}, u32[]{:S(2)}) collective-permute-start(bf16[96,2048]{1,0:T(8,128)(2,1)S(1)} %add_convert_fusion.13), channel_id=1, source_target_pairs={{0,8},{8,0},{16,24},{24,16},{1,9},{9,1},{17,25},{25,17},{2,10},{10... | collective-permute-start | bytes 1179656 | tf_op jit(solution)/shard_map/ppermute | solution.py:163
  247.7 43.2 %collective-permute-start.23 = (bf16[96,2048]{1,0:T(8,128)(2,1)S(1)}, bf16[96,2048]{1,0:T(8,128)(2,1)S(1)}, u32[]{:S(2)}, u32[]{:S(2)}) collective-permute-start(bf16[96,2048]{1,0:T(8,128)(2,1)S(1)} %add_convert_fusion.21), channel_id=1, source_target_pairs={{0,8},{8,0},{16,24},{24,16},{1,9},{9,1},{17,25},{25,17},{2,10},{10... | collective-permute-start | bytes 1179656 | tf_op jit(solution)/shard_map/ppermute | solution.py:163
  250.0 48.0 %collective-permute-start.3 = (bf16[96,2048]{1,0:T(8,128)(2,1)S(1)}, bf16[96,2048]{1,0:T(8,128)(2,1)S(1)}, u32[]{:S(2)}, u32[]{:S(2)}) collective-permute-start(bf16[96,2048]{1,0:T(8,128)(2,1)S(1)} %add_convert_fusion.23), channel_id=1, source_target_pairs={{0,8},{8,0},{16,24},{24,16},{1,9},{9,1},{17,25},{25,17},{2,10},{10... | collective-permute-start | bytes 1179656 | tf_op jit(solution)/shard_map/ppermute | solution.py:163
  257.2 45.3 %collective-permute-start.64 = (bf16[96,2048]{1,0:T(8,128)(2,1)S(1)}, bf16[96,2048]{1,0:T(8,128)(2,1)S(1)}, u32[]{:S(2)}, u32[]{:S(2)}) collective-permute-start(bf16[96,2048]{1,0:T(8,128)(2,1)S(1)} %fusion.20), channel_id=1, source_target_pairs={{0,16},{16,0},{8,24},{24,8},{1,17},{17,1},{9,25},{25,9},{2,18},{18... | collective-permute-start | bytes 1179656 | tf_op jit(solution)/shard_map/ppermute | solution.py:166
  274.0 28.8 %collective-permute-start.56 = (bf16[96,2048]{1,0:T(8,128)(2,1)S(1)}, bf16[96,2048]{1,0:T(8,128)(2,1)S(1)}, u32[]{:S(2)}, u32[]{:S(2)}) collective-permute-start(bf16[96,2048]{1,0:T(8,128)(2,1)S(1)} %fusion.19), channel_id=1, source_target_pairs={{0,16},{16,0},{8,24},{24,8},{1,17},{17,1},{9,25},{25,9},{2,18},{18... | collective-permute-start | bytes 1179656 | tf_op jit(solution)/shard_map/ppermute | solution.py:166
  290.9 56.4 %collective-permute-start.48 = (bf16[96,2048]{1,0:T(8,128)(2,1)S(1)}, bf16[96,2048]{1,0:T(8,128)(2,1)S(1)}, u32[]{:S(2)}, u32[]{:S(2)}) collective-permute-start(bf16[96,2048]{1,0:T(8,128)(2,1)S(1)} %fusion.18), channel_id=1, source_target_pairs={{0,16},{16,0},{8,24},{24,8},{1,17},{17,1},{9,25},{25,9},{2,18},{18... | collective-permute-start | bytes 1179656 | tf_op jit(solution)/shard_map/ppermute | solution.py:166
  297.9 62.1 %collective-permute-start.40 = (bf16[96,2048]{1,0:T(8,128)(2,1)S(1)}, bf16[96,2048]{1,0:T(8,128)(2,1)S(1)}, u32[]{:S(2)}, u32[]{:S(2)}) collective-permute-start(bf16[96,2048]{1,0:T(8,128)(2,1)S(1)} %fusion.17), channel_id=1, source_target_pairs={{0,16},{16,0},{8,24},{24,8},{1,17},{17,1},{9,25},{25,9},{2,18},{18... | collective-permute-start | bytes 1179656 | tf_op jit(solution)/shard_map/ppermute | solution.py:166
  298.2 70.3 %collective-permute-start.32 = (bf16[96,2048]{1,0:T(8,128)(2,1)S(1)}, bf16[96,2048]{1,0:T(8,128)(2,1)S(1)}, u32[]{:S(2)}, u32[]{:S(2)}) collective-permute-start(bf16[96,2048]{1,0:T(8,128)(2,1)S(1)} %fusion.16), channel_id=1, source_target_pairs={{0,16},{16,0},{8,24},{24,8},{1,17},{17,1},{9,25},{25,9},{2,18},{18... | collective-permute-start | bytes 1179656 | tf_op jit(solution)/shard_map/ppermute | solution.py:166
  302.4 74.4 %collective-permute-start.24 = (bf16[96,2048]{1,0:T(8,128)(2,1)S(1)}, bf16[96,2048]{1,0:T(8,128)(2,1)S(1)}, u32[]{:S(2)}, u32[]{:S(2)}) collective-permute-start(bf16[96,2048]{1,0:T(8,128)(2,1)S(1)} %fusion.15), channel_id=1, source_target_pairs={{0,16},{16,0},{8,24},{24,8},{1,17},{17,1},{9,25},{25,9},{2,18},{18... | collective-permute-start | bytes 1179656 | tf_op jit(solution)/shard_map/ppermute | solution.py:166
  302.9 98.6 %collective-permute-start.4 = (bf16[96,2048]{1,0:T(8,128)(2,1)S(1)}, bf16[96,2048]{1,0:T(8,128)(2,1)S(1)}, u32[]{:S(2)}, u32[]{:S(2)}) collective-permute-start(bf16[96,2048]{1,0:T(8,128)(2,1)S(1)} %fusion.14), channel_id=1, source_target_pairs={{0,16},{16,0},{8,24},{24,8},{1,17},{17,1},{9,25},{25,9},{2,18},{18... | collective-permute-start | bytes 1179656 | tf_op jit(solution)/shard_map/ppermute | solution.py:166
  347.3 45.7 %collective-permute-start.65 = (bf16[96,2048]{1,0:T(8,128)(2,1)S(1)}, bf16[96,2048]{1,0:T(8,128)(2,1)S(1)}, u32[]{:S(2)}, u32[]{:S(2)}) collective-permute-start(bf16[96,2048]{1,0:T(8,128)(2,1)S(1)} %add_convert_fusion.10), channel_id=1, source_target_pairs={{0,8},{8,0},{16,24},{24,16},{1,9},{9,1},{17,25},{25,17},{2,10},{10... | collective-permute-start | bytes 1179656 | tf_op jit(solution)/shard_map/ppermute | solution.py:163
  360.0 41.3 %collective-permute-start.57 = (bf16[96,2048]{1,0:T(8,128)(2,1)S(1)}, bf16[96,2048]{1,0:T(8,128)(2,1)S(1)}, u32[]{:S(2)}, u32[]{:S(2)}) collective-permute-start(bf16[96,2048]{1,0:T(8,128)(2,1)S(1)} %add_convert_fusion.12), channel_id=1, source_target_pairs={{0,8},{8,0},{16,24},{24,16},{1,9},{9,1},{17,25},{25,17},{2,10},{10... | collective-permute-start | bytes 1179656 | tf_op jit(solution)/shard_map/ppermute | solution.py:163
  368.5 41.3 %collective-permute-start.49 = (bf16[96,2048]{1,0:T(8,128)(2,1)S(1)}, bf16[96,2048]{1,0:T(8,128)(2,1)S(1)}, u32[]{:S(2)}, u32[]{:S(2)}) collective-permute-start(bf16[96,2048]{1,0:T(8,128)(2,1)S(1)} %add_convert_fusion.14), channel_id=1, source_target_pairs={{0,8},{8,0},{16,24},{24,16},{1,9},{9,1},{17,25},{25,17},{2,10},{10... | collective-permute-start | bytes 1179656 | tf_op jit(solution)/shard_map/ppermute | solution.py:163
  376.9 41.3 %collective-permute-start.41 = (bf16[96,2048]{1,0:T(8,128)(2,1)S(1)}, bf16[96,2048]{1,0:T(8,128)(2,1)S(1)}, u32[]{:S(2)}, u32[]{:S(2)}) collective-permute-start(bf16[96,2048]{1,0:T(8,128)(2,1)S(1)} %add_convert_fusion.16), channel_id=1, source_target_pairs={{0,8},{8,0},{16,24},{24,16},{1,9},{9,1},{17,25},{25,17},{2,10},{10... | collective-permute-start | bytes 1179656 | tf_op jit(solution)/shard_map/ppermute | solution.py:163
  401.5 42.2 %collective-permute-start.66 = (bf16[192,2048]{1,0:T(8,128)(2,1)S(1)}, bf16[192,2048]{1,0:T(8,128)(2,1)S(1)}, u32[]{:S(2)}, u32[]{:S(2)}) collective-permute-start(bf16[192,2048]{1,0:T(8,128)(2,1)S(1)} %pad_maximum_fusion.9.refs_0_), channel_id=1, source_target_pairs={{0,2},{2,0},{1,3},{3,1},{4,6},{6,4},{5,7},{7,5},{8,10},{10,8},{9,1... | collective-permute-start | bytes 2359304 | tf_op jit(solution)/shard_map/ppermute | solution.py:160
  409.8 34.8 %collective-permute-start.67 = (bf16[192,2048]{1,0:T(8,128)(2,1)S(1)}, bf16[192,2048]{1,0:T(8,128)(2,1)S(1)}, u32[]{:S(2)}, u32[]{:S(2)}) collective-permute-start(bf16[192,2048]{1,0:T(8,128)(2,1)S(1)} %pad_maximum_fusion.9.refs_0_), channel_id=1, source_target_pairs={{0,1},{1,0},{2,3},{3,2},{4,5},{5,4},{6,7},{7,6},{8,9},{9,8},{10,11... | collective-permute-start | bytes 2359304 | tf_op jit(solution)/shard_map/ppermute | solution.py:157
  418.2 27.5 %collective-permute-start.58 = (bf16[192,2048]{1,0:T(8,128)(2,1)S(1)}, bf16[192,2048]{1,0:T(8,128)(2,1)S(1)}, u32[]{:S(2)}, u32[]{:S(2)}) collective-permute-start(bf16[192,2048]{1,0:T(8,128)(2,1)S(1)} %pad_maximum_fusion.8.refs_0_), channel_id=1, source_target_pairs={{0,2},{2,0},{1,3},{3,1},{4,6},{6,4},{5,7},{7,5},{8,10},{10,8},{9,1... | collective-permute-start | bytes 2359304 | tf_op jit(solution)/shard_map/ppermute | solution.py:160
  423.0 76.8 %collective-permute-start.20 = (f32[1024,512]{1,0:T(8,128)}, f32[1024,512]{1,0:T(8,128)}, u32[]{:S(2)}, u32[]{:S(2)}) collective-permute-start(f32[1024,512]{1,0:T(8,128)} %pad_maximum_fusion.1), channel_id=1, source_target_pairs={{0,4},{4,0},{1,5},{5,1},{2,6},{6,2},{3,7},{7,3},{8,12},{12,8},{9,1... | collective-permute-start | bytes 6291464 | tf_op jit(solution)/shard_map/ppermute | solution.py:233
  446.7 34.0 %collective-permute-start.42 = (bf16[192,2048]{1,0:T(8,128)(2,1)S(1)}, bf16[192,2048]{1,0:T(8,128)(2,1)}, u32[]{:S(2)}, u32[]{:S(2)}) collective-permute-start(bf16[192,2048]{1,0:T(8,128)(2,1)S(1)} %pad_maximum_fusion.6.refs_0_), channel_id=1, source_target_pairs={{0,2},{2,0},{1,3},{3,1},{4,6},{6,4},{5,7},{7,5},{8,10},{10,8},{9,1... | collective-permute-start | bytes 2359304 | tf_op jit(solution)/shard_map/ppermute | solution.py:160
  451.0 30.7 %collective-permute-start.43 = (bf16[192,2048]{1,0:T(8,128)(2,1)S(1)}, bf16[192,2048]{1,0:T(8,128)(2,1)}, u32[]{:S(2)}, u32[]{:S(2)}) collective-permute-start(bf16[192,2048]{1,0:T(8,128)(2,1)S(1)} %pad_maximum_fusion.6.refs_0_), channel_id=1, source_target_pairs={{0,1},{1,0},{2,3},{3,2},{4,5},{5,4},{6,7},{7,6},{8,9},{9,8},{10,11... | collective-permute-start | bytes 2359304 | tf_op jit(solution)/shard_map/ppermute | solution.py:157
  483.2 27.0 %collective-permute-start.6 = (bf16[192,2048]{1,0:T(8,128)(2,1)S(1)}, bf16[192,2048]{1,0:T(8,128)(2,1)S(1)}, u32[]{:S(2)}, u32[]{:S(2)}) collective-permute-start(bf16[192,2048]{1,0:T(8,128)(2,1)S(1)} %pad_maximum_fusion.3.refs_0_), channel_id=1, source_target_pairs={{0,8},{8,0},{16,24},{24,16},{1,9},{9,1},{17,25},{25,17},{2,10},{10... | collective-permute-start | bytes 2359304 | tf_op jit(solution)/shard_map/ppermute | solution.py:163
  (58 other events, 1852.4 us)
